TPU v7x, 128 devices: a whole 4x4x4 slice. The times are simulated.
128 devices in a mesh: rep: 4 (over x), expert: 32 (over z, y, core).
Axes of the slice: x: 4, y: 4, z: 4, core: 2. Of those that a mesh axis runs over, the one named last changes fastest.
Arguments:
- tokens: bfloat16 [32768, 1536], P(('rep', 'expert')), may hold values from -6 to 6
- routes: int32 [32768, 4], P(('rep', 'expert')), may hold values from 0 to 31, all different within a row; in each aligned block of 256 rows (0 to 255, 256 to 511, ...) at most 64 rows name the same one
- history: int32 [128], P(('rep', 'expert')), may hold values from 0 to 12287, as said below
- cache_keys: bfloat16 [128, 2, 4100, 128], P(('rep', 'expert')), may hold values from -400 to 400
- cache_values: bfloat16 [128, 2, 4100, 128], P(('rep', 'expert')), may hold values from -6 to 6
- attn_gain: bfloat16 [1536], replicated, may hold values from 0.099609375 to 1.8984375
- w_query: bfloat16 [1536, 1536], replicated, may hold values from -0.15625 to 0.15625
- w_key: bfloat16 [1536, 256], replicated, may hold values from -0.15625 to 0.15625
- w_value: bfloat16 [1536, 256], replicated, may hold values from -0.15625 to 0.15625
- w_out: bfloat16 [1536, 1536], replicated, may hold values from -0.15625 to 0.15625
- ffn_gain: bfloat16 [1536], replicated, may hold values from 0.099609375 to 1.8984375
- w_router: bfloat16 [1536, 32], replicated, may hold values from -0.15625 to 0.15625
- expert_gate: bfloat16 [32, 1536, 768], P('expert'), may hold values from -0.15625 to 0.15625
- expert_up: bfloat16 [32, 1536, 768], P('expert'), may hold values from -0.15625 to 0.15625
- expert_down: bfloat16 [32, 768, 1536], P('expert'), may hold values from -0.21875 to 0.21875
Outputs:
- layer_out: bfloat16 [32768, 1536], P(('rep', 'expert'))
- new_keys: bfloat16 [32768, 256], P(('rep', 'expert'))
- new_values: bfloat16 [32768, 256], P(('rep', 'expert'))
Inputs may be any that keep to these rules, and one draw needn't show every extreme that they name: `routes`: each row names 4 different experts. Among the rows of one request no expert is named by more than 64 rows, and in every draw some expert is named by exactly 64 rows of some request. Some request has no history and some has 12287 tokens.
All inputs are finite; a program needn't handle non-finite values.
Results may differ from a plain program's by a relative error of at most 0.007.
The roundings to bfloat16 on the way count: a program that leaves them out, or rounds other values in their place, can miss the bound.
Values may be sent and summed in bfloat16 or wider, within the bound.
A program may use at most 192 MiB of HBM per device.

v0:
```python
import jax
import jax.numpy as jnp
from jax import lax
from jax.sharding import PartitionSpec as P

HEADS = 12
KV_HEADS = 2
HEAD_DIM = 128
TOP = 4
SINK = 4
WINDOW = 4096


theta_base = 1000000.0
eps_norm = 1e-06


def rms_norm(values, gain):
    mean_square = jnp.mean(values * values, axis=-1, keepdims=True)
    return values * lax.rsqrt(mean_square + eps_norm) * gain.astype(jnp.float32)


def rotate(vectors, positions):
    half_dim = vectors.shape[-1] // 2
    exponent = jnp.arange(half_dim, dtype=jnp.float32) * (2.0 / vectors.shape[-1])
    inverse_freq = theta_base ** (-exponent)
    angles = positions.astype(jnp.float32)[:, None] * inverse_freq[None, :]
    cosine = jnp.cos(angles)[:, None, :]
    sine_part = jnp.sin(angles)[:, None, :]
    first = vectors[..., :half_dim]
    second = vectors[..., half_dim:]
    return jnp.concatenate(
        [first * cosine - second * sine_part, second * cosine + first * sine_part], axis=-1
    )


def shards(
    tokens,
    routes,
    history,
    cache_keys,
    cache_values,
    attn_gain,
    w_query,
    w_key,
    w_value,
    w_out,
    ffn_gain,
    w_router,
    expert_gate,
    expert_up,
    expert_down,
):
    row_count = tokens.shape[0]
    model_width = tokens.shape[1]
    past_tokens = history[0]
    residual_in = tokens.astype(jnp.float32)
    normed = rms_norm(residual_in, attn_gain).astype(jnp.bfloat16)
    positions = past_tokens + jnp.arange(row_count, dtype=jnp.int32)
    queries = rotate(
        jnp.dot(normed, w_query, preferred_element_type=jnp.float32).reshape(
            row_count, HEADS, HEAD_DIM
        ),
        positions,
    ).astype(jnp.bfloat16)
    keys_new = rotate(
        jnp.dot(normed, w_key, preferred_element_type=jnp.float32).reshape(
            row_count, KV_HEADS, HEAD_DIM
        ),
        positions,
    ).astype(jnp.bfloat16)
    values_new = (
        jnp.dot(normed, w_value, preferred_element_type=jnp.float32)
        .astype(jnp.bfloat16)
        .reshape(row_count, KV_HEADS, HEAD_DIM)
    )
    keys_all = jnp.concatenate([cache_keys[0], jnp.transpose(keys_new, (1, 0, 2))], axis=1)
    values_all = jnp.concatenate([cache_values[0], jnp.transpose(values_new, (1, 0, 2))], axis=1)
    slot_count = cache_keys.shape[2]
    slot_ids = jnp.arange(slot_count, dtype=jnp.int32)
    slot_pos = jnp.where(
        slot_ids < SINK, slot_ids, slot_ids + WINDOW * ((past_tokens - 1 - slot_ids) // WINDOW)
    )
    key_pos = jnp.concatenate([slot_pos, positions])
    key_live = jnp.concatenate([slot_ids < past_tokens, jnp.ones((row_count,), dtype=bool)])
    group_size = HEADS // KV_HEADS
    score_scale = HEAD_DIM ** (-0.5)
    expert_count = lax.axis_size("expert")
    capacity_full = 2 * row_count * TOP // expert_count
    block_rows = min(128, row_count)

    def one_block(block_index):
        start_row = 0 + block_index * block_rows
        block_query = lax.dynamic_slice_in_dim(queries, start_row, block_rows, 0).reshape(
            block_rows, KV_HEADS, group_size, HEAD_DIM
        )
        query_pos = past_tokens + start_row + jnp.arange(block_rows, dtype=jnp.int32)
        allowed = (
            key_live[None, :]
            & (key_pos[None, :] <= query_pos[:, None])
            & ((key_pos[None, :] < SINK) | (key_pos[None, :] > query_pos[:, None] - WINDOW))
        )
        scores = (
            jnp.einsum("tkgd,ksd->kgts", block_query, keys_all, preferred_element_type=jnp.float32)
            * score_scale
        )
        scores = jnp.where(allowed[None, None], scores, -1e30)
        row_max = jnp.max(scores, axis=-1, keepdims=True)
        expo = jnp.exp(scores - row_max)
        probability = (expo / jnp.sum(expo, axis=-1, keepdims=True)).astype(jnp.bfloat16)
        attended = jnp.einsum(
            "kgts,ksd->tkgd", probability, values_all, preferred_element_type=jnp.float32
        ).astype(jnp.bfloat16)
        return attended.reshape(block_rows, HEADS * HEAD_DIM)

    stacked = lax.map(one_block, jnp.arange(row_count // block_rows, dtype=jnp.int32))
    attended = stacked.reshape(row_count, HEADS * HEAD_DIM)
    mixed_rows = residual_in + jnp.dot(attended, w_out, preferred_element_type=jnp.float32)
    ffn_in = rms_norm(mixed_rows, ffn_gain).astype(jnp.bfloat16)
    span_rows = ffn_in.shape[0]
    expert_ids = routes.reshape(-1)
    routed_total = span_rows * TOP
    expert_range = jnp.arange(expert_count, dtype=jnp.int32)
    one_hot = (expert_ids[:, None] == expert_range[None, :]).astype(jnp.int32)
    rank_within = jnp.sum((jnp.cumsum(one_hot, axis=0) - one_hot) * one_hot, axis=1)
    flat_target = expert_ids * capacity_full + rank_within
    source_table = jnp.full((expert_count * capacity_full,), span_rows, dtype=jnp.int32)
    source_table = source_table.at[flat_target].set(
        jnp.arange(routed_total, dtype=jnp.int32) // TOP
    )
    padded_rows = jnp.concatenate([ffn_in, jnp.zeros((1, model_width), dtype=jnp.bfloat16)], axis=0)
    send_buffer = padded_rows[source_table].reshape(expert_count, capacity_full, model_width)
    received = lax.all_to_all(send_buffer, "expert", split_axis=0, concat_axis=0, tiled=True)
    flat_rows = received.reshape(-1, model_width)
    gate_part = jnp.dot(flat_rows, expert_gate[0], preferred_element_type=jnp.float32)
    up_part = jnp.dot(flat_rows, expert_up[0], preferred_element_type=jnp.float32)
    hidden = (jnp.maximum(gate_part, 0.0) * up_part).astype(jnp.bfloat16)
    expert_out = jnp.dot(hidden, expert_down[0], preferred_element_type=jnp.float32).astype(
        jnp.bfloat16
    )
    returned = lax.all_to_all(
        expert_out.reshape(received.shape), "expert", split_axis=0, concat_axis=0, tiled=True
    )
    expert_out = returned.reshape(expert_count * capacity_full, model_width)[flat_target].reshape(
        span_rows, TOP, model_width
    )
    logits = jnp.dot(ffn_in, w_router, preferred_element_type=jnp.float32)
    chosen_logits = jnp.sum(
        jnp.where(routes[:, :, None] == expert_range[None, None, :], logits[:, None, :], 0.0),
        axis=-1,
    )
    gate_scores = jax.nn.sigmoid(chosen_logits)
    mix_weights = gate_scores / jnp.sum(gate_scores, axis=1, keepdims=True)
    combined = jnp.sum(mix_weights[:, :, None] * expert_out.astype(jnp.float32), axis=1)
    layer_out = (mixed_rows + combined).astype(jnp.bfloat16)
    return (
        layer_out,
        keys_new.reshape(row_count, KV_HEADS * HEAD_DIM),
        values_new.reshape(row_count, KV_HEADS * HEAD_DIM),
    )


def solution(mesh):
    in_specs = (
        P(("rep", "expert"), None),
        P(("rep", "expert"), None),
        P(("rep", "expert")),
        P(("rep", "expert"), None, None, None),
        P(("rep", "expert"), None, None, None),
        P(),
        P(),
        P(),
        P(),
        P(),
        P(),
        P(),
        P("expert", None, None),
        P("expert", None, None),
        P("expert", None, None),
    )
    out_specs = (P(("rep", "expert"), None), P(("rep", "expert"), None), P(("rep", "expert"), None))
    return jax.shard_map(shards, mesh=mesh, in_specs=in_specs, out_specs=out_specs, check_vma=False)
```

profile of v0, /device:TPU:2, one launch (start us, length us, event | category | flops | bytes accessed | tf_op | source)
XLA Modules:
  0.0 394.7 jit_solution(17902147981103096921)
XLA Ops:
  8.5 9.0 %reduce-window.6 = s32[32,8,128]{2,1,0:T(8,128)S(1)} reduce-window(s32[32,8,128]{2,1,0:T(8,128)S(1)} %fusion.27, s32[]{:T(128)} %constant.109.clone.1), window={size=1x1x128 pad=0_0x0_0x127_0}, to_apply=%region_8.9 | reduce-window | flops 4161536 | bytes 262148 | tf_op jit(solution)/shard_map/reduce-window
  18.1 4.3 %scatter_custom_fusion = s32[2048]{0:T(1024)S(1)} fusion(s32[1024]{0:T(1024)S(1)} %bitcast.125, s32[1024]{0:T(1024)S(1)} %add_select_fusion.1, s32[]{:T(128)} %constant.124.clone.1), kind=kCustom, calls=%fused_computation.90 | custom fusion | bytes 8196 | tf_op jit(solution)/shard_map/scatter | solution.py:128
  23.0 1.9 convolution_convert_fusion.1
  29.6 4.6 %fusion.44 = f32[256,1536]{0,1:T(8,128)S(1)} fusion(bf16[1536,1536]{1,0:T(8,128)(2,1)} %param.23, bf16[256,1536]{1,0:T(8,128)(2,1)} %param.17, f32[1536]{0:T(1024)S(1)} %convert_element_type.72, f32[256]{0:T(256)} %copy-done.23), kind=kOutput, calls=%fused_computation.104 | convolution fusion | flops 1209532416 | bytes 7085056 | tf_op jit(solution)/shard_map/dot_general | solution.py:61
  41.7 127.4 %while.12 = (s32[]{:T(128)}, bf16[2,128,1536]{2,1,0:T(8,128)(2,1)}, pred[4356]{0:T(1024)(128)(4,1)S(1)}, s32[4356]{0:T(1024)S(1)}, s32[2]{0:T(128)S(1)}, /*index...) while((s32[]{:T(128)}, bf16[2,128,1536]{2,1,0:T(8,128)(2,1)}, ...), condition=%wide.region_4.5_spmd, body=%wide.region_1.4_spmd.sunk | while | flops 3482217728 | bytes 115836928 | solution.py:116
  44.8 3.4 or_and_fusion.2
  48.2 14.1 %fusion.72 = f32[2,128,6,4356]{1,3,2,0:T(8,128)} fusion(bf16[128,2,6,128]{0,3,2,1:T(8,128)(2,1)S(1)} %bitcast.110, bf16[2,4356,128]{2,1,0:T(8,128)(2,1)} %get-tuple-element.274), kind=kOutput, calls=%fused_computation.15.clone.1 | convolution fusion | flops 1712848896 | bytes 29386752 | tf_op jit(solution)/shard_map/while/body/eval_jaxpr/tkgd,ksd->kgts/dot_general | solution.py:104
  62.3 31.2 %fusion.73 = (f32[2,6,128]{2,1,0:T(8,128)S(1)}, f32[2,6,128,4356]{2,3,1,0:T(8,128)}) fusion(f32[2,128,6,4356]{1,3,2,0:T(8,128)} %fusion.72, pred[128,4356]{0,1:T(8,128)(4,1)S(1)} %or_and_fusion.2), kind=kOutput, calls=%fused_computation.105.clone.1 | output fusion | flops 40149252 | bytes 54090240 | tf_op jit(solution)/shard_map/while/body/eval_jaxpr/sub | solution.py:109
  93.5 10.9 %fusion.74 = bf16[2,6,128,128]{2,3,1,0:T(8,128)(2,1)S(1)} fusion(bf16[2,4356,128]{2,1,0:T(8,128)(2,1)} %get-tuple-element.275, f32[2,6,128,4356]{2,3,1,0:T(8,128)} %get-tuple-element.239, f32[2,6,128]{2,1,0:T(8,128)S(1)} %get-tuple-element.240), kind=kOutput, calls=%fused_computation.18.clone.1 | convolution fusion | flops 1726427136 | bytes 29392896 | tf_op jit(solution)/shard_map/while/body/eval_jaxpr/kgts,ksd->tkgd/dot_general | solution.py:111
  108.3 3.4 or_and_fusion.2
  111.7 14.1 %fusion.72 = f32[2,128,6,4356]{1,3,2,0:T(8,128)} fusion(bf16[128,2,6,128]{0,3,2,1:T(8,128)(2,1)S(1)} %bitcast.110, bf16[2,4356,128]{2,1,0:T(8,128)(2,1)} %get-tuple-element.274), kind=kOutput, calls=%fused_computation.15.clone.1 | convolution fusion | flops 1712848896 | bytes 29386752 | tf_op jit(solution)/shard_map/while/body/eval_jaxpr/tkgd,ksd->kgts/dot_general | solution.py:104
  125.8 31.2 %fusion.73 = (f32[2,6,128]{2,1,0:T(8,128)S(1)}, f32[2,6,128,4356]{2,3,1,0:T(8,128)}) fusion(f32[2,128,6,4356]{1,3,2,0:T(8,128)} %fusion.72, pred[128,4356]{0,1:T(8,128)(4,1)S(1)} %or_and_fusion.2), kind=kOutput, calls=%fused_computation.105.clone.1 | output fusion | flops 40149252 | bytes 54090240 | tf_op jit(solution)/shard_map/while/body/eval_jaxpr/sub | solution.py:109
  157.0 10.9 %fusion.74 = bf16[2,6,128,128]{2,3,1,0:T(8,128)(2,1)S(1)} fusion(bf16[2,4356,128]{2,1,0:T(8,128)(2,1)} %get-tuple-element.275, f32[2,6,128,4356]{2,3,1,0:T(8,128)} %get-tuple-element.239, f32[2,6,128]{2,1,0:T(8,128)S(1)} %get-tuple-element.240), kind=kOutput, calls=%fused_computation.18.clone.1 | convolution fusion | flops 1726427136 | bytes 29392896 | tf_op jit(solution)/shard_map/while/body/eval_jaxpr/kgts,ksd->tkgd/dot_general | solution.py:111
  169.1 4.3 %multiply_reduce_fusion.1 = (f32[256]{0:T(256)S(1)}, f32[256,1536]{1,0:T(8,128)S(1)}) fusion(bf16[256,1536]{1,0:T(8,128)(2,1)} %bitcast.127, bf16[1536,1536]{1,0:T(8,128)(2,1)} %param.26, bf16[256,1536]{1,0:T(8,128)(2,1)} %param.17), kind=kOutput, calls=%fused_computation.45 | convolution fusion | flops 1209532160 | bytes 7865344 | tf_op jit(solution)/shard_map/dot_general | solution.py:118
  175.7 10.1 %gather_fusion = bf16[2048,1536]{1,0:T(8,128)(2,1)} fusion(bf16[257,1536]{1,0:T(8,128)(2,1)S(1)} %concatenate.28, s32[2048]{0:T(1024)S(1)} %copy-done.19), kind=kCustom, calls=%fused_computation | custom fusion | bytes 12591104 | tf_op jit(solution)/shard_map/gather | solution.py:132
  185.8 82.0 %all_to_all.10 = bf16[32,64,1536]{2,1,0:T(8,128)(2,1)S(1)} all-to-all(bf16[32,64,1536]{2,1,0:T(8,128)(2,1)} %bitcast.111), channel_id=1, replica_groups=mesh['rep'=4,'expert'=32] {'expert'}, dimensions={0} | all-to-all | bytes 12582912 | tf_op jit(solution)/shard_map/all_to_all | solution.py:133
  267.8 5.1 %fusion.19 = f32[2048,768]{1,0:T(8,128)S(1)} fusion(bf16[2048,1536]{1,0:T(8,128)(2,1)S(1)} %bitcast.116, bf16[1,1536,768]{2,1,0:T(8,128)(2,1)S(1)} %copy-done.24), kind=kOutput, calls=%fused_computation.34 | convolution fusion | flops 4831838208 | bytes 14942208 | tf_op jit(solution)/shard_map/dot_general | solution.py:135
  272.9 5.2 %multiply_convert_fusion = bf16[2048,768]{1,0:T(8,128)(2,1)S(1)} fusion(f32[2048,768]{1,0:T(8,128)S(1)} %fusion.19, bf16[2048,1536]{1,0:T(8,128)(2,1)S(1)} %bitcast.117, bf16[1,1536,768]{2,1,0:T(8,128)(2,1)S(1)} %copy-done.25), kind=kOutput, calls=%fused_computation.28 | convolution fusion | flops 4836556800 | bytes 18087936 | tf_op jit(solution)/shard_map/dot_general | solution.py:136
  278.2 6.9 %convolution_convert_fusion = bf16[2048,1536]{1,0:T(8,128)(2,1)} fusion(bf16[2048,768]{1,0:T(8,128)(2,1)S(1)} %multiply_convert_fusion, bf16[1,768,1536]{2,1,0:T(8,128)(2,1)S(1)} %copy-done), kind=kOutput, calls=%fused_computation.26 | convolution fusion | flops 4834983936 | bytes 11796480 | tf_op jit(solution)/shard_map/dot_general | solution.py:138
  285.1 5.3 %all-to-all-start.1 = ((bf16[32,64,1536]{2,1,0:T(8,128)(2,1)}), bf16[32,64,1536]{2,1,0:T(8,128)(2,1)}, u32[]{:S(2)}, u32[]{:S(2)}) async-start(bf16[32,64,1536]{2,1,0:T(8,128)(2,1)} %bitcast.115), calls=%async_computation.1 | async-start | bytes 12582912 | tf_op jit(solution)/shard_map/all_to_all | solution.py:141
  293.4 74.7 %all-to-all-done.1 = bf16[32,64,1536]{2,1,0:T(8,128)(2,1)} async-done(((bf16[32,64,1536]{2,1,0:T(8,128)(2,1)}), bf16[32,64,1536]{2,1,0:T(8,128)(2,1)}, u32[]{:S(2)}, u32[]{:S(2)}) %all-to-all-start.1) | async-done | bytes 6291488 | tf_op jit(solution)/shard_map/all_to_all | solution.py:141
  368.1 10.9 %gather_fusion.1 = bf16[1024,1536]{1,0:T(8,128)(2,1)} fusion(bf16[2048,1536]{1,0:T(8,128)(2,1)} %bitcast.28, s32[1024]{0:T(1024)S(1)} %broadcast_clamp_fusion), kind=kCustom, calls=%fused_computation.1 | custom fusion | bytes 6295552 | tf_op jit(solution)/shard_map/gather | solution.py:144
  379.0 6.7 %reshape.305 = f32[256,4,1536]{2,1,0:T(4,128)} reshape(bf16[1024,1536]{1,0:T(8,128)(2,1)} %gather_fusion.1) | data formatting | bytes 9437184 | tf_op jit(solution)/shard_map/convert_element_type | solution.py:154
  385.7 7.5 %multiply_reduce_fusion = f32[256,1536]{1,0:T(8,128)S(1)} fusion(f32[256,4,1536]{2,1,0:T(4,128)} %reshape.305, f32[256,4]{1,0:T(8,128)S(1)} %copy.58), kind=kLoop, calls=%fused_computation.27 | loop fusion | flops 2752512 | bytes 7868416 | tf_op jit(solution)/shard_map/reduce_sum | solution.py:154
  (121 shorter events, 31.8 us)
Async XLA Ops:
  0.6 277.5 %copy-start = (bf16[1,768,1536]{2,1,0:T(8,128)(2,1)S(1)}, bf16[1,768,1536]{2,1,0:T(8,128)(2,1)}, u32[]{:S(2)}) copy-start(bf16[1,768,1536]{2,1,0:T(8,128)(2,1)} %param.31) | copy-start | bytes 7077892
  0.6 26.9 %copy-start.11 = (bf16[256,1536]{1,0:T(8,128)(2,1)S(1)}, bf16[256,1536]{1,0:T(8,128)(2,1)}, u32[]{:S(2)}) copy-start(bf16[256,1536]{1,0:T(8,128)(2,1)} %param.17) | copy-start | bytes 2359300
  5.0 19.9 %copy-start.23 = (f32[256]{0:T(256)}, f32[256]{0:T(256)S(1)}, u32[]{:S(2)}) copy-start(f32[256]{0:T(256)S(1)} %add_rsqrt_fusion.1) | copy-start | bytes 3076
  18.1 6.9 %copy-start.20 = (s32[1024,1]{0,1:T(1,128)}, s32[1024,1]{0,1:T(1,128)S(1)}, u32[]{:S(2)}) copy-start(s32[1024,1]{0,1:T(1,128)S(1)} %compare_select_fusion) | copy-start | bytes 12292
  24.9 4.4 %copy-start.12 = (bf16[256,256]{0,1:T(8,128)(2,1)}, bf16[256,256]{0,1:T(8,128)(2,1)S(1)}, u32[]{:S(2)}) copy-start(bf16[256,256]{0,1:T(8,128)(2,1)S(1)} %convolution_convert_fusion.1) | copy-start | bytes 393220
  34.2 1.6 copy-start.5
  34.2 2.2 copy-start.6
  36.4 0.9 copy-start.14
  36.4 1.0 copy-start.15
  37.5 1.1 copy-start.7
  37.5 1.1 copy-start.9
  169.1 5.5 %copy-start.18 = (f32[1536]{0:T(1024)S(1)}, f32[1536]{0:T(1024)}, u32[]{:S(2)}) copy-start(f32[1536]{0:T(1024)} %convert_element_type.77) | copy-start | bytes 18436
  173.3 1.2 copy-start.3
  173.4 2.3 copy-start.19
  185.8 82.0 %copy-start.24 = (bf16[1,1536,768]{2,1,0:T(8,128)(2,1)S(1)}, bf16[1,1536,768]{2,1,0:T(8,128)(2,1)}, u32[]{:S(2)}) copy-start(bf16[1,1536,768]{2,1,0:T(8,128)(2,1)} %param.29) | copy-start | bytes 7077892
  267.8 5.1 %copy-start.25 = (bf16[1,1536,768]{2,1,0:T(8,128)(2,1)S(1)}, bf16[1,1536,768]{2,1,0:T(8,128)(2,1)}, u32[]{:S(2)}) copy-start(bf16[1,1536,768]{2,1,0:T(8,128)(2,1)} %param.30) | copy-start | bytes 7077892
  285.0 5.3 %copy-start.13 = (bf16[256,256]{0,1:T(8,128)(2,1)S(1)}, bf16[256,256]{0,1:T(8,128)(2,1)}, u32[]{:S(2)}) copy-start(bf16[256,256]{0,1:T(8,128)(2,1)} %copy-done.12) | copy-start | bytes 393220
  285.0 6.1 %copy-start.2 = (bf16[256,1536]{1,0:T(8,128)(2,1)S(1)}, bf16[256,1536]{1,0:T(8,128)(2,1)}, u32[]{:S(2)}) copy-start(bf16[256,1536]{1,0:T(8,128)(2,1)} %copy-done.1) | copy-start | bytes 2359300
  285.0 7.3 %copy-start.17 = (s32[256,4]{0,1:T(4,128)S(1)}, s32[256,4]{0,1:T(4,128)}, u32[]{:S(2)}) copy-start(s32[256,4]{0,1:T(4,128)} %param.18) | copy-start | bytes 12292
  285.0 7.6 %copy-start.8 = (bf16[256,2,64]{2,0,1:T(8,128)(2,1)S(1)}, bf16[256,2,64]{2,0,1:T(8,128)(2,1)}, u32[]{:S(2)}) copy-start(bf16[256,2,64]{2,0,1:T(8,128)(2,1)} %copy-done.7) | copy-start | bytes 196612
  285.1 7.6 %copy-start.10 = (bf16[256,2,64]{2,0,1:T(8,128)(2,1)S(1)}, bf16[256,2,64]{2,0,1:T(8,128)(2,1)}, u32[]{:S(2)}) copy-start(bf16[256,2,64]{2,0,1:T(8,128)(2,1)} %copy-done.9) | copy-start | bytes 196612
  285.1 8.3 %copy-start.21 = (s32[1024,1]{0,1:T(1,128)S(1)}, s32[1024,1]{0,1:T(1,128)}, u32[]{:S(2)}) copy-start(s32[1024,1]{0,1:T(1,128)} %copy-done.20) | copy-start | bytes 12292
  285.1 83.1 %all-to-all-start.1 = ((bf16[32,64,1536]{2,1,0:T(8,128)(2,1)}), bf16[32,64,1536]{2,1,0:T(8,128)(2,1)}, u32[]{:S(2)}, u32[]{:S(2)}) async-start(bf16[32,64,1536]{2,1,0:T(8,128)(2,1)} %bitcast.115), calls=%async_computation.1 | async-start | bytes 12582912 | tf_op jit(solution)/shard_map/all_to_all | solution.py:141
  385.7 7.5 %copy-start.4 = (f32[256,1536]{1,0:T(8,128)S(1)}, f32[256,1536]{1,0:T(8,128)}, u32[]{:S(2)}) copy-start(f32[256,1536]{1,0:T(8,128)} %copy-done.3) | copy-start | bytes 4718596
  (3 other events, 2.3 us)
where the time goes:
time: 401 us; the launch traced here: 395 us
  other arithmetic  100 us (25%)
  blocking collectives  82 us (20%)
  matrix products  80.9 us (20%)
  waiting for transfers between devices  74.7 us (19%)
  local copies, waits for them, and re-layouts  46.6 us (12%)
  starting transfers between devices  5.29 us (1%)
    all_to_all x1, blocking collectives, shards(): lax.all_to_all(send_buffer, 'expert', split_axis=0, concat_axis=0, tiled=...  82 us
    all_to_all x1, waiting for transfers between devices, shards(): lax.all_to_all(expert_out.reshape(received.shape), 'expert', split_axis=0...  74.7 us
    sub x2, other arithmetic, one_block(): expo = jnp.exp(scores - row_max)  62.5 us
    dot_general x2, matrix products, one_block(): jnp.einsum('tkgd,ksd->kgts', block_query, keys_all, preferred_element_typ...  28.1 us
    dot_general x2, matrix products, one_block(): jnp.einsum('kgts,ksd->tkgd', probability, values_all, preferred_element_t...  21.8 us
    gather x1, local copies, waits for them, and re-layouts, shards(): returned.reshape(expert_count * capacity_full, model_width)[flat_target]  10.9 us
    gather x1, local copies, waits for them, and re-layouts, shards(): padded_rows[source_table].reshape(expert_count, capacity_full, model_width)  10.1 us
    another operation x4, other arithmetic  9.37 us
  transfers between devices with their start and end apart: 1, of which 1 were waited for; matrix products, arithmetic and copies ran while one was open for 1% of the time, Pallas kernels for 0%

commit v1 on v0

v1 whole, which is shorter than its diff:
```python
import functools

import jax
import jax.numpy as jnp
from jax import lax
from jax.experimental import pallas as pl
from jax.experimental.pallas import tpu as pltpu
from jax.sharding import PartitionSpec as P

HEADS = 12
KV_HEADS = 2
HEAD_DIM = 128
TOP = 4
SINK = 4
WINDOW = 4096
CAP = 64
EXPERTS = 32

theta_base = 1000000.0
eps_norm = 1e-06

f32 = jnp.float32
bf16 = jnp.bfloat16
MB = 1024 * 1024


def dot(a, b):
    return jnp.dot(a, b, preferred_element_type=f32)


def dot_nt(a, b):
    return lax.dot_general(a, b, (((1,), (1,)), ((), ())), preferred_element_type=f32)


def rope_tables(positions):
    half = HEAD_DIM // 2
    exponent = jnp.arange(half, dtype=f32) * (2.0 / HEAD_DIM)
    inverse_freq = theta_base ** (-exponent)
    angles = positions.astype(f32)[:, None] * inverse_freq[None, :]
    cosine, sine = jnp.cos(angles), jnp.sin(angles)
    return jnp.concatenate([cosine, cosine], 1), jnp.concatenate([-sine, sine], 1)


def norm_rows(x, gain):
    mean_square = jnp.mean(x * x, axis=-1, keepdims=True)
    return (x * lax.rsqrt(mean_square + eps_norm) * gain).astype(bf16)


Q_BLOCK = 512


def qkv_kernel(tok_ref, gain_ref, wq_ref, wk_ref, wv_ref, cos_ref, sin_ref, q_ref, k_ref, v_ref, normed):
    cosine, sine = cos_ref[...], sin_ref[...]

    def rope(x):
        return (x * cosine + pltpu.roll(x, HEAD_DIM // 2, 1) * sine).astype(bf16)

    @pl.when(pl.program_id(0) == 0)
    def _():
        normed[...] = norm_rows(tok_ref[...].astype(f32), gain_ref[...].astype(f32))
        keys = dot(normed[...], wk_ref[...])
        for h in range(KV_HEADS):
            k_ref[:, h * HEAD_DIM:(h + 1) * HEAD_DIM] = rope(keys[:, h * HEAD_DIM:(h + 1) * HEAD_DIM])
        v_ref[...] = dot(normed[...], wv_ref[...]).astype(bf16)

    y = dot(normed[...], wq_ref[...])
    for h in range(Q_BLOCK // HEAD_DIM):
        q_ref[h] = rope(y[:, h * HEAD_DIM:(h + 1) * HEAD_DIM])


def project(tokens, gain, w_query, w_key, w_value, cosine, sine):
    rows, width = tokens.shape
    kv = w_key.shape[1]
    heads = Q_BLOCK // HEAD_DIM
    full = lambda a: pl.BlockSpec(a.shape, lambda i: (0,) * a.ndim)
    return pl.pallas_call(
        qkv_kernel,
        grid=(w_query.shape[1] // Q_BLOCK,),
        in_specs=[
            full(tokens), full(gain),
            pl.BlockSpec((width, Q_BLOCK), lambda i: (0, i)),
            full(w_key), full(w_value), full(cosine), full(sine),
        ],
        out_specs=[
            pl.BlockSpec((heads, rows, HEAD_DIM), lambda i: (i, 0, 0)),
            pl.BlockSpec((rows, kv), lambda i: (0, 0)),
            pl.BlockSpec((rows, kv), lambda i: (0, 0)),
        ],
        out_shape=[
            jax.ShapeDtypeStruct((HEADS, rows, HEAD_DIM), bf16),
            jax.ShapeDtypeStruct((rows, kv), bf16),
            jax.ShapeDtypeStruct((rows, kv), bf16),
        ],
        scratch_shapes=[pltpu.VMEM((rows, width), bf16)],
        compiler_params=pltpu.CompilerParams(vmem_limit_bytes=32 * MB),
        name="project",
    )(tokens, gain, w_query, w_key, w_value, cosine, sine)


KB = 512
HT = 3
EXTRA = 384
SCALE2 = HEAD_DIM ** (-0.5) * 1.4426950408889634
LOW = -1e30


def attn_kernel(past_ref, q_ref, kc_ref, vc_ref, kn_ref, vn_ref, o_ref, s_main, s_tail, m_scr, l_scr, acc, kx, vx):
    rows = kn_ref.shape[0]
    tile = HT * rows
    past = past_ref[0]

    @pl.when(pl.program_id(1) == 0)
    def _():
        for new, cache, out in ((kn_ref, kc_ref, kx), (vn_ref, vc_ref, vx)):
            out[0:rows] = new[...]
            out[rows:EXTRA] = jnp.zeros((EXTRA - rows, HEAD_DIM), bf16)
            out[rows:rows + SINK] = cache[0, 0, WINDOW:WINDOW + SINK]

    q = q_ref[...].reshape(tile, HEAD_DIM)
    row = lax.broadcasted_iota(jnp.int32, (tile, 1), 0) & (rows - 1)
    blocks = jnp.minimum((past + (KB - 1)) // KB, WINDOW // KB)

    def limit(slot):
        back = (slot - past) & (WINDOW - 1)
        return jnp.where(slot < past, jnp.where(slot < SINK, 1 << 20, back), 0)

    def lane_max(s):
        out = s[:, 0:128]
        for c in range(1, s.shape[1] // 128):
            out = jnp.maximum(out, s[:, c * 128:(c + 1) * 128])
        return out

    def lane_sum(s):
        out = s[:, 0:128]
        for c in range(1, s.shape[1] // 128):
            out = out + s[:, c * 128:(c + 1) * 128]
        return out

    column = lax.broadcasted_iota(jnp.int32, (1, EXTRA), 1)
    tail_limit = limit(column + (WINDOW - rows))
    tail_limit = jnp.where(column < rows, rows, jnp.where(column < rows + SINK, tail_limit, 0))
    first_row = jnp.where(column < rows, column, 0)
    s = dot_nt(q, kx[...]) * SCALE2
    s = jnp.where((row >= first_row) & (row < tail_limit), s, LOW)
    s_tail[...] = s
    m_scr[...] = lane_max(s)

    def score(j, carry):
        start = pl.multiple_of(j * KB, KB)
        s = dot_nt(q, kc_ref[0, 0, pl.ds(start, KB), :]) * SCALE2
        offset = (start - past) & (WINDOW - 1)
        plain = (start + KB <= past) & (offset >= rows) & (offset + KB <= WINDOW)

        @pl.when(plain)
        def _():
            s_main[j] = s
            m_scr[...] = jnp.maximum(m_scr[...], lane_max(s))

        @pl.when(jnp.logical_not(plain))
        def _():
            slot = lax.broadcasted_iota(jnp.int32, (1, KB), 1) + start
            masked = jnp.where(row < limit(slot), s, LOW)
            s_main[j] = masked
            m_scr[...] = jnp.maximum(m_scr[...], lane_max(masked))

        return carry

    lax.fori_loop(0, blocks, score, 0)
    top = jnp.max(m_scr[...], axis=1, keepdims=True)
    p = jnp.exp2(s_tail[...] - top)
    l_scr[...] = lane_sum(p)
    acc[...] = dot(p.astype(bf16), vx[...])

    def weigh(j, carry):
        start = pl.multiple_of(j * KB, KB)
        p = jnp.exp2(s_main[j] - top)
        l_scr[...] += lane_sum(p)
        acc[...] += dot(p.astype(bf16), vc_ref[0, 0, pl.ds(start, KB), :])
        return carry

    lax.fori_loop(0, blocks, weigh, 0)
    total = jnp.sum(l_scr[...], axis=1, keepdims=True)
    out = (acc[...] / total).astype(bf16)
    for h in range(HT):
        o_ref[:, h * HEAD_DIM:(h + 1) * HEAD_DIM] = out[h * rows:(h + 1) * rows]


def attend(past, q, cache_keys, cache_values, keys_new, values_new):
    rows = keys_new.shape[0]
    slots = cache_keys.shape[2]
    tile = HT * rows
    per_group = HEADS // KV_HEADS // HT
    cache_spec = pl.BlockSpec((1, 1, slots, HEAD_DIM), lambda g, i, *_: (0, g, 0, 0))
    new_spec = pl.BlockSpec((rows, HEAD_DIM), lambda g, i, *_: (0, g))
    return pl.pallas_call(
        attn_kernel,
        grid_spec=pltpu.PrefetchScalarGridSpec(
            num_scalar_prefetch=1,
            grid=(KV_HEADS, per_group),
            in_specs=[
                pl.BlockSpec((HT, rows, HEAD_DIM), lambda g, i, *_: (g * per_group + i, 0, 0)),
                cache_spec, cache_spec, new_spec, new_spec,
            ],
            out_specs=pl.BlockSpec((rows, HT * HEAD_DIM), lambda g, i, *_: (0, g * per_group + i)),
            scratch_shapes=[
                pltpu.VMEM((WINDOW // KB, tile, KB), f32),
                pltpu.VMEM((tile, EXTRA), f32),
                pltpu.VMEM((tile, 128), f32),
                pltpu.VMEM((tile, 128), f32),
                pltpu.VMEM((tile, HEAD_DIM), f32),
                pltpu.VMEM((EXTRA, HEAD_DIM), bf16),
                pltpu.VMEM((EXTRA, HEAD_DIM), bf16),
            ],
        ),
        out_shape=jax.ShapeDtypeStruct((rows, HEADS * HEAD_DIM), bf16),
        compiler_params=pltpu.CompilerParams(vmem_limit_bytes=48 * MB),
        name="attend",
    )(past, q, cache_keys, cache_values, keys_new, values_new)


O_BLOCK = 512
PACK = 4


def out_kernel(att_ref, wo_ref, tok_ref, gain_ref, wr_ref, routes_ref, routes_t_ref,
               mixed_ref, mix_ref, rank_ref, send_ref, ffn, rank_t):
    n = pl.program_id(0)
    rows, width = tok_ref.shape
    steps = width // O_BLOCK
    experts = wr_ref.shape[1]
    block = PACK * CAP

    @pl.when(n < steps)
    def _():
        cols = pl.ds(pl.multiple_of(n * O_BLOCK, O_BLOCK), O_BLOCK)
        mixed_ref[:, cols] = tok_ref[:, cols].astype(f32) + dot(att_ref[...], wo_ref[...])

    @pl.when(n == steps - 1)
    def _():
        ffn[...] = norm_rows(mixed_ref[...], gain_ref[...].astype(f32))
        expert = lax.broadcasted_iota(jnp.int32, (rows, experts), 1)
        expert_t = lax.broadcasted_iota(jnp.int32, (experts, rows), 0)
        named = routes_ref[:, 0:1] == expert
        named_t = routes_t_ref[0:1, :] == expert_t
        for j in range(1, TOP):
            named = named | (routes_ref[:, j:j + 1] == expert)
            named_t = named_t | (routes_t_ref[j:j + 1, :] == expert_t)
        a = lax.broadcasted_iota(jnp.int32, (rows, rows), 0)
        b = lax.broadcasted_iota(jnp.int32, (rows, rows), 1)
        one, zero = jnp.ones((), f32), jnp.zeros((), f32)
        before = jnp.where(b < a, one, zero).astype(bf16)
        before_t = jnp.where(a < b, one, zero).astype(bf16)
        ranks = dot(before, jnp.where(named, one, zero).astype(bf16))
        ranks_t = dot(jnp.where(named_t, one, zero).astype(bf16), before_t)
        rank_ref[...] = jnp.where(named, ranks, -1.0).astype(bf16)
        rank_t[...] = jnp.where(named_t, ranks_t, -1.0).astype(bf16)
        logits = dot(ffn[...], wr_ref[...])
        score = jnp.where(named, jax.nn.sigmoid(logits), 0.0)
        mix_ref[...] = score / jnp.sum(score, axis=1, keepdims=True)

    @pl.when(n >= steps)
    def _():
        first = (n - steps) * PACK
        slot = lax.broadcasted_iota(jnp.int32, (block, experts), 0)
        expert = lax.broadcasted_iota(jnp.int32, (block, experts), 1)
        spread = jnp.where(slot // CAP + first == expert, 1.0, 0.0).astype(bf16)
        wanted = dot(spread, rank_t[...])
        place = (lax.broadcasted_iota(jnp.int32, (block, rows), 0) % CAP).astype(f32)
        select = jnp.where(wanted == place, 1.0, 0.0).astype(bf16)
        send_ref[...] = dot(select, ffn[...]).astype(bf16)


def finish(attended, w_out, tokens, gain, w_router, routes, routes_t):
    rows, width = tokens.shape
    experts = w_router.shape[1]
    steps = width // O_BLOCK
    packs = experts // PACK
    full = lambda a: pl.BlockSpec(a.shape, lambda n: (0,) * a.ndim)
    whole = lambda shape: pl.BlockSpec(shape, lambda n: (0, 0))
    return pl.pallas_call(
        out_kernel,
        grid=(steps + packs,),
        in_specs=[
            full(attended),
            pl.BlockSpec((width, O_BLOCK), lambda n: (0, jnp.minimum(n, steps - 1))),
            full(tokens), full(gain), full(w_router), full(routes), full(routes_t),
        ],
        out_specs=[
            whole((rows, width)), whole((rows, experts)), whole((rows, experts)),
            pl.BlockSpec((PACK * CAP, width), lambda n: (jnp.maximum(n - steps, 0), 0)),
        ],
        out_shape=[
            jax.ShapeDtypeStruct((rows, width), f32),
            jax.ShapeDtypeStruct((rows, experts), f32),
            jax.ShapeDtypeStruct((rows, experts), bf16),
            jax.ShapeDtypeStruct((experts * CAP, width), bf16),
        ],
        scratch_shapes=[pltpu.VMEM((rows, width), bf16), pltpu.VMEM((experts, rows), bf16)],
        compiler_params=pltpu.CompilerParams(vmem_limit_bytes=32 * MB),
        name="finish",
    )(attended, w_out, tokens, gain, w_router, routes, routes_t)


def combine_kernel(mixed_ref, mix_ref, rank_ref, rows_ref, out_ref, total):
    n = pl.program_id(0)
    rows, experts = mix_ref.shape
    block = PACK * CAP
    expert = lax.broadcasted_iota(jnp.int32, (experts, block), 0)
    slot = lax.broadcasted_iota(jnp.int32, (experts, block), 1)
    spread = jnp.where(slot // CAP + n * PACK == expert, 1.0, 0.0).astype(bf16)
    mix = mix_ref[...]
    high = mix.astype(bf16)
    low = (mix - high.astype(f32)).astype(bf16)
    place = (lax.broadcasted_iota(jnp.int32, (rows, block), 1) % CAP).astype(f32)
    here = dot(rank_ref[...], spread) == place
    c_high = jnp.where(here, dot(high, spread), 0.0).astype(bf16)
    c_low = jnp.where(here, dot(low, spread), 0.0).astype(bf16)
    part = dot(c_high, rows_ref[...]) + dot(c_low, rows_ref[...])

    @pl.when(n == 0)
    def _():
        total[...] = part

    @pl.when(n > 0)
    def _():
        total[...] += part

    @pl.when(n == pl.num_programs(0) - 1)
    def _():
        out_ref[...] = (mixed_ref[...] + total[...]).astype(bf16)


def combine(mixed, mix, rank, returned):
    rows, width = mixed.shape
    experts = mix.shape[1]
    full = lambda a: pl.BlockSpec(a.shape, lambda n: (0,) * a.ndim)
    return pl.pallas_call(
        combine_kernel,
        grid=(experts // PACK,),
        in_specs=[full(mixed), full(mix), full(rank), pl.BlockSpec((PACK * CAP, width), lambda n: (n, 0))],
        out_specs=pl.BlockSpec((rows, width), lambda n: (0, 0)),
        out_shape=jax.ShapeDtypeStruct((rows, width), bf16),
        scratch_shapes=[pltpu.VMEM((rows, width), f32)],
        compiler_params=pltpu.CompilerParams(vmem_limit_bytes=32 * MB),
        name="combine",
    )(mixed, mix, rank, returned)


def shards(tokens, routes, history, cache_keys, cache_values, attn_gain, w_query, w_key, w_value, w_out,
           ffn_gain, w_router, expert_gate, expert_up, expert_down):
    rows, width = tokens.shape
    positions = history[0] + jnp.arange(rows, dtype=jnp.int32)
    cosine, sine = rope_tables(positions)
    q, keys_new, values_new = project(tokens, attn_gain[None], w_query, w_key, w_value, cosine, sine)
    attended = attend(history, q, cache_keys, cache_values, keys_new, values_new)
    mixed, mix, rank, send = finish(
        attended, w_out, tokens, ffn_gain[None], w_router, routes, jnp.transpose(routes)
    )
    experts = w_router.shape[1]
    received = lax.all_to_all(
        send.reshape(experts, CAP, width), "expert", split_axis=0, concat_axis=0, tiled=True
    )
    flat = received.reshape(-1, width)
    gate_part = dot(flat, expert_gate[0])
    up_part = dot(flat, expert_up[0])
    hidden = (jnp.maximum(gate_part, 0.0) * up_part).astype(bf16)
    expert_out = dot(hidden, expert_down[0]).astype(bf16)
    returned = lax.all_to_all(
        expert_out.reshape(received.shape), "expert", split_axis=0, concat_axis=0, tiled=True
    )
    layer_out = combine(mixed, mix, rank, returned.reshape(-1, width))
    return layer_out, keys_new, values_new


def solution(mesh):
    both = ("rep", "expert")
    in_specs = (
        P(both, None), P(both, None), P(both), P(both, None, None, None), P(both, None, None, None),
        P(), P(), P(), P(), P(), P(), P(),
        P("expert", None, None), P("expert", None, None), P("expert", None, None),
    )
    out_specs = (P(both, None), P(both, None), P(both, None))
    return jax.shard_map(shards, mesh=mesh, in_specs=in_specs, out_specs=out_specs, check_vma=False)
```

time: 401 us -> 243 us (0.61); the launches traced: 395 us -> 241 us
  other arithmetic: 100 us -> 0.69 us
  blocking collectives: 82 us -> 176 us
  waiting for transfers between devices: 74.7 us -> 0 us
  matrix products: 80.9 us -> 15.5 us
  Pallas kernels: 0 us -> 38.3 us
  local copies, waits for them, and re-layouts: 46.6 us -> 9.47 us
  starting transfers between devices: 5.29 us -> 0 us
    all_to_all x1 -> x2, blocking collectives: 82 us -> 176 us  [the longest x1 97.7 us: shards(): lax.all_to_all(send.reshape(experts, CAP, width), 'expert', split_axis=0,...]
    all_to_all x1 -> x0, waiting for transfers between devices: 74.7 us -> none  [shards(): lax.all_to_all(expert_out.reshape(received.shape), 'expert', split_axis=0...]
    dot_general x12 -> x3, matrix products: 80.9 us -> 15.5 us  [dot(): return jnp.dot(a, b, preferred_element_type=f32)]
    sub x3 -> x0, other arithmetic: 62.5 us -> none  [the longest x2 62.5 us: one_block(): expo = jnp.exp(scores - row_max)]
    pallas_call x0 -> x4, Pallas kernels: none -> 38.3 us  [the longest x1 20.2 us: attend(): pl.pallas_call(attn_kernel, grid_spec=pltpu.PrefetchScalarGridSpec(num_sc...]
    gather x2 -> x0, local copies, waits for them, and re-layouts: 21 us -> none  [the longest x1 10.9 us: shards(): returned.reshape(expert_count * capacity_full, model_width)[flat_target]]
    another operation x4 -> x0, other arithmetic: 9.37 us -> none
    reduce_sum x5 -> x0, other arithmetic: 8.98 us -> none  [the longest x1 7.51 us: shards(): jnp.sum(mix_weights[:, :, None] * expert_out.astype(jnp.float32), axis=1)]
  transfers between devices with their start and end apart: 1 -> 0, of which waited for: 1 -> 0; matrix products, arithmetic and copies ran while one was open for 1% -> 0% of each run, Pallas kernels for 0% -> 0%
where the time goes in v1:
time: 243 us; the launch traced here: 241 us
  blocking collectives  176 us (72%)
  Pallas kernels  38.3 us (16%)
  matrix products  15.5 us (6%)
  local copies, waits for them, and re-layouts  9.47 us (4%)
    all_to_all x1, blocking collectives, shards(): lax.all_to_all(send.reshape(experts, CAP, width), 'expert', split_axis=0,...  97.7 us
    all_to_all x1, blocking collectives, shards(): lax.all_to_all(expert_out.reshape(received.shape), 'expert', split_axis=0...  77.9 us
    pallas_call x1, Pallas kernels, attend(): pl.pallas_call(attn_kernel, grid_spec=pltpu.PrefetchScalarGridSpec(num_sc...  20.2 us
    dot_general x3, matrix products, dot(): return jnp.dot(a, b, preferred_element_type=f32)  15.5 us
    unnamed x28, local copies, waits for them, and re-layouts  8.09 us
    pallas_call x1, Pallas kernels, combine(): pl.pallas_call(combine_kernel, grid=(experts // PACK,), in_specs=[full(mi...  7.91 us
    pallas_call x1, Pallas kernels, finish(): pl.pallas_call(out_kernel, grid=(steps + packs,), in_specs=[full(attended...  6.79 us

profile of v1, /device:TPU:2, one launch (start us, length us, event | category | flops | bytes accessed | tf_op | source)
XLA Modules:
  0.0 241.2 jit_solution(5411286007034771230)
XLA Ops:
  0.6 0.0 copy-start
  1.5 0.7 broadcast_in_dim.8.gain_ref
  2.2 0.7 broadcast_in_dim.9.gain_ref
  2.9 0.8 copy.21.routes_ref
  3.7 1.1 copy.20.wr_ref
  4.8 0.0 copy-start.2
  4.8 2.0 copy.18.kc_ref
  6.9 2.0 copy.19.vc_ref
  8.9 0.5 fusion.4
  9.4 0.1 pad_maximum_fusion
  9.6 0.0 slice-start
  9.6 0.3 copy-done.1
  9.9 3.4 %project.1 = (bf16[12,256,128]{2,1,0:T(8,128)(2,1)S(1)}, bf16[256,256]{1,0:T(8,128)(2,1)}, bf16[256,256]{1,0:T(8,128)(2,1)}) custom-call(bf16[256,1536]{1,0:T(8,128)(2,1)S(1)} %copy-done.2, bf16[1,1536]{1,0:T(2,128)(2,1)S(1)} %broadcast_in_dim.8.gain_ref, bf16[1536,1536]{1,0:T(8,128)(2,1)S(1)} %copy-done.1, bf16[1536,256]{1,0:T(8,128)(2,1)S(1)} %copy-done.3, ...), custom_call_target="tpu_custom_call" | custom-call | tf_op jit(solution)/shard_map/project/pallas_call | solution.py:76
  13.3 0.0 copy-start.5
  13.3 0.9 copy-done.5
  14.2 0.9 copy-done.6
  15.1 20.2 %attend.1.att_ref = bf16[256,1536]{1,0:T(8,128)(2,1)S(1)} custom-call(s32[1]{0:T(128)} %copy.22.past_ref, bf16[12,256,128]{2,1,0:T(8,128)(2,1)S(1)} %get-tuple-element.10.q_ref, bf16[1,2,4100,128]{3,2,1,0:T(8,128)(2,1)S(1)} %copy.18.kc_ref, bf16[1,2,4100,128]{3,2,1,0:T(8,128)(2,1)S(1)} %copy.19.vc_ref, bf16[256,256]{1,0:T(8,128)(2,1)S(1)} %copy-done.5, ...), custom_call_target="tpu_custom_call" | custom-call | tf_op jit(solution)/shard_map/attend/pallas_call | solution.py:195
  35.3 6.8 %finish.1 = (f32[256,1536]{1,0:T(8,128)S(1)}, f32[256,32]{1,0:T(8,128)S(1)}, bf16[256,32]{1,0:T(8,128)(2,1)S(1)}, bf16[2048,1536]{1,0:T(8,128)(2,1)S(1)}) custom-call(bf16[256,1536]{1,0:T(8,128)(2,1)S(1)} %attend.1.att_ref, bf16[1536,1536]{1,0:T(8,128)(2,1)S(1)} %bitcast.22, bf16[256,1536]{1,0:T(8,128)(2,1)S(1)} %copy-done.2, ...), custom_call_target="tpu_custom_call" | custom-call | tf_op jit(solution)/shard_map/finish/pallas_call | solution.py:280
  42.1 97.7 %all_to_all.10 = bf16[32,64,1536]{2,1,0:T(8,128)(2,1)S(1)} all-to-all(bf16[32,64,1536]{2,1,0:T(8,128)(2,1)S(1)} %bitcast.20), channel_id=1, replica_groups=mesh['rep'=4,'expert'=32] {'expert'}, dimensions={0} | all-to-all | bytes 12582912 | tf_op jit(solution)/shard_map/all_to_all | solution.py:360
  139.9 5.1 %fusion.2 = f32[2048,768]{1,0:T(8,128)S(1)} fusion(bf16[2048,1536]{1,0:T(8,128)(2,1)S(1)} %bitcast.24, bf16[1,1536,768]{2,1,0:T(8,128)(2,1)S(1)} %copy-done.8), kind=kOutput, calls=%fused_computation.4 | convolution fusion | flops 4831838208 | bytes 14942208 | tf_op jit(solution)/shard_map/dot_general | solution.py:28
  145.0 5.2 %multiply_convert_fusion = bf16[2048,768]{1,0:T(8,128)(2,1)S(1)} fusion(f32[2048,768]{1,0:T(8,128)S(1)} %fusion.2, bf16[2048,1536]{1,0:T(8,128)(2,1)S(1)} %bitcast.25, bf16[1,1536,768]{2,1,0:T(8,128)(2,1)S(1)} %copy-done.9), kind=kOutput, calls=%fused_computation.1 | convolution fusion | flops 4836556800 | bytes 18087936 | tf_op jit(solution)/shard_map/dot_general | solution.py:28
  150.2 5.2 %convolution_convert_fusion = bf16[2048,1536]{1,0:T(8,128)(2,1)S(1)} fusion(bf16[2048,768]{1,0:T(8,128)(2,1)S(1)} %multiply_convert_fusion, bf16[1,768,1536]{2,1,0:T(8,128)(2,1)S(1)} %copy-done), kind=kOutput, calls=%fused_computation | convolution fusion | flops 4834983936 | bytes 11796480 | tf_op jit(solution)/shard_map/dot_general | solution.py:28
  155.5 77.9 %all_to_all.11 = bf16[32,64,1536]{2,1,0:T(8,128)(2,1)S(1)} all-to-all(bf16[32,64,1536]{2,1,0:T(8,128)(2,1)S(1)} %bitcast.26), channel_id=1, replica_groups=mesh['rep'=4,'expert'=32] {'expert'}, dimensions={0} | all-to-all | bytes 12582912 | tf_op jit(solution)/shard_map/all_to_all | solution.py:368
  233.3 7.9 %combine.1 = bf16[256,1536]{1,0:T(8,128)(2,1)} custom-call(f32[256,1536]{1,0:T(8,128)S(1)} %get-tuple-element.13.mixed_ref, f32[256,32]{1,0:T(8,128)S(1)} %get-tuple-element.14.mix_ref, bf16[256,32]{1,0:T(8,128)(2,1)S(1)} %get-tuple-element.15.rank_ref, bf16[2048,1536]{1,0:T(8,128)(2,1)S(1)} %bitcast.19), custom_call_target="tpu_custom_call" | custom-call | tf_op jit(solution)/shard_map/combine/pallas_call | solution.py:337
  (20 shorter events, 0.1 us)
Async XLA Ops:
  0.6 149.6 %copy-start = (bf16[1,768,1536]{2,1,0:T(8,128)(2,1)S(1)}, bf16[1,768,1536]{2,1,0:T(8,128)(2,1)}, u32[]{:S(2)}) copy-start(bf16[1,768,1536]{2,1,0:T(8,128)(2,1)} %param.29) | copy-start | bytes 7077892
  4.8 4.8 %copy-start.2 = (bf16[256,1536]{1,0:T(8,128)(2,1)S(1)}, bf16[256,1536]{1,0:T(8,128)(2,1)}, u32[]{:S(2)}) copy-start(bf16[256,1536]{1,0:T(8,128)(2,1)} %tok_ref.3) | copy-start | bytes 2359300
  4.8 4.8 %copy-start.3 = (bf16[1536,256]{1,0:T(8,128)(2,1)S(1)}, bf16[1536,256]{1,0:T(8,128)(2,1)}, u32[]{:S(2)}) copy-start(bf16[1536,256]{1,0:T(8,128)(2,1)} %wk_ref.1) | copy-start | bytes 2359300
  4.8 4.8 %copy-start.4 = (bf16[1536,256]{1,0:T(8,128)(2,1)S(1)}, bf16[1536,256]{1,0:T(8,128)(2,1)}, u32[]{:S(2)}) copy-start(bf16[1536,256]{1,0:T(8,128)(2,1)} %wv_ref.1) | copy-start | bytes 2359300
  6.9 3.0 %copy-start.1 = (bf16[1536,1536]{1,0:T(8,128)(2,1)S(1)}, bf16[1536,1536]{1,0:T(8,128)(2,1)}, u32[]{:S(2)}) copy-start(bf16[1536,1536]{1,0:T(8,128)(2,1)} %wq_ref.1) | copy-start | bytes 14155780
  9.6 25.7 %slice-start = ((s8[4718592]{0:T(1024)(128)(4,1)}), s8[4194304]{0:T(1024)(128)(4,1)S(1)}, s32[]{:S(2)}) async-start(s8[4718592]{0:T(1024)(128)(4,1)} %bitcast.21), calls=%async_computation.2 | async-start | bytes 8388608
  9.9 25.4 %slice-start.1 = ((s8[4718592]{0:T(1024)(128)(4,1)}), s8[524288]{0:T(1024)(128)(4,1)S(1)}, s32[]{:S(2)}) async-start(s8[4718592]{0:T(1024)(128)(4,1)} %bitcast.21), calls=%async_computation.3 | async-start | bytes 1048576
  13.3 22.0 %copy-start.7 = (s32[256,4]{0,1:T(4,128)S(1)}, s32[256,4]{0,1:T(4,128)}, u32[]{:S(2)}) copy-start(s32[256,4]{0,1:T(4,128)} %param.16) | copy-start | bytes 12292
  13.3 0.9 copy-start.5
  14.2 0.9 copy-start.6
  42.1 97.7 %copy-start.8 = (bf16[1,1536,768]{2,1,0:T(8,128)(2,1)S(1)}, bf16[1,1536,768]{2,1,0:T(8,128)(2,1)}, u32[]{:S(2)}) copy-start(bf16[1,1536,768]{2,1,0:T(8,128)(2,1)} %param.27) | copy-start | bytes 7077892
  139.9 5.1 %copy-start.9 = (bf16[1,1536,768]{2,1,0:T(8,128)(2,1)S(1)}, bf16[1,1536,768]{2,1,0:T(8,128)(2,1)}, u32[]{:S(2)}) copy-start(bf16[1,1536,768]{2,1,0:T(8,128)(2,1)} %param.28) | copy-start | bytes 7077892

commit v2 on v1

--- a/solution.py
+++ b/solution.py
@@ -219,131 +219,362 @@
 
 
 O_BLOCK = 512
-PACK = 4
-
-
-def out_kernel(att_ref, wo_ref, tok_ref, gain_ref, wr_ref, routes_ref, routes_t_ref,
-               mixed_ref, mix_ref, rank_ref, send_ref, ffn, rank_t):
+META = 128
+
+
+def out_kernel(att_ref, wo_ref, tok_ref, gain_ref, wr_ref, routes_ref, mixed_ref, pay_ref):
     n = pl.program_id(0)
     rows, width = tok_ref.shape
     steps = width // O_BLOCK
+    half = width // 2
     experts = wr_ref.shape[1]
-    block = PACK * CAP
-
-    @pl.when(n < steps)
-    def _():
-        cols = pl.ds(pl.multiple_of(n * O_BLOCK, O_BLOCK), O_BLOCK)
-        mixed_ref[:, cols] = tok_ref[:, cols].astype(f32) + dot(att_ref[...], wo_ref[...])
+    cols = pl.ds(pl.multiple_of(n * O_BLOCK, O_BLOCK), O_BLOCK)
+    mixed_ref[:, cols] = tok_ref[:, cols].astype(f32) + dot(att_ref[...], wo_ref[...])
 
     @pl.when(n == steps - 1)
     def _():
-        ffn[...] = norm_rows(mixed_ref[...], gain_ref[...].astype(f32))
+        ffn = norm_rows(mixed_ref[...], gain_ref[...].astype(f32))
         expert = lax.broadcasted_iota(jnp.int32, (rows, experts), 1)
-        expert_t = lax.broadcasted_iota(jnp.int32, (experts, rows), 0)
         named = routes_ref[:, 0:1] == expert
-        named_t = routes_t_ref[0:1, :] == expert_t
         for j in range(1, TOP):
             named = named | (routes_ref[:, j:j + 1] == expert)
-            named_t = named_t | (routes_t_ref[j:j + 1, :] == expert_t)
         a = lax.broadcasted_iota(jnp.int32, (rows, rows), 0)
         b = lax.broadcasted_iota(jnp.int32, (rows, rows), 1)
-        one, zero = jnp.ones((), f32), jnp.zeros((), f32)
-        before = jnp.where(b < a, one, zero).astype(bf16)
-        before_t = jnp.where(a < b, one, zero).astype(bf16)
-        ranks = dot(before, jnp.where(named, one, zero).astype(bf16))
-        ranks_t = dot(jnp.where(named_t, one, zero).astype(bf16), before_t)
-        rank_ref[...] = jnp.where(named, ranks, -1.0).astype(bf16)
-        rank_t[...] = jnp.where(named_t, ranks_t, -1.0).astype(bf16)
-        logits = dot(ffn[...], wr_ref[...])
-        score = jnp.where(named, jax.nn.sigmoid(logits), 0.0)
-        mix_ref[...] = score / jnp.sum(score, axis=1, keepdims=True)
-
-    @pl.when(n >= steps)
-    def _():
-        first = (n - steps) * PACK
-        slot = lax.broadcasted_iota(jnp.int32, (block, experts), 0)
-        expert = lax.broadcasted_iota(jnp.int32, (block, experts), 1)
-        spread = jnp.where(slot // CAP + first == expert, 1.0, 0.0).astype(bf16)
-        wanted = dot(spread, rank_t[...])
-        place = (lax.broadcasted_iota(jnp.int32, (block, rows), 0) % CAP).astype(f32)
-        select = jnp.where(wanted == place, 1.0, 0.0).astype(bf16)
-        send_ref[...] = dot(select, ffn[...]).astype(bf16)
-
-
-def finish(attended, w_out, tokens, gain, w_router, routes, routes_t):
+        before = jnp.where(b < a, 1.0, 0.0).astype(bf16)
+        rank = jnp.where(named, dot(before, jnp.where(named, 1.0, 0.0).astype(bf16)), -1.0).astype(bf16)
+        score = jnp.where(named, jax.nn.sigmoid(dot(ffn, wr_ref[...])), 0.0)
+        mix = score / jnp.sum(score, axis=1, keepdims=True)
+        high = mix.astype(bf16)
+        low = (mix - high.astype(f32)).astype(bf16)
+        source = lax.broadcasted_iota(jnp.int32, (experts, META), 0)
+        column = lax.broadcasted_iota(jnp.int32, (experts, META), 1)
+        put = lambda x, i: dot(x, jnp.where(column == source + i * experts, 1.0, 0.0).astype(bf16))
+        meta = (put(high, 0) + put(low, 1) + put(rank, 2)).astype(bf16)
+        for h in range(2):
+            pay_ref[h, :, 0:half] = ffn[:, h * half:(h + 1) * half]
+            pay_ref[h, :, half:half + META] = meta
+
+
+def finish(attended, w_out, tokens, gain, w_router, routes):
     rows, width = tokens.shape
-    experts = w_router.shape[1]
-    steps = width // O_BLOCK
-    packs = experts // PACK
     full = lambda a: pl.BlockSpec(a.shape, lambda n: (0,) * a.ndim)
-    whole = lambda shape: pl.BlockSpec(shape, lambda n: (0, 0))
     return pl.pallas_call(
         out_kernel,
-        grid=(steps + packs,),
+        grid=(width // O_BLOCK,),
         in_specs=[
-            full(attended),
-            pl.BlockSpec((width, O_BLOCK), lambda n: (0, jnp.minimum(n, steps - 1))),
-            full(tokens), full(gain), full(w_router), full(routes), full(routes_t),
+            full(attended), pl.BlockSpec((width, O_BLOCK), lambda n: (0, n)),
+            full(tokens), full(gain), full(w_router), full(routes),
         ],
         out_specs=[
-            whole((rows, width)), whole((rows, experts)), whole((rows, experts)),
-            pl.BlockSpec((PACK * CAP, width), lambda n: (jnp.maximum(n - steps, 0), 0)),
+            pl.BlockSpec((rows, width), lambda n: (0, 0)),
+            pl.BlockSpec((2, rows, width // 2 + META), lambda n: (0, 0, 0)),
         ],
         out_shape=[
             jax.ShapeDtypeStruct((rows, width), f32),
-            jax.ShapeDtypeStruct((rows, experts), f32),
-            jax.ShapeDtypeStruct((rows, experts), bf16),
-            jax.ShapeDtypeStruct((experts * CAP, width), bf16),
-        ],
-        scratch_shapes=[pltpu.VMEM((rows, width), bf16), pltpu.VMEM((experts, rows), bf16)],
+            jax.ShapeDtypeStruct((2, rows, width // 2 + META), bf16),
+        ],
         compiler_params=pltpu.CompilerParams(vmem_limit_bytes=32 * MB),
         name="finish",
-    )(attended, w_out, tokens, gain, w_router, routes, routes_t)
-
-
-def combine_kernel(mixed_ref, mix_ref, rank_ref, rows_ref, out_ref, total):
-    n = pl.program_id(0)
-    rows, experts = mix_ref.shape
-    block = PACK * CAP
-    expert = lax.broadcasted_iota(jnp.int32, (experts, block), 0)
-    slot = lax.broadcasted_iota(jnp.int32, (experts, block), 1)
-    spread = jnp.where(slot // CAP + n * PACK == expert, 1.0, 0.0).astype(bf16)
-    mix = mix_ref[...]
-    high = mix.astype(bf16)
-    low = (mix - high.astype(f32)).astype(bf16)
-    place = (lax.broadcasted_iota(jnp.int32, (rows, block), 1) % CAP).astype(f32)
-    here = dot(rank_ref[...], spread) == place
-    c_high = jnp.where(here, dot(high, spread), 0.0).astype(bf16)
-    c_low = jnp.where(here, dot(low, spread), 0.0).astype(bf16)
-    part = dot(c_high, rows_ref[...]) + dot(c_low, rows_ref[...])
-
-    @pl.when(n == 0)
-    def _():
-        total[...] = part
-
-    @pl.when(n > 0)
-    def _():
-        total[...] += part
-
-    @pl.when(n == pl.num_programs(0) - 1)
-    def _():
-        out_ref[...] = (mixed_ref[...] + total[...]).astype(bf16)
-
-
-def combine(mixed, mix, rank, returned):
+    )(attended, w_out, tokens, gain, w_router, routes)
+
+
+SIDE = 4
+GROUPS = 2 * SIDE
+
+
+def position():
+    me = lax.axis_index("expert")
+    return me // (2 * SIDE), (me // 2) % SIDE, me % 2
+
+
+def peer(axis, step, flip):
+    z, y, core = position()
+    if axis == 0:
+        z = (z + step) % SIDE
+    else:
+        y = (y + step) % SIDE
+    return z * 2 * SIDE + y * 2 + (core + flip) % 2
+
+
+def remote(src, dst, sems, i, to):
+    return pltpu.make_async_remote_copy(
+        src_ref=src, dst_ref=dst, send_sem=sems.at[0, i], recv_sem=sems.at[1, i],
+        device_id={"expert": to}, device_id_type=pl.DeviceIdType.MESH,
+    )
+
+
+def greet():
+    barrier = pltpu.get_barrier_semaphore()
+    others = [peer(0, 0, 1)]
+    for axis in range(2):
+        for step in (1, SIDE - 1):
+            for flip in range(2):
+                others.append(peer(axis, step, flip))
+    for other in others:
+        pl.semaphore_signal(barrier, inc=1, device_id={"expert": other}, device_id_type=pl.DeviceIdType.MESH)
+    pl.semaphore_wait(barrier, len(others))
+
+
+def group_expert(h, index):
+    z, y, core = position()
+    step, flip = index >> 1, index & 1
+    if h == 0:
+        y = (y + step) & (SIDE - 1)
+    else:
+        z = (z + step) & (SIDE - 1)
+    return z * (2 * SIDE) + y * 2 + ((core + flip) & 1)
+
+
+class Spread:
+    def __init__(self, h, src, dst, relay, sems, base):
+        axis = 1 - h
+        unit = lambda step, flip: src.at[h, step * 2 + flip]
+        slot = lambda step, flip: dst.at[h, (SIDE - step) % SIDE * 2 + flip]
+        self.relays = [
+            remote(unit(2, 0), relay.at[h, 0], sems, base, peer(axis, 1, 0)),
+            remote(unit(2, 1), relay.at[h, 1], sems, base + 1, peer(axis, SIDE - 1, 0)),
+        ]
+        self.direct = [
+            remote(unit(step, flip), slot(step, flip), sems, base + 2 + i, peer(axis, step, flip))
+            for i, (step, flip) in enumerate(((1, 0), (3, 0), (1, 1), (3, 1), (0, 1)))
+        ]
+        self.onward = [
+            remote(relay.at[h, 0], slot(2, 0), sems, base + 7, peer(axis, 1, 0)),
+            remote(relay.at[h, 1], slot(2, 1), sems, base + 8, peer(axis, SIDE - 1, 1)),
+        ]
+
+    def start(self):
+        for copy in self.relays + self.direct:
+            copy.start()
+
+    def forward(self):
+        for first, then in zip(self.relays, self.onward):
+            first.wait_recv()
+            then.start()
+
+    def finish(self):
+        for copy in self.direct + self.onward:
+            copy.wait_recv()
+        for copy in self.relays + self.direct + self.onward:
+            copy.wait_send()
+
+
+SPREAD_COPIES = 9
+
+
+def dispatch_kernel(pay_ref, x_ref, near_ref, send, relay, own_sem, sems):
+    rows = pay_ref.shape[1]
+    half = x_ref.shape[3]
+    mid = rows // 2
+    slots = GROUPS * CAP
+    greet()
+    top, low = pl.ds(0, mid), pl.ds(mid, mid)
+    own = [pltpu.make_async_copy(pay_ref.at[h], near_ref.at[h, 0], own_sem.at[h]) for h in range(2)]
+    gather, passing, spreads = [], [], []
+    for h in range(2):
+        up, down = peer(h, 1, 0), peer(h, SIDE - 1, 0)
+        base = h * 15
+        gather.append([
+            remote(pay_ref.at[h, top], near_ref.at[h, 3, top], sems, base, up),
+            remote(pay_ref.at[h, low], near_ref.at[h, 1, low], sems, base + 1, down),
+            remote(pay_ref.at[h, low], near_ref.at[h, 3, low], sems, base + 2, up),
+            remote(pay_ref.at[h, top], near_ref.at[h, 1, top], sems, base + 3, down),
+        ])
+        passing.append([
+            remote(near_ref.at[h, 3, top], near_ref.at[h, 2, top], sems, base + 4, up),
+            remote(near_ref.at[h, 1, low], near_ref.at[h, 2, low], sems, base + 5, down),
+        ])
+        spreads.append(Spread(h, send, x_ref, relay, sems, base + 6))
+    for i in range(4):
+        for h in range(2):
+            gather[h][i].start()
+    for h in range(2):
+        own[h].start()
+
+    place = (lax.broadcasted_iota(jnp.int32, (slots, rows), 0) % CAP).astype(f32)
+    group = lax.broadcasted_iota(jnp.int32, (slots, META), 0) // CAP
+    column = lax.broadcasted_iota(jnp.int32, (slots, META), 1)
+
+    def choose(h, s):
+        spread = jnp.where(column == group_expert(h, group) + 2 * 4 * GROUPS, 1.0, 0.0).astype(bf16)
+        wanted = dot_nt(spread, near_ref[h, s, :, half:half + META])
+        select = jnp.where(wanted == place, 1.0, 0.0).astype(bf16)
+        chosen = dot(select, near_ref[h, s, :, 0:half]).astype(bf16)
+        for g in range(GROUPS):
+            send[h, g, s * CAP:(s + 1) * CAP] = chosen[g * CAP:(g + 1) * CAP]
+
+    for h in range(2):
+        own[h].wait()
+        choose(h, 0)
+    for i in range(2):
+        for h in range(2):
+            gather[h][i].wait_recv()
+            passing[h][i].start()
+    for i, s in ((2, 3), (3, 1)):
+        for h in range(2):
+            gather[h][i].wait_recv()
+            choose(h, s)
+    for h in range(2):
+        for copy in passing[h]:
+            copy.wait_recv()
+        choose(h, 2)
+        spreads[h].start()
+    for h in range(2):
+        x_ref[h, 0] = send[h, 0]
+    for h in range(2):
+        spreads[h].forward()
+    for h in range(2):
+        spreads[h].finish()
+        for copy in gather[h] + passing[h]:
+            copy.wait_send()
+
+
+def dispatch(pay):
+    _, rows, wide = pay.shape
+    half = wide - META
+    vmem = pl.BlockSpec(memory_space=pltpu.VMEM)
+    return pl.pallas_call(
+        dispatch_kernel,
+        in_specs=[vmem],
+        out_specs=[vmem, vmem],
+        out_shape=[
+            jax.ShapeDtypeStruct((2, GROUPS, SIDE * CAP, half), bf16),
+            jax.ShapeDtypeStruct((2, SIDE, rows, wide), bf16),
+        ],
+        scratch_shapes=[
+            pltpu.VMEM((2, GROUPS, SIDE * CAP, half), bf16),
+            pltpu.VMEM((2, 2, SIDE * CAP, half), bf16),
+            pltpu.SemaphoreType.DMA((2,)),
+            pltpu.SemaphoreType.DMA((2, 30)),
+        ],
+        compiler_params=pltpu.CompilerParams(collective_id=1, has_side_effects=True, vmem_limit_bytes=40 * MB),
+        name="dispatch",
+    )(pay)
+
+
+def expert_kernel(x_ref, gate_ref, up_ref, down_ref, y_ref):
+    half = x_ref.shape[3]
+
+    def block(g, carry):
+        step, flip = g // 2, g % 2
+        spot = pl.ds(pl.multiple_of(step * CAP, CAP), CAP)
+        a = x_ref[0, g]
+        b = jnp.concatenate([x_ref[1, 2 * s + flip, spot] for s in range(SIDE)], axis=0)
+        gate = dot(a, gate_ref[0, 0:half]) + dot(b, gate_ref[0, half:2 * half])
+        up = dot(a, up_ref[0, 0:half]) + dot(b, up_ref[0, half:2 * half])
+        hidden = (jnp.maximum(gate, 0.0) * up).astype(bf16)
+        y_ref[0, g] = dot(hidden, down_ref[0, :, 0:half]).astype(bf16)
+        other = dot(hidden, down_ref[0, :, half:2 * half]).astype(bf16)
+        for s in range(SIDE):
+            y_ref[1, 2 * s + flip, spot] = other[s * CAP:(s + 1) * CAP]
+        return carry
+
+    lax.fori_loop(0, GROUPS, block, 0)
+
+
+def run_expert(x, gate, up, down):
+    vmem = pl.BlockSpec(memory_space=pltpu.VMEM)
+    return pl.pallas_call(
+        expert_kernel,
+        in_specs=[vmem] * 4,
+        out_specs=vmem,
+        out_shape=jax.ShapeDtypeStruct(x.shape, bf16),
+        compiler_params=pltpu.CompilerParams(vmem_limit_bytes=40 * MB),
+        name="expert",
+    )(x, gate, up, down)
+
+
+def return_kernel(y_ref, near_ref, mixed_ref, out_ref, back, relay, parts, passed, final, sems):
+    rows, width = mixed_ref.shape
+    half = width // 2
+    mid = rows // 2
+    slots = GROUPS * CAP
+    greet()
+    top, low = pl.ds(0, mid), pl.ds(mid, mid)
+    spreads, passing, last = [], [], []
+    for h in range(2):
+        up, down = peer(h, 1, 0), peer(h, SIDE - 1, 0)
+        base = h * 13
+        spreads.append(Spread(h, y_ref, back, relay, sems, base))
+        passing.append([
+            remote(parts.at[h, 1, top], passed.at[h, 0], sems, base + 9, up),
+            remote(parts.at[h, 1, low], passed.at[h, 1], sems, base + 10, down),
+        ])
+        last.append([
+            remote(parts.at[h, 0], final.at[h, 0], sems, base + 11, up),
+            remote(parts.at[h, 2], final.at[h, 1], sems, base + 12, down),
+        ])
+    for h in range(2):
+        spreads[h].start()
+    for h in range(2):
+        back[h, 0] = y_ref[h, 0]
+    for h in range(2):
+        spreads[h].forward()
+    for h in range(2):
+        spreads[h].finish()
+
+    place = (lax.broadcasted_iota(jnp.int32, (rows, slots), 1) % CAP).astype(f32)
+    column = lax.broadcasted_iota(jnp.int32, (META, slots), 0)
+    group = lax.broadcasted_iota(jnp.int32, (META, slots), 1) // CAP
+
+    def weigh(h, s):
+        meta = near_ref[h, s, :, half:half + META]
+        expert = group_expert(h, group)
+        take = lambda i: dot(meta, jnp.where(column == expert + i * 4 * GROUPS, 1.0, 0.0).astype(bf16))
+        here = take(2) == place
+        outs = jnp.concatenate([back[h, g, s * CAP:(s + 1) * CAP] for g in range(GROUPS)], axis=0)
+        high = jnp.where(here, take(0), 0.0).astype(bf16)
+        rest = jnp.where(here, take(1), 0.0).astype(bf16)
+        return dot(high, outs) + dot(rest, outs)
+
+    for h in range(2):
+        parts[h, 1] = weigh(h, 2).astype(bf16)
+        for copy in passing[h]:
+            copy.start()
+    sums = [[weigh(h, 1), weigh(h, 3)] for h in range(2)]
+    for h in range(2):
+        first, second = sums[h]
+        passing[h][0].wait_recv()
+        parts[h, 0, 0:mid] = (first[0:mid] + passed[h, 0].astype(f32)).astype(bf16)
+        parts[h, 0, mid:rows] = first[mid:rows].astype(bf16)
+        last[h][0].start()
+        passing[h][1].wait_recv()
+        parts[h, 2, 0:mid] = second[0:mid].astype(bf16)
+        parts[h, 2, mid:rows] = (second[mid:rows] + passed[h, 1].astype(f32)).astype(bf16)
+        last[h][1].start()
+    mine = [weigh(h, 0) for h in range(2)]
+    for h in range(2):
+        for copy in last[h]:
+            copy.wait_recv()
+        cols = slice(h * half, (h + 1) * half)
+        out_ref[:, cols] = (
+            mixed_ref[:, cols] + (mine[h] + final[h, 0].astype(f32) + final[h, 1].astype(f32))
+        ).astype(bf16)
+    for h in range(2):
+        for copy in passing[h] + last[h]:
+            copy.wait_send()
+
+
+def give_back(y, near, mixed):
     rows, width = mixed.shape
-    experts = mix.shape[1]
-    full = lambda a: pl.BlockSpec(a.shape, lambda n: (0,) * a.ndim)
+    half = width // 2
+    vmem = pl.BlockSpec(memory_space=pltpu.VMEM)
     return pl.pallas_call(
-        combine_kernel,
-        grid=(experts // PACK,),
-        in_specs=[full(mixed), full(mix), full(rank), pl.BlockSpec((PACK * CAP, width), lambda n: (n, 0))],
-        out_specs=pl.BlockSpec((rows, width), lambda n: (0, 0)),
+        return_kernel,
+        in_specs=[vmem] * 3,
+        out_specs=vmem,
         out_shape=jax.ShapeDtypeStruct((rows, width), bf16),
-        scratch_shapes=[pltpu.VMEM((rows, width), f32)],
-        compiler_params=pltpu.CompilerParams(vmem_limit_bytes=32 * MB),
-        name="combine",
-    )(mixed, mix, rank, returned)
+        scratch_shapes=[
+            pltpu.VMEM((2, GROUPS, SIDE * CAP, half), bf16),
+            pltpu.VMEM((2, 2, SIDE * CAP, half), bf16),
+            pltpu.VMEM((2, 3, rows, half), bf16),
+            pltpu.VMEM((2, 2, rows // 2, half), bf16),
+            pltpu.VMEM((2, 2, rows, half), bf16),
+            pltpu.SemaphoreType.DMA((2, 26)),
+        ],
+        compiler_params=pltpu.CompilerParams(collective_id=2, has_side_effects=True, vmem_limit_bytes=48 * MB),
+        name="give_back",
+    )(y, near, mixed)
 
 
 def shards(tokens, routes, history, cache_keys, cache_values, attn_gain, w_query, w_key, w_value, w_out,
@@ -353,22 +584,10 @@
     cosine, sine = rope_tables(positions)
     q, keys_new, values_new = project(tokens, attn_gain[None], w_query, w_key, w_value, cosine, sine)
     attended = attend(history, q, cache_keys, cache_values, keys_new, values_new)
-    mixed, mix, rank, send = finish(
-        attended, w_out, tokens, ffn_gain[None], w_router, routes, jnp.transpose(routes)
-    )
-    experts = w_router.shape[1]
-    received = lax.all_to_all(
-        send.reshape(experts, CAP, width), "expert", split_axis=0, concat_axis=0, tiled=True
-    )
-    flat = received.reshape(-1, width)
-    gate_part = dot(flat, expert_gate[0])
-    up_part = dot(flat, expert_up[0])
-    hidden = (jnp.maximum(gate_part, 0.0) * up_part).astype(bf16)
-    expert_out = dot(hidden, expert_down[0]).astype(bf16)
-    returned = lax.all_to_all(
-        expert_out.reshape(received.shape), "expert", split_axis=0, concat_axis=0, tiled=True
-    )
-    layer_out = combine(mixed, mix, rank, returned.reshape(-1, width))
+    mixed, pay = finish(attended, w_out, tokens, ffn_gain[None], w_router, routes)
+    x, near = dispatch(pay)
+    y = run_expert(x, expert_gate, expert_up, expert_down)
+    layer_out = give_back(y, near, mixed)
     return layer_out, keys_new, values_new
 
 

time: 243 us -> 207 us (0.85)
  blocking collectives: 176 us -> 0 us
  Pallas kernels: 38.3 us -> 181 us
  matrix products: 15.5 us -> 0 us
  local copies, waits for them, and re-layouts: 9.47 us -> 22.4 us
    all_to_all x2 -> x0, blocking collectives: 176 us -> none  [the longest x1 97.7 us: shards(): lax.all_to_all(send.reshape(experts, CAP, width), 'expert', split_axis=0,...]
    pallas_call x2 -> x4, Pallas kernels: 14.7 us -> 166 us  [the longest x1 83.2 us: dispatch(): pl.pallas_call(dispatch_kernel, in_specs=[vmem], out_specs=[vmem, vmem],...]
    dot_general x3 -> x0, matrix products: 15.5 us -> none  [dot(): return jnp.dot(a, b, preferred_element_type=f32)]
    unnamed x28 -> x43, local copies, waits for them, and re-layouts: 8.09 us -> 21 us
    pallas_call x1, Pallas kernels: 20.2 us -> 12.1 us  [attend(): pl.pallas_call(attn_kernel, grid_spec=pltpu.PrefetchScalarGridSpec(num_sc...]
where the time goes in v2:
time: 207 us; the launch traced here: 206 us
  Pallas kernels  181 us (87%)
  local copies, waits for them, and re-layouts  22.4 us (11%)
    pallas_call x1, Pallas kernels, dispatch(): pl.pallas_call(dispatch_kernel, in_specs=[vmem], out_specs=[vmem, vmem],...  83.2 us
    pallas_call x1, Pallas kernels, give_back(): pl.pallas_call(return_kernel, in_specs=[vmem] * 3, out_specs=vmem, out_sh...  60.3 us
    unnamed x43, local copies, waits for them, and re-layouts  21 us
    pallas_call x1, Pallas kernels, run_expert(): pl.pallas_call(expert_kernel, in_specs=[vmem] * 4, out_specs=vmem, out_sh...  19.2 us
    pallas_call x1, Pallas kernels, attend(): pl.pallas_call(attn_kernel, grid_spec=pltpu.PrefetchScalarGridSpec(num_sc...  12.1 us

profile of v2, /device:TPU:2, one launch (start us, length us, event | category | flops | bytes accessed | tf_op | source)
XLA Modules:
  0.0 205.9 jit_solution(8316934809558508155)
XLA Ops:
  1.3 0.7 broadcast_in_dim.8.gain_ref
  2.0 0.7 broadcast_in_dim.9.gain_ref
  2.7 1.5 copy.21.routes_ref
  4.2 0.5 fusion
  4.9 1.1 copy.20.wr_ref
  6.0 2.3 %copy-done.2 = bf16[1536,1536]{1,0:T(8,128)(2,1)S(1)} copy-done((bf16[1536,1536]{1,0:T(8,128)(2,1)S(1)}, bf16[1536,1536]{1,0:T(8,128)(2,1)}, u32[]{:S(2)}) %copy-start.2) | copy-done | bytes 4718616
  8.3 1.1 copy-done.3
  9.5 1.1 copy-done.10
  10.6 1.1 copy-done.11
  11.7 3.4 %project.1 = (bf16[12,256,128]{2,1,0:T(8,128)(2,1)S(1)}, bf16[256,256]{1,0:T(8,128)(2,1)}, bf16[256,256]{1,0:T(8,128)(2,1)}) custom-call(bf16[256,1536]{1,0:T(8,128)(2,1)S(1)} %copy-done.3, bf16[1,1536]{1,0:T(2,128)(2,1)S(1)} %broadcast_in_dim.8.gain_ref, bf16[1536,1536]{1,0:T(8,128)(2,1)S(1)} %copy-done.2, bf16[1536,256]{1,0:T(8,128)(2,1)S(1)} %copy-done.10, ...), custom_call_target="tpu_custom_call" | custom-call | tf_op jit(solution)/shard_map/project/pallas_call | solution.py:76
  15.2 0.3 copy.18.kc_ref
  15.4 1.3 copy-done.16
  17.0 0.9 copy-done.13
  17.9 12.1 %attend.1.att_ref = bf16[256,1536]{1,0:T(8,128)(2,1)S(1)} custom-call(s32[1]{0:T(128)} %copy.23.past_ref, bf16[12,256,128]{2,1,0:T(8,128)(2,1)S(1)} %get-tuple-element.10.q_ref, bf16[1,2,4100,128]{3,2,1,0:T(8,128)(2,1)S(1)} %copy.18.kc_ref, bf16[1,2,4100,128]{3,2,1,0:T(8,128)(2,1)S(1)} %copy.19.vc_ref, bf16[256,256]{1,0:T(8,128)(2,1)S(1)} %copy-done.13, ...), custom_call_target="tpu_custom_call" | custom-call | tf_op jit(solution)/shard_map/attend/pallas_call | solution.py:195
  30.1 0.9 copy-done.12
  31.0 3.1 %finish.1 = (f32[256,1536]{1,0:T(8,128)S(1)}, bf16[2,256,896]{2,1,0:T(8,128)(2,1)S(1)}) custom-call(bf16[256,1536]{1,0:T(8,128)(2,1)S(1)} %attend.1.att_ref, bf16[1536,1536]{1,0:T(8,128)(2,1)S(1)} %bitcast.3, bf16[256,1536]{1,0:T(8,128)(2,1)S(1)} %copy-done.4, bf16[1,1536]{1,0:T(2,128)(2,1)S(1)} %broadcast_in_dim.9.gain_ref, ...), custom_call_target="tpu_custom_call" | custom-call | tf_op jit(solution)/shard_map/finish/pallas_call | solution.py:261
  34.1 1.1 copy-done.8
  35.3 83.2 %dispatch.1 = (bf16[2,8,256,768]{3,2,1,0:T(8,128)(2,1)S(1)}, bf16[2,4,256,896]{3,2,1,0:T(8,128)(2,1)S(1)}) custom-call(bf16[2,256,896]{2,1,0:T(8,128)(2,1)S(1)} %get-tuple-element.13.pay_ref), custom_call_target="tpu_custom_call" | custom-call | tf_op jit(solution)/shard_map/dispatch/pallas_call | solution.py:436
  118.5 2.6 %copy-done.1 = bf16[2,8,256,768]{3,2,1,0:T(8,128)(2,1)} copy-done((bf16[2,8,256,768]{3,2,1,0:T(8,128)(2,1)}, bf16[2,8,256,768]{3,2,1,0:T(8,128)(2,1)S(1)}, u32[]{:S(2)}) %copy-start.1) | copy-done | bytes 6291480
  121.2 1.7 copy-done.7
  122.8 19.2 %expert.1.y_ref = bf16[2,8,256,768]{3,2,1,0:T(8,128)(2,1)S(1)} custom-call(bf16[2,8,256,768]{3,2,1,0:T(8,128)(2,1)} %copy-done.1, bf16[1,1536,768]{2,1,0:T(8,128)(2,1)S(1)} %copy-done.5, bf16[1,1536,768]{2,1,0:T(8,128)(2,1)S(1)} %copy-done.6, bf16[1,768,1536]{2,1,0:T(8,128)(2,1)S(1)} %copy-done.7), custom_call_target="tpu_custom_call" | custom-call | tf_op jit(solution)/shard_map/expert/pallas_call | solution.py:477
  142.0 2.6 %copy-done = bf16[2,8,256,768]{3,2,1,0:T(8,128)(2,1)} copy-done((bf16[2,8,256,768]{3,2,1,0:T(8,128)(2,1)}, bf16[2,8,256,768]{3,2,1,0:T(8,128)(2,1)S(1)}, u32[]{:S(2)}) %copy-start) | copy-done | bytes 6291480
  144.7 60.3 %give_back.1 = bf16[256,1536]{1,0:T(8,128)(2,1)S(1)} custom-call(bf16[2,8,256,768]{3,2,1,0:T(8,128)(2,1)} %copy-done, bf16[2,4,256,896]{3,2,1,0:T(8,128)(2,1)S(1)} %get-tuple-element.15.near_ref, f32[256,1536]{1,0:T(8,128)S(1)} %copy-done.9), custom_call_target="tpu_custom_call" | custom-call | tf_op jit(solution)/shard_map/give_back/pallas_call | solution.py:562
  205.0 0.9 copy.24
  (32 shorter events, 0.5 us)
Async XLA Ops:
  6.0 2.3 %copy-start.2 = (bf16[1536,1536]{1,0:T(8,128)(2,1)S(1)}, bf16[1536,1536]{1,0:T(8,128)(2,1)}, u32[]{:S(2)}) copy-start(bf16[1536,1536]{1,0:T(8,128)(2,1)} %wq_ref.1) | copy-start | bytes 14155780
  8.3 1.1 copy-start.3
  9.5 1.1 copy-start.10
  10.6 1.1 copy-start.11
  11.7 3.4 %copy-start.15 = (bf16[1,2,4100,128]{3,1,2,0:T(2,128)(2,1)S(1)}, bf16[1,2,4100,128]{3,1,2,0:T(2,128)(2,1)}, u32[]{:S(2)}) copy-start(bf16[1,2,4100,128]{3,1,2,0:T(2,128)(2,1)} %param.18) | copy-start | bytes 6297604
  15.1 1.6 copy-start.16
  15.2 14.9 %slice-start = ((s8[4718592]{0:T(1024)(128)(4,1)}), s8[4194304]{0:T(1024)(128)(4,1)S(1)}, s32[]{:S(2)}) async-start(s8[4718592]{0:T(1024)(128)(4,1)} %bitcast.2), calls=%async_computation | async-start | bytes 8388608
  16.7 1.2 copy-start.13
  16.7 1.2 copy-start.14
  16.7 13.4 %slice-start.1 = ((s8[4718592]{0:T(1024)(128)(4,1)}), s8[524288]{0:T(1024)(128)(4,1)S(1)}, s32[]{:S(2)}) async-start(s8[4718592]{0:T(1024)(128)(4,1)} %bitcast.2), calls=%async_computation.1 | async-start | bytes 1048576
  17.9 12.2 %copy-start.4 = (bf16[256,1536]{1,0:T(8,128)(2,1)S(1)}, bf16[256,1536]{1,0:T(8,128)(2,1)}, u32[]{:S(2)}) copy-start(bf16[256,1536]{1,0:T(8,128)(2,1)} %tok_ref.3) | copy-start | bytes 2359300
  30.1 0.9 copy-start.12
  31.0 90.1 %copy-start.5 = (bf16[1,1536,768]{2,1,0:T(8,128)(2,1)S(1)}, bf16[1,1536,768]{2,1,0:T(8,128)(2,1)}, u32[]{:S(2)}) copy-start(bf16[1,1536,768]{2,1,0:T(8,128)(2,1)} %gate_ref.1) | copy-start | bytes 7077892
  31.0 90.1 %copy-start.6 = (bf16[1,1536,768]{2,1,0:T(8,128)(2,1)S(1)}, bf16[1,1536,768]{2,1,0:T(8,128)(2,1)}, u32[]{:S(2)}) copy-start(bf16[1,1536,768]{2,1,0:T(8,128)(2,1)} %up_ref.1) | copy-start | bytes 7077892
  34.1 1.2 copy-start.8
  118.5 2.7 %copy-start.1 = (bf16[2,8,256,768]{3,2,1,0:T(8,128)(2,1)}, bf16[2,8,256,768]{3,2,1,0:T(8,128)(2,1)S(1)}, u32[]{:S(2)}) copy-start(bf16[2,8,256,768]{3,2,1,0:T(8,128)(2,1)S(1)} %get-tuple-element.14.x_ref) | copy-start | bytes 18874372
  121.2 1.7 copy-start.7
  122.8 21.9 %copy-start.9 = (f32[256,1536]{1,0:T(8,128)S(1)}, f32[256,1536]{1,0:T(8,128)}, u32[]{:S(2)}) copy-start(f32[256,1536]{1,0:T(8,128)} %copy-done.8) | copy-start | bytes 4718596
  142.0 2.7 %copy-start = (bf16[2,8,256,768]{3,2,1,0:T(8,128)(2,1)}, bf16[2,8,256,768]{3,2,1,0:T(8,128)(2,1)S(1)}, u32[]{:S(2)}) copy-start(bf16[2,8,256,768]{3,2,1,0:T(8,128)(2,1)S(1)} %expert.1.y_ref) | copy-start | bytes 18874372

commit v3 on v2

v3 whole, which is shorter than its diff:
```python
import functools

import jax
import jax.numpy as jnp
from jax import lax
from jax.experimental import pallas as pl
from jax.experimental.pallas import tpu as pltpu
from jax.sharding import PartitionSpec as P

HEADS = 12
KV_HEADS = 2
HEAD_DIM = 128
TOP = 4
SINK = 4
WINDOW = 4096
CAP = 64
EXPERTS = 32

theta_base = 1000000.0
eps_norm = 1e-06

f32 = jnp.float32
bf16 = jnp.bfloat16
MB = 1024 * 1024


def dot(a, b):
    return jnp.dot(a, b, preferred_element_type=f32)


def dot_nt(a, b):
    return lax.dot_general(a, b, (((1,), (1,)), ((), ())), preferred_element_type=f32)


def rope_tables(positions):
    half = HEAD_DIM // 2
    exponent = jnp.arange(half, dtype=f32) * (2.0 / HEAD_DIM)
    inverse_freq = theta_base ** (-exponent)
    angles = positions.astype(f32)[:, None] * inverse_freq[None, :]
    cosine, sine = jnp.cos(angles), jnp.sin(angles)
    return jnp.concatenate([cosine, cosine], 1), jnp.concatenate([-sine, sine], 1)


def norm_rows(x, gain):
    mean_square = jnp.mean(x * x, axis=-1, keepdims=True)
    return (x * lax.rsqrt(mean_square + eps_norm) * gain).astype(bf16)


Q_BLOCK = 512


def qkv_kernel(tok_ref, gain_ref, wq_ref, wk_ref, wv_ref, cos_ref, sin_ref, q_ref, k_ref, v_ref, k2_ref, v2_ref, normed):
    cosine, sine = cos_ref[...], sin_ref[...]

    def rope(x):
        return (x * cosine + pltpu.roll(x, HEAD_DIM // 2, 1) * sine).astype(bf16)

    @pl.when(pl.program_id(0) == 0)
    def _():
        normed[...] = norm_rows(tok_ref[...].astype(f32), gain_ref[0:1])
        keys = dot(normed[...], wk_ref[...])
        for h in range(KV_HEADS):
            turned = rope(keys[:, h * HEAD_DIM:(h + 1) * HEAD_DIM])
            k_ref[:, h * HEAD_DIM:(h + 1) * HEAD_DIM] = turned
            k2_ref[:, h * HEAD_DIM:(h + 1) * HEAD_DIM] = turned
        values = dot(normed[...], wv_ref[...]).astype(bf16)
        v_ref[...] = values
        v2_ref[...] = values

    y = dot(normed[...], wq_ref[...])
    for h in range(Q_BLOCK // HEAD_DIM):
        q_ref[h] = rope(y[:, h * HEAD_DIM:(h + 1) * HEAD_DIM])


def project(tokens, gain, w_query, w_key, w_value, cosine, sine):
    rows, width = tokens.shape
    kv = w_key.shape[1]
    heads = Q_BLOCK // HEAD_DIM
    full = lambda a: pl.BlockSpec(a.shape, lambda i: (0,) * a.ndim)
    return pl.pallas_call(
        qkv_kernel,
        grid=(w_query.shape[1] // Q_BLOCK,),
        in_specs=[
            full(tokens), full(gain),
            pl.BlockSpec((width, Q_BLOCK), lambda i: (0, i)),
            full(w_key), full(w_value), full(cosine), full(sine),
        ],
        out_specs=[
            pl.BlockSpec((heads, rows, HEAD_DIM), lambda i: (i, 0, 0)),
        ] + [pl.BlockSpec((rows, kv), lambda i: (0, 0))] * 4,
        out_shape=[
            jax.ShapeDtypeStruct((HEADS, rows, HEAD_DIM), bf16),
        ] + [jax.ShapeDtypeStruct((rows, kv), bf16)] * 4,
        scratch_shapes=[pltpu.VMEM((rows, width), bf16)],
        compiler_params=pltpu.CompilerParams(vmem_limit_bytes=32 * MB),
        name="project",
    )(tokens, gain, w_query, w_key, w_value, cosine, sine)


KB = 512
HT = 3
EXTRA = 384
SCALE2 = HEAD_DIM ** (-0.5) * 1.4426950408889634
LOW = -1e30


def attn_kernel(past_ref, q_ref, kc_ref, vc_ref, kn_ref, vn_ref, o_ref, s_main, s_tail, m_scr, l_scr, acc, kx, vx):
    rows = kn_ref.shape[0]
    tile = HT * rows
    past = past_ref[0]

    @pl.when(pl.program_id(1) == 0)
    def _():
        for new, cache, out in ((kn_ref, kc_ref, kx), (vn_ref, vc_ref, vx)):
            out[0:rows] = new[...]
            out[rows:EXTRA] = jnp.zeros((EXTRA - rows, HEAD_DIM), bf16)
            out[rows:rows + SINK] = cache[0, 0, WINDOW:WINDOW + SINK]

    q = q_ref[...].reshape(tile, HEAD_DIM)
    row = lax.broadcasted_iota(jnp.int32, (tile, 1), 0) & (rows - 1)
    blocks = jnp.minimum((past + (KB - 1)) // KB, WINDOW // KB)

    def limit(slot):
        back = (slot - past) & (WINDOW - 1)
        return jnp.where(slot < past, jnp.where(slot < SINK, 1 << 20, back), 0)

    def lane_max(s):
        out = s[:, 0:128]
        for c in range(1, s.shape[1] // 128):
            out = jnp.maximum(out, s[:, c * 128:(c + 1) * 128])
        return out

    def lane_sum(s):
        out = s[:, 0:128]
        for c in range(1, s.shape[1] // 128):
            out = out + s[:, c * 128:(c + 1) * 128]
        return out

    column = lax.broadcasted_iota(jnp.int32, (1, EXTRA), 1)
    tail_limit = limit(column + (WINDOW - rows))
    tail_limit = jnp.where(column < rows, rows, jnp.where(column < rows + SINK, tail_limit, 0))
    first_row = jnp.where(column < rows, column, 0)
    s = dot_nt(q, kx[...]) * SCALE2
    s = jnp.where((row >= first_row) & (row < tail_limit), s, LOW)
    s_tail[...] = s
    m_scr[...] = lane_max(s)

    def score(j, carry):
        start = pl.multiple_of(j * KB, KB)
        s = dot_nt(q, kc_ref[0, 0, pl.ds(start, KB), :]) * SCALE2
        offset = (start - past) & (WINDOW - 1)
        plain = (start + KB <= past) & (offset >= rows) & (offset + KB <= WINDOW)

        @pl.when(plain)
        def _():
            s_main[j] = s
            m_scr[...] = jnp.maximum(m_scr[...], lane_max(s))

        @pl.when(jnp.logical_not(plain))
        def _():
            slot = lax.broadcasted_iota(jnp.int32, (1, KB), 1) + start
            masked = jnp.where(row < limit(slot), s, LOW)
            s_main[j] = masked
            m_scr[...] = jnp.maximum(m_scr[...], lane_max(masked))

        return carry

    lax.fori_loop(0, blocks, score, 0)
    top = jnp.max(m_scr[...], axis=1, keepdims=True)
    p = jnp.exp2(s_tail[...] - top)
    l_scr[...] = lane_sum(p)
    acc[...] = dot(p.astype(bf16), vx[...])

    def weigh(j, carry):
        start = pl.multiple_of(j * KB, KB)
        p = jnp.exp2(s_main[j] - top)
        l_scr[...] += lane_sum(p)
        acc[...] += dot(p.astype(bf16), vc_ref[0, 0, pl.ds(start, KB), :])
        return carry

    lax.fori_loop(0, blocks, weigh, 0)
    total = jnp.sum(l_scr[...], axis=1, keepdims=True)
    out = (acc[...] / total).astype(bf16)
    for h in range(HT):
        o_ref[:, h * HEAD_DIM:(h + 1) * HEAD_DIM] = out[h * rows:(h + 1) * rows]


def attend(past, q, cache_keys, cache_values, keys_new, values_new):
    rows = keys_new.shape[0]
    slots = cache_keys.shape[2]
    tile = HT * rows
    per_group = HEADS // KV_HEADS // HT
    cache_spec = pl.BlockSpec((1, 1, slots, HEAD_DIM), lambda g, i, *_: (0, g, 0, 0))
    new_spec = pl.BlockSpec((rows, HEAD_DIM), lambda g, i, *_: (0, g))
    return pl.pallas_call(
        attn_kernel,
        grid_spec=pltpu.PrefetchScalarGridSpec(
            num_scalar_prefetch=1,
            grid=(KV_HEADS, per_group),
            in_specs=[
                pl.BlockSpec((HT, rows, HEAD_DIM), lambda g, i, *_: (g * per_group + i, 0, 0)),
                cache_spec, cache_spec, new_spec, new_spec,
            ],
            out_specs=pl.BlockSpec((rows, HT * HEAD_DIM), lambda g, i, *_: (0, g * per_group + i)),
            scratch_shapes=[
                pltpu.VMEM((WINDOW // KB, tile, KB), f32),
                pltpu.VMEM((tile, EXTRA), f32),
                pltpu.VMEM((tile, 128), f32),
                pltpu.VMEM((tile, 128), f32),
                pltpu.VMEM((tile, HEAD_DIM), f32),
                pltpu.VMEM((EXTRA, HEAD_DIM), bf16),
                pltpu.VMEM((EXTRA, HEAD_DIM), bf16),
            ],
        ),
        out_shape=jax.ShapeDtypeStruct((rows, HEADS * HEAD_DIM), bf16),
        compiler_params=pltpu.CompilerParams(vmem_limit_bytes=48 * MB),
        name="attend",
    )(past, q, cache_keys, cache_values, keys_new, values_new)


O_BLOCK = 512
META = 128


def out_kernel(att_ref, wo_ref, tok_ref, gain_ref, wr_t_ref, routes_t_ref, mixed_ref, pay_ref):
    n = pl.program_id(0)
    rows, width = tok_ref.shape
    steps = width // O_BLOCK
    half = width // 2
    experts = wr_t_ref.shape[0]
    cols = pl.ds(pl.multiple_of(n * O_BLOCK, O_BLOCK), O_BLOCK)
    mixed_ref[:, cols] = tok_ref[:, cols].astype(f32) + dot(att_ref[...], wo_ref[...])

    @pl.when(n == steps - 1)
    def _():
        ffn = norm_rows(mixed_ref[...], gain_ref[1:2])
        expert = lax.broadcasted_iota(jnp.int32, (experts, rows), 0)
        named_t = routes_t_ref[0:1] == expert
        for j in range(1, TOP):
            named_t = named_t | (routes_t_ref[j:j + 1] == expert)
        named_t = jnp.where(named_t, 1.0, 0.0).astype(bf16)
        a = lax.broadcasted_iota(jnp.int32, (rows, rows), 0)
        b = lax.broadcasted_iota(jnp.int32, (rows, rows), 1)
        named = dot_nt(jnp.where(a == b, 1.0, 0.0).astype(bf16), named_t) > 0.5
        ranks = dot_nt(jnp.where(b < a, 1.0, 0.0).astype(bf16), named_t)
        rank = jnp.where(named, ranks, -1.0).astype(bf16)
        score = jnp.where(named, jax.nn.sigmoid(dot_nt(ffn, wr_t_ref[...])), 0.0)
        mix = score / jnp.sum(score, axis=1, keepdims=True)
        high = mix.astype(bf16)
        low = (mix - high.astype(f32)).astype(bf16)
        source = lax.broadcasted_iota(jnp.int32, (experts, META), 0)
        column = lax.broadcasted_iota(jnp.int32, (experts, META), 1)
        put = lambda x, i: dot(x, jnp.where(column == source + i * experts, 1.0, 0.0).astype(bf16))
        meta = (put(high, 0) + put(low, 1) + put(rank, 2)).astype(bf16)
        for h in range(2):
            pay_ref[h, :, 0:half] = ffn[:, h * half:(h + 1) * half]
            pay_ref[h, :, half:half + META] = meta


def finish(attended, w_out, tokens, gain, router_t, routes_t):
    rows, width = tokens.shape
    full = lambda a: pl.BlockSpec(a.shape, lambda n: (0,) * a.ndim)
    return pl.pallas_call(
        out_kernel,
        grid=(width // O_BLOCK,),
        in_specs=[
            full(attended), pl.BlockSpec((width, O_BLOCK), lambda n: (0, n)),
            full(tokens), full(gain), full(router_t), full(routes_t),
        ],
        out_specs=[
            pl.BlockSpec((rows, width), lambda n: (0, 0)),
            pl.BlockSpec((2, rows, width // 2 + META), lambda n: (0, 0, 0)),
        ],
        out_shape=[
            jax.ShapeDtypeStruct((rows, width), f32),
            jax.ShapeDtypeStruct((2, rows, width // 2 + META), bf16),
        ],
        compiler_params=pltpu.CompilerParams(vmem_limit_bytes=32 * MB),
        name="finish",
    )(attended, w_out, tokens, gain, router_t, routes_t)


SIDE = 4
GROUPS = 2 * SIDE


def position():
    me = lax.axis_index("expert")
    return me // (2 * SIDE), (me // 2) % SIDE, me % 2


def peer(axis, step, flip):
    z, y, core = position()
    if axis == 0:
        z = (z + step) % SIDE
    else:
        y = (y + step) % SIDE
    return z * 2 * SIDE + y * 2 + (core + flip) % 2


def remote(src, dst, sems, i, to):
    return pltpu.make_async_remote_copy(
        src_ref=src, dst_ref=dst, send_sem=sems.at[0, i], recv_sem=sems.at[1, i],
        device_id={"expert": to}, device_id_type=pl.DeviceIdType.MESH,
    )


def greet():
    barrier = pltpu.get_barrier_semaphore()
    others = [peer(0, 0, 1)]
    for axis in range(2):
        for step in (1, SIDE - 1):
            for flip in range(2):
                others.append(peer(axis, step, flip))
    for other in others:
        pl.semaphore_signal(barrier, inc=1, device_id={"expert": other}, device_id_type=pl.DeviceIdType.MESH)
    pl.semaphore_wait(barrier, len(others))


def group_expert(h, index):
    z, y, core = position()
    step, flip = index >> 1, index & 1
    if h == 0:
        y = (y + step) & (SIDE - 1)
    else:
        z = (z + step) & (SIDE - 1)
    return z * (2 * SIDE) + y * 2 + ((core + flip) & 1)


class Spread:
    copies = 7

    def __init__(self, h, flip, src, dst, relay, sems, base):
        axis, rows = 1 - h, src.shape[2]
        top, low = pl.ds(0, rows // 2), pl.ds(rows // 2, rows // 2)
        unit = lambda step: (h, step * 2 + flip)
        slot = lambda step: (h, (SIDE - step) % SIDE * 2 + flip)
        self.relays, self.onward = [], []
        for i, (step, part) in enumerate(((1, top), (SIDE - 1, low))):
            self.relays.append(
                remote(src.at[unit(2) + (part,)], relay.at[h, flip, i], sems, base + i, peer(axis, step, 0)))
            self.onward.append(
                remote(relay.at[h, flip, i], dst.at[slot(2) + (part,)], sems, base + 2 + i, peer(axis, step, flip)))
        self.direct = [
            remote(src.at[unit(step)], dst.at[slot(step)], sems, base + 4 + i, peer(axis, step, flip))
            for i, step in enumerate((1, SIDE - 1, 0)[:2 + flip])
        ]

    def forward(self):
        for first, then in zip(self.relays, self.onward):
            first.wait_recv()
            then.start()

    def wait_recv(self):
        for copy in self.direct + self.onward:
            copy.wait_recv()

    def wait_src(self):
        for copy in self.relays + self.direct:
            copy.wait_send()

    def wait_onward(self):
        for copy in self.onward:
            copy.wait_send()


def start(copies):
    for copy in copies:
        copy.start()


def experts_kernel(pay_ref, mixed_ref, gate_hbm, up_hbm, down_hbm, out_ref, near, send, x, relay_out, back, relay_in,
                   sums, parts, passed, final, gate_w, up_w, down_w, own_sem, weight_sem, sems):
    rows, width = mixed_ref.shape
    half = width // 2
    mid = rows // 2
    slots = SIDE * CAP
    top, low = pl.ds(0, mid), pl.ds(mid, mid)
    both = (0, 1)
    weights = [
        pltpu.make_async_copy(src.at[0], dst, weight_sem.at[i])
        for i, (src, dst) in enumerate(((gate_hbm, gate_w), (up_hbm, up_w), (down_hbm, down_w)))
    ]
    own = [pltpu.make_async_copy(pay_ref.at[h], near.at[h, 0], own_sem.at[h]) for h in both]
    start(own)
    greet()
    gather, passing, out, home, pass_back, last = [], [], [], [], [], []
    for h in both:
        up, down = peer(h, 1, 0), peer(h, SIDE - 1, 0)
        base = h * 38
        gather.append([
            remote(pay_ref.at[h, top], near.at[h, 3, top], sems, base, up),
            remote(pay_ref.at[h, low], near.at[h, 1, low], sems, base + 1, down),
            remote(pay_ref.at[h, low], near.at[h, 3, low], sems, base + 2, up),
            remote(pay_ref.at[h, top], near.at[h, 1, top], sems, base + 3, down),
        ])
        passing.append([
            remote(near.at[h, 3, top], near.at[h, 2, top], sems, base + 4, up),
            remote(near.at[h, 1, low], near.at[h, 2, low], sems, base + 5, down),
        ])
        out.append([Spread(h, d, send, x, relay_out, sems, base + 6 + d * Spread.copies) for d in both])
        home.append([Spread(h, d, send, back, relay_in, sems, base + 20 + d * Spread.copies) for d in both])
        pass_back.append([
            remote(parts.at[h, 1, top], passed.at[h, 0], sems, base + 34, up),
            remote(parts.at[h, 1, low], passed.at[h, 1], sems, base + 35, down),
        ])
        last.append([
            remote(parts.at[h, 0], final.at[h, 0], sems, base + 36, up),
            remote(parts.at[h, 2], final.at[h, 1], sems, base + 37, down),
        ])

    for i in range(4):
        for h in both:
            gather[h][i].start()
    start(weights)

    place = (lax.broadcasted_iota(jnp.int32, (slots, rows), 0) % CAP).astype(f32)
    step_rows = (lax.broadcasted_iota(jnp.int32, (slots, META), 0) // CAP) * 2
    meta_column = lax.broadcasted_iota(jnp.int32, (slots, META), 1)

    def choose(h, s, d):
        spread = jnp.where(meta_column == group_expert(h, step_rows + d) + 2 * EXPERTS, 1.0, 0.0).astype(bf16)
        wanted = dot_nt(spread, near[h, s, :, half:half + META])
        select = jnp.where(wanted == place, 1.0, 0.0).astype(bf16)
        chosen = dot(select, near[h, s, :, 0:half]).astype(bf16)
        for k in range(SIDE):
            send[h, 2 * k + d, s * CAP:(s + 1) * CAP] = chosen[k * CAP:(k + 1) * CAP]

    for h in both:
        own[h].wait()
        for d in both:
            choose(h, 0, d)
    for i in both:
        for h in both:
            gather[h][i].wait_recv()
            passing[h][i].start()
    for i, s in ((2, 3), (3, 1)):
        for h in both:
            gather[h][i].wait_recv()
            for d in both:
                choose(h, s, d)
    for h in both:
        for copy in passing[h]:
            copy.wait_recv()
        choose(h, 2, 0)
        start(out[h][0].relays + out[h][0].direct)
    for h in both:
        choose(h, 2, 1)
        start(out[h][1].relays)
    for h in both:
        x[h, 0] = send[h, 0]
    for d in both:
        for h in both:
            out[h][d].forward()
    for h in both:
        start(out[h][1].direct)
    for copy in weights:
        copy.wait()

    def run_expert(d):
        def block(k, carry):
            spot = pl.ds(pl.multiple_of(k * CAP, CAP), CAP)
            a = x[0, 2 * k + d]
            b = jnp.concatenate([x[1, 2 * s + d, spot] for s in range(SIDE)], axis=0)
            gate = dot(a, gate_w[0:half]) + dot(b, gate_w[half:2 * half])
            up = dot(a, up_w[0:half]) + dot(b, up_w[half:2 * half])
            hidden = (jnp.maximum(gate, 0.0) * up).astype(bf16)
            send[0, 2 * k + d] = dot(hidden, down_w[:, 0:half]).astype(bf16)
            other = dot(hidden, down_w[:, half:2 * half]).astype(bf16)
            for s in range(SIDE):
                send[1, 2 * s + d, spot] = other[s * CAP:(s + 1) * CAP]
            return carry

        for h in both:
            out[h][d].wait_recv()
            out[h][d].wait_src()
        lax.fori_loop(0, SIDE, block, 0)

    run_expert(0)
    for h in both:
        start(home[h][0].relays + home[h][0].direct)
    run_expert(1)
    for h in both:
        start(home[h][1].relays)
    for h in both:
        back[h, 0] = send[h, 0]
    for d in both:
        for h in both:
            home[h][d].forward()
    for h in both:
        start(home[h][1].direct)

    place_back = (lax.broadcasted_iota(jnp.int32, (rows, slots), 1) % CAP).astype(f32)
    meta_row = lax.broadcasted_iota(jnp.int32, (META, slots), 0)
    step_columns = (lax.broadcasted_iota(jnp.int32, (META, slots), 1) // CAP) * 2

    def weigh(h, s, d):
        meta = near[h, s, :, half:half + META]
        expert = group_expert(h, step_columns + d)
        take = lambda i: dot(meta, jnp.where(meta_row == expert + i * EXPERTS, 1.0, 0.0).astype(bf16))
        here = take(2) == place_back
        outs = jnp.concatenate([back[h, 2 * k + d, s * CAP:(s + 1) * CAP] for k in range(SIDE)], axis=0)
        high = jnp.where(here, take(0), 0.0).astype(bf16)
        rest = jnp.where(here, take(1), 0.0).astype(bf16)
        return dot(high, outs) + dot(rest, outs)

    for h in both:
        home[h][0].wait_recv()
        for s in range(SIDE):
            sums[h, s] = weigh(h, s, 0)
    for h in both:
        home[h][1].wait_recv()
        parts[h, 1] = (sums[h, 2] + weigh(h, 2, 1)).astype(bf16)
        start(pass_back[h])
    for h in both:
        for s in (1, 3):
            sums[h, s] += weigh(h, s, 1)
    for h in both:
        pass_back[h][0].wait_recv()
        parts[h, 0, 0:mid] = (sums[h, 1, 0:mid] + passed[h, 0].astype(f32)).astype(bf16)
        parts[h, 0, mid:rows] = sums[h, 1, mid:rows].astype(bf16)
        last[h][0].start()
        pass_back[h][1].wait_recv()
        parts[h, 2, 0:mid] = sums[h, 3, 0:mid].astype(bf16)
        parts[h, 2, mid:rows] = (sums[h, 3, mid:rows] + passed[h, 1].astype(f32)).astype(bf16)
        last[h][1].start()
    for h in both:
        sums[h, 0] += weigh(h, 0, 1)
    for h in both:
        for copy in last[h]:
            copy.wait_recv()
        cols = slice(h * half, (h + 1) * half)
        out_ref[:, cols] = (
            mixed_ref[:, cols] + (sums[h, 0] + final[h, 0].astype(f32) + final[h, 1].astype(f32))
        ).astype(bf16)
    for h in both:
        for copy in gather[h] + passing[h] + pass_back[h] + last[h]:
            copy.wait_send()
        for d in both:
            out[h][d].wait_onward()
            home[h][d].wait_src()
            home[h][d].wait_onward()


def run_experts(pay, mixed, gate, up, down):
    rows, width = mixed.shape
    half, ff = width // 2, gate.shape[2]
    vmem = pl.BlockSpec(memory_space=pltpu.VMEM)
    hbm = pl.BlockSpec(memory_space=pl.ANY)
    unit = (SIDE * CAP, half)
    part = (SIDE * CAP // 2, half)
    return pl.pallas_call(
        experts_kernel,
        in_specs=[vmem, vmem, hbm, hbm, hbm],
        out_specs=vmem,
        out_shape=jax.ShapeDtypeStruct((rows, width), bf16),
        scratch_shapes=[
            pltpu.VMEM((2, SIDE, rows, half + META), bf16),
            pltpu.VMEM((2, GROUPS) + unit, bf16),
            pltpu.VMEM((2, GROUPS) + unit, bf16),
            pltpu.VMEM((2, 2, 2) + part, bf16),
            pltpu.VMEM((2, GROUPS) + unit, bf16),
            pltpu.VMEM((2, 2, 2) + part, bf16),
            pltpu.VMEM((2, SIDE, rows, half), f32),
            pltpu.VMEM((2, 3, rows, half), bf16),
            pltpu.VMEM((2, 2, rows // 2, half), bf16),
            pltpu.VMEM((2, 2, rows, half), bf16),
            pltpu.VMEM((width, ff), bf16),
            pltpu.VMEM((width, ff), bf16),
            pltpu.VMEM((ff, width), bf16),
            pltpu.SemaphoreType.DMA((2,)),
            pltpu.SemaphoreType.DMA((3,)),
            pltpu.SemaphoreType.DMA((2, 76)),
        ],
        compiler_params=pltpu.CompilerParams(collective_id=1, has_side_effects=True, vmem_limit_bytes=50 * MB),
        name="experts",
    )(pay, mixed, gate, up, down)


def shards(tokens, routes, history, cache_keys, cache_values, attn_gain, w_query, w_key, w_value, w_out,
           ffn_gain, w_router, expert_gate, expert_up, expert_down):
    rows, width = tokens.shape
    positions = history[0] + jnp.arange(rows, dtype=jnp.int32)
    cosine, sine = rope_tables(positions)
    gains = jnp.stack([attn_gain, ffn_gain]).astype(f32)
    q, keys_new, values_new, keys_near, values_near = project(tokens, gains, w_query, w_key, w_value, cosine, sine)
    attended = attend(history, q, cache_keys, cache_values, keys_near, values_near)
    mixed, pay = finish(attended, w_out, tokens, gains, jnp.transpose(w_router), jnp.transpose(routes))
    layer_out = run_experts(pay, mixed, expert_gate, expert_up, expert_down)
    return layer_out, keys_new, values_new


def solution(mesh):
    both = ("rep", "expert")
    in_specs = (
        P(both, None), P(both, None), P(both), P(both, None, None, None), P(both, None, None, None),
        P(), P(), P(), P(), P(), P(), P(),
        P("expert", None, None), P("expert", None, None), P("expert", None, None),
    )
    out_specs = (P(both, None), P(both, None), P(both, None))
    return jax.shard_map(shards, mesh=mesh, in_specs=in_specs, out_specs=out_specs, check_vma=False)
```

time: 207 us -> 168 us (0.81)
  Pallas kernels: 181 us -> 155 us
  local copies, waits for them, and re-layouts: 22.4 us -> 9.86 us
    pallas_call x3 -> x1, Pallas kernels: 163 us -> 136 us  [run_experts(): pl.pallas_call(experts_kernel, in_specs=[vmem, vmem, hbm, hbm, hbm], out_...]
    unnamed x43 -> x25, local copies, waits for them, and re-layouts: 21 us -> 8.47 us
where the time goes in v3:
time: 168 us; the launch traced here: 167 us
  Pallas kernels  155 us (92%)
  local copies, waits for them, and re-layouts  9.86 us (6%)
    pallas_call x1, Pallas kernels, run_experts(): pl.pallas_call(experts_kernel, in_specs=[vmem, vmem, hbm, hbm, hbm], out_...  136 us
    pallas_call x1, Pallas kernels, attend(): pl.pallas_call(attn_kernel, grid_spec=pltpu.PrefetchScalarGridSpec(num_sc...  12.1 us
    unnamed x25, local copies, waits for them, and re-layouts  8.47 us
    pallas_call x1, Pallas kernels, project(): pl.pallas_call(qkv_kernel, grid=(w_query.shape[1] // Q_BLOCK,), in_specs=...  3.39 us

profile of v3, /device:TPU:2, one launch (start us, length us, event | category | flops | bytes accessed | tf_op | source)
XLA Modules:
  0.0 166.8 jit_solution(2679264666725954408)
XLA Ops:
  1.3 0.7 stack.9
  2.0 0.7 stack.10
  2.7 0.5 fusion
  3.3 0.1 pad_maximum_fusion
  3.4 0.0 copy-start
  3.4 2.3 %copy-done = bf16[1536,1536]{1,0:T(8,128)(2,1)S(1)} copy-done((bf16[1536,1536]{1,0:T(8,128)(2,1)S(1)}, bf16[1536,1536]{1,0:T(8,128)(2,1)}, u32[]{:S(2)}) %copy-start) | copy-done | bytes 4718616
  5.7 1.1 copy-done.1
  6.9 1.1 copy-done.3
  8.0 1.1 copy-done.4
  9.1 3.4 %project.1 = (bf16[12,256,128]{2,1,0:T(8,128)(2,1)S(1)}, bf16[256,256]{1,0:T(8,128)(2,1)}, bf16[256,256]{1,0:T(8,128)(2,1)}, bf16[256,256]{1,0:T(8,128)(2,1)S(1)}, bf16[256,256]{1,0:T(8,128)(2,1)S(1)}) custom-call(bf16[256,1536]{1,0:T(8,128)(2,1)S(1)} %copy-done.1, f32[2,1536]{1,0:T(2,128)S(1)} %maximum_convert_fusion.gain_ref, ...), custom_call_target="tpu_custom_call" | custom-call | tf_op jit(solution)/shard_map/project/pallas_call | solution.py:80
  12.5 0.0 copy-start.8
  12.6 0.0 slice-start
  12.6 0.3 copy.18.kc_ref
  12.9 1.3 copy-done.8
  14.1 0.3 copy.19.vc_ref
  14.4 0.0 copy-start.2
  14.4 0.0 copy-start.5
  14.4 0.0 copy-start.6
  14.4 12.1 %attend.1.att_ref = bf16[256,1536]{1,0:T(8,128)(2,1)S(1)} custom-call(s32[1]{0:T(128)} %copy.21.past_ref, bf16[12,256,128]{2,1,0:T(8,128)(2,1)S(1)} %get-tuple-element.10.q_ref, bf16[1,2,4100,128]{3,2,1,0:T(8,128)(2,1)S(1)} %copy.18.kc_ref, bf16[1,2,4100,128]{3,2,1,0:T(8,128)(2,1)S(1)} %copy.19.vc_ref, bf16[256,256]{1,0:T(8,128)(2,1)S(1)} %get-tuple-element.11.kn_ref, ...), custom_call_target="tpu_custom_call" | custom-call | tf_op jit(solution)/shard_map/attend/pallas_call | solution.py:195
  26.6 0.0 slice-done
  26.6 0.0 slice-done.1
  26.7 3.0 %finish.1 = (f32[256,1536]{1,0:T(8,128)S(1)}, bf16[2,256,896]{2,1,0:T(8,128)(2,1)S(1)}) custom-call(bf16[256,1536]{1,0:T(8,128)(2,1)S(1)} %attend.1.att_ref, bf16[1536,1536]{1,0:T(8,128)(2,1)S(1)} %bitcast.5, bf16[256,1536]{1,0:T(8,128)(2,1)S(1)} %copy-done.2, f32[2,1536]{1,0:T(2,128)S(1)} %maximum_convert_fusion.gain_ref, bf16[32,1536]{1,0:T(8,128)(2,1)S(1)} %bitcast.6, ...), custom_call_target="tpu_custom_call" | custom-call | tf_op jit(solution)/shard_map/finish/pallas_call | solution.py:263
  29.6 136.2 %experts.1 = bf16[256,1536]{1,0:T(8,128)(2,1)S(1)} custom-call(bf16[2,256,896]{2,1,0:T(8,128)(2,1)S(1)} %get-tuple-element.13.pay_ref, f32[256,1536]{1,0:T(8,128)S(1)} %get-tuple-element.14.mixed_ref, bf16[1,1536,768]{2,1,0:T(8,128)(2,1)} %gate_hbm.1, bf16[1,1536,768]{2,1,0:T(8,128)(2,1)} %up_hbm.1, bf16[1,768,1536]{2,1,0:T(8,128)(2,1)} %down_hbm.1), custom_call_target="tpu_custom_call" | custom-call | tf_op jit(solution)/shard_map/experts/pallas_call | solution.py:552
  165.9 0.9 copy.22
  (13 shorter events, 0.1 us)
Async XLA Ops:
  3.4 2.3 %copy-start = (bf16[1536,1536]{1,0:T(8,128)(2,1)S(1)}, bf16[1536,1536]{1,0:T(8,128)(2,1)}, u32[]{:S(2)}) copy-start(bf16[1536,1536]{1,0:T(8,128)(2,1)} %wq_ref.1) | copy-start | bytes 14155780
  5.7 1.1 copy-start.1
  6.9 1.1 copy-start.3
  8.0 1.1 copy-start.4
  9.1 3.4 %copy-start.7 = (bf16[1,2,4100,128]{3,1,2,0:T(2,128)(2,1)S(1)}, bf16[1,2,4100,128]{3,1,2,0:T(2,128)(2,1)}, u32[]{:S(2)}) copy-start(bf16[1,2,4100,128]{3,1,2,0:T(2,128)(2,1)} %param.18) | copy-start | bytes 6297604
  12.5 1.6 copy-start.8
  12.6 14.0 %slice-start = ((s8[4718592]{0:T(1024)(128)(4,1)}), s8[4194304]{0:T(1024)(128)(4,1)S(1)}, s32[]{:S(2)}) async-start(s8[4718592]{0:T(1024)(128)(4,1)} %bitcast.4), calls=%async_computation | async-start | bytes 8388608
  14.1 12.5 %slice-start.1 = ((s8[4718592]{0:T(1024)(128)(4,1)}), s8[524288]{0:T(1024)(128)(4,1)S(1)}, s32[]{:S(2)}) async-start(s8[4718592]{0:T(1024)(128)(4,1)} %bitcast.4), calls=%async_computation.1 | async-start | bytes 1048576
  14.4 12.2 %copy-start.2 = (bf16[256,1536]{1,0:T(8,128)(2,1)S(1)}, bf16[256,1536]{1,0:T(8,128)(2,1)}, u32[]{:S(2)}) copy-start(bf16[256,1536]{1,0:T(8,128)(2,1)} %tok_ref.3) | copy-start | bytes 2359300
  14.4 12.2 %copy-start.5 = (bf16[1536,32]{0,1:T(8,128)(2,1)S(1)}, bf16[1536,32]{0,1:T(8,128)(2,1)}, u32[]{:S(2)}) copy-start(bf16[1536,32]{0,1:T(8,128)(2,1)} %param.26) | copy-start | bytes 294916
  14.4 12.2 %copy-start.6 = (s32[256,4]{0,1:T(4,128)S(1)}, s32[256,4]{0,1:T(4,128)}, u32[]{:S(2)}) copy-start(s32[256,4]{0,1:T(4,128)} %param.16) | copy-start | bytes 12292

commit v4 on v3

--- a/solution.py
+++ b/solution.py
@@ -97,8 +97,8 @@
     )(tokens, gain, w_query, w_key, w_value, cosine, sine)
 
 
-KB = 512
-HT = 3
+KB = 1024
+HT = 6
 EXTRA = 384
 SCALE2 = HEAD_DIM ** (-0.5) * 1.4426950408889634
 LOW = -1e30
@@ -147,21 +147,22 @@
 
     def score(j, carry):
         start = pl.multiple_of(j * KB, KB)
-        s = dot_nt(q, kc_ref[0, 0, pl.ds(start, KB), :]) * SCALE2
+        raw = lambda: dot_nt(q, kc_ref[0, 0, pl.ds(start, KB), :]) * SCALE2
         offset = (start - past) & (WINDOW - 1)
         plain = (start + KB <= past) & (offset >= rows) & (offset + KB <= WINDOW)
 
         @pl.when(plain)
         def _():
+            s = raw()
             s_main[j] = s
             m_scr[...] = jnp.maximum(m_scr[...], lane_max(s))
 
         @pl.when(jnp.logical_not(plain))
         def _():
             slot = lax.broadcasted_iota(jnp.int32, (1, KB), 1) + start
-            masked = jnp.where(row < limit(slot), s, LOW)
-            s_main[j] = masked
-            m_scr[...] = jnp.maximum(m_scr[...], lane_max(masked))
+            s = jnp.where(row < limit(slot), raw(), LOW)
+            s_main[j] = s
+            m_scr[...] = jnp.maximum(m_scr[...], lane_max(s))
 
         return carry
 
@@ -327,36 +328,50 @@
     return z * (2 * SIDE) + y * 2 + ((core + flip) & 1)
 
 
+def lane(s):
+    return (3 * s) % SIDE
+
+
 class Spread:
-    copies = 7
-
-    def __init__(self, h, flip, src, dst, relay, sems, base):
+    copies = 10
+
+    def __init__(self, h, flip, src, dst, relay, sems, base, split=False):
         axis, rows = 1 - h, src.shape[2]
         top, low = pl.ds(0, rows // 2), pl.ds(rows // 2, rows // 2)
         unit = lambda step: (h, step * 2 + flip)
         slot = lambda step: (h, (SIDE - step) % SIDE * 2 + flip)
+        ways = (1, SIDE - 1) if flip == 0 else (SIDE - 1, 1)
         self.relays, self.onward = [], []
-        for i, (step, part) in enumerate(((1, top), (SIDE - 1, low))):
+        for i, (step, part) in enumerate(zip(ways, (top, low))):
             self.relays.append(
                 remote(src.at[unit(2) + (part,)], relay.at[h, flip, i], sems, base + i, peer(axis, step, 0)))
             self.onward.append(
                 remote(relay.at[h, flip, i], dst.at[slot(2) + (part,)], sems, base + 2 + i, peer(axis, step, flip)))
+        steps = (1, SIDE - 1, 0)[:2 + flip]
+        parts = ((low,), (top,)) if split else ((),)
         self.direct = [
-            remote(src.at[unit(step)], dst.at[slot(step)], sems, base + 4 + i, peer(axis, step, flip))
-            for i, step in enumerate((1, SIDE - 1, 0)[:2 + flip])
+            [
+                remote(src.at[unit(step) + part], dst.at[slot(step) + part], sems,
+                       base + 4 + i * len(steps) + j, peer(axis, step, flip))
+                for j, step in enumerate(steps)
+            ]
+            for i, part in enumerate(parts)
         ]
 
-    def forward(self):
-        for first, then in zip(self.relays, self.onward):
-            first.wait_recv()
-            then.start()
+    def forward(self, i):
+        self.relays[i].wait_recv()
+        self.onward[i].start()
+
+    def wait_part(self, i):
+        for copy in self.direct[i] + [self.onward[1 - i]]:
+            copy.wait_recv()
 
     def wait_recv(self):
-        for copy in self.direct + self.onward:
+        for copy in sum(self.direct, []) + self.onward:
             copy.wait_recv()
 
     def wait_src(self):
-        for copy in self.relays + self.direct:
+        for copy in self.relays + sum(self.direct, []):
             copy.wait_send()
 
     def wait_onward(self):
@@ -387,7 +402,7 @@
     gather, passing, out, home, pass_back, last = [], [], [], [], [], []
     for h in both:
         up, down = peer(h, 1, 0), peer(h, SIDE - 1, 0)
-        base = h * 38
+        base = h * 54
         gather.append([
             remote(pay_ref.at[h, top], near.at[h, 3, top], sems, base, up),
             remote(pay_ref.at[h, low], near.at[h, 1, low], sems, base + 1, down),
@@ -399,14 +414,18 @@
             remote(near.at[h, 1, low], near.at[h, 2, low], sems, base + 5, down),
         ])
         out.append([Spread(h, d, send, x, relay_out, sems, base + 6 + d * Spread.copies) for d in both])
-        home.append([Spread(h, d, send, back, relay_in, sems, base + 20 + d * Spread.copies) for d in both])
+        home.append([
+            Spread(h, d, send, back, relay_in, sems, base + 26 + d * Spread.copies, split=d == 1) for d in both
+        ])
         pass_back.append([
-            remote(parts.at[h, 1, top], passed.at[h, 0], sems, base + 34, up),
-            remote(parts.at[h, 1, low], passed.at[h, 1], sems, base + 35, down),
+            remote(parts.at[h, 1, top], passed.at[h, 0], sems, base + 46, up),
+            remote(parts.at[h, 1, low], passed.at[h, 1], sems, base + 47, down),
         ])
         last.append([
-            remote(parts.at[h, 0], final.at[h, 0], sems, base + 36, up),
-            remote(parts.at[h, 2], final.at[h, 1], sems, base + 37, down),
+            remote(parts.at[h, 0, low], final.at[h, 0, low], sems, base + 48, up),
+            remote(parts.at[h, 2, top], final.at[h, 1, top], sems, base + 49, down),
+            remote(parts.at[h, 0, top], final.at[h, 0, top], sems, base + 50, up),
+            remote(parts.at[h, 2, low], final.at[h, 1, low], sems, base + 51, down),
         ])
 
     for i in range(4):
@@ -424,7 +443,7 @@
         select = jnp.where(wanted == place, 1.0, 0.0).astype(bf16)
         chosen = dot(select, near[h, s, :, 0:half]).astype(bf16)
         for k in range(SIDE):
-            send[h, 2 * k + d, s * CAP:(s + 1) * CAP] = chosen[k * CAP:(k + 1) * CAP]
+            send[h, 2 * k + d, lane(s) * CAP:(lane(s) + 1) * CAP] = chosen[k * CAP:(k + 1) * CAP]
 
     for h in both:
         own[h].wait()
@@ -434,41 +453,46 @@
         for h in both:
             gather[h][i].wait_recv()
             passing[h][i].start()
-    for i, s in ((2, 3), (3, 1)):
-        for h in both:
-            gather[h][i].wait_recv()
-            for d in both:
-                choose(h, s, d)
+    for h in both:
+        gather[h][2].wait_recv()
+        for d in both:
+            choose(h, 3, d)
+        start([out[h][d].relays[0] for d in both])
+    for h in both:
+        gather[h][3].wait_recv()
+        for d in both:
+            choose(h, 1, d)
     for h in both:
         for copy in passing[h]:
             copy.wait_recv()
         choose(h, 2, 0)
-        start(out[h][0].relays + out[h][0].direct)
+        start([out[h][0].relays[1]] + out[h][0].direct[0])
     for h in both:
         choose(h, 2, 1)
-        start(out[h][1].relays)
+        start([out[h][1].relays[1]])
     for h in both:
         x[h, 0] = send[h, 0]
-    for d in both:
-        for h in both:
-            out[h][d].forward()
-    for h in both:
-        start(out[h][1].direct)
+    for i in both:
+        for d in both:
+            for h in both:
+                out[h][d].forward(i)
+    for h in both:
+        start(out[h][1].direct[0])
     for copy in weights:
         copy.wait()
 
     def run_expert(d):
         def block(k, carry):
-            spot = pl.ds(pl.multiple_of(k * CAP, CAP), CAP)
+            spot = pl.ds(pl.multiple_of(lane(k) * CAP, CAP), CAP)
             a = x[0, 2 * k + d]
-            b = jnp.concatenate([x[1, 2 * s + d, spot] for s in range(SIDE)], axis=0)
+            b = jnp.concatenate([x[1, 2 * lane(i) + d, spot] for i in range(SIDE)], axis=0)
             gate = dot(a, gate_w[0:half]) + dot(b, gate_w[half:2 * half])
             up = dot(a, up_w[0:half]) + dot(b, up_w[half:2 * half])
             hidden = (jnp.maximum(gate, 0.0) * up).astype(bf16)
             send[0, 2 * k + d] = dot(hidden, down_w[:, 0:half]).astype(bf16)
             other = dot(hidden, down_w[:, half:2 * half]).astype(bf16)
-            for s in range(SIDE):
-                send[1, 2 * s + d, spot] = other[s * CAP:(s + 1) * CAP]
+            for i in range(SIDE):
+                send[1, 2 * lane(i) + d, spot] = other[i * CAP:(i + 1) * CAP]
             return carry
 
         for h in both:
@@ -478,17 +502,22 @@
 
     run_expert(0)
     for h in both:
-        start(home[h][0].relays + home[h][0].direct)
+        start(home[h][0].relays + home[h][0].direct[0])
     run_expert(1)
     for h in both:
-        start(home[h][1].relays)
+        start(home[h][1].relays[::-1])
+    for i in both:
+        for h in both:
+            home[h][0].forward(i)
+    for h in both:
+        start(home[h][1].direct[0])
     for h in both:
         back[h, 0] = send[h, 0]
-    for d in both:
+    for i in (1, 0):
         for h in both:
-            home[h][d].forward()
-    for h in both:
-        start(home[h][1].direct)
+            home[h][1].forward(i)
+    for h in both:
+        start(home[h][1].direct[1])
 
     place_back = (lax.broadcasted_iota(jnp.int32, (rows, slots), 1) % CAP).astype(f32)
     meta_row = lax.broadcasted_iota(jnp.int32, (META, slots), 0)
@@ -499,7 +528,7 @@
         expert = group_expert(h, step_columns + d)
         take = lambda i: dot(meta, jnp.where(meta_row == expert + i * EXPERTS, 1.0, 0.0).astype(bf16))
         here = take(2) == place_back
-        outs = jnp.concatenate([back[h, 2 * k + d, s * CAP:(s + 1) * CAP] for k in range(SIDE)], axis=0)
+        outs = jnp.concatenate([back[h, 2 * k + d, lane(s) * CAP:(lane(s) + 1) * CAP] for k in range(SIDE)], axis=0)
         high = jnp.where(here, take(0), 0.0).astype(bf16)
         rest = jnp.where(here, take(1), 0.0).astype(bf16)
         return dot(high, outs) + dot(rest, outs)
@@ -509,21 +538,25 @@
         for s in range(SIDE):
             sums[h, s] = weigh(h, s, 0)
     for h in both:
-        home[h][1].wait_recv()
+        home[h][1].wait_part(0)
         parts[h, 1] = (sums[h, 2] + weigh(h, 2, 1)).astype(bf16)
         start(pass_back[h])
     for h in both:
-        for s in (1, 3):
-            sums[h, s] += weigh(h, s, 1)
+        sums[h, 1] += weigh(h, 1, 1)
+        parts[h, 0, mid:rows] = sums[h, 1, mid:rows].astype(bf16)
+        last[h][0].start()
+    for h in both:
+        home[h][1].wait_part(1)
+        sums[h, 3] += weigh(h, 3, 1)
+        parts[h, 2, 0:mid] = sums[h, 3, 0:mid].astype(bf16)
+        last[h][1].start()
     for h in both:
         pass_back[h][0].wait_recv()
         parts[h, 0, 0:mid] = (sums[h, 1, 0:mid] + passed[h, 0].astype(f32)).astype(bf16)
-        parts[h, 0, mid:rows] = sums[h, 1, mid:rows].astype(bf16)
-        last[h][0].start()
+        last[h][2].start()
         pass_back[h][1].wait_recv()
-        parts[h, 2, 0:mid] = sums[h, 3, 0:mid].astype(bf16)
         parts[h, 2, mid:rows] = (sums[h, 3, mid:rows] + passed[h, 1].astype(f32)).astype(bf16)
-        last[h][1].start()
+        last[h][3].start()
     for h in both:
         sums[h, 0] += weigh(h, 0, 1)
     for h in both:
@@ -570,7 +603,7 @@
             pltpu.VMEM((ff, width), bf16),
             pltpu.SemaphoreType.DMA((2,)),
             pltpu.SemaphoreType.DMA((3,)),
-            pltpu.SemaphoreType.DMA((2, 76)),
+            pltpu.SemaphoreType.DMA((2, 108)),
         ],
         compiler_params=pltpu.CompilerParams(collective_id=1, has_side_effects=True, vmem_limit_bytes=50 * MB),
         name="experts",
@@ -582,8 +615,10 @@
     rows, width = tokens.shape
     positions = history[0] + jnp.arange(rows, dtype=jnp.int32)
     cosine, sine = rope_tables(positions)
-    gains = jnp.stack([attn_gain, ffn_gain]).astype(f32)
-    q, keys_new, values_new, keys_near, values_near = project(tokens, gains, w_query, w_key, w_value, cosine, sine)
+    gains = jnp.concatenate([attn_gain, ffn_gain]).astype(f32).reshape(2, width)
+    keep = lambda a: pltpu.with_memory_space_constraint(a, pltpu.HBM)
+    q, keys_new, values_new, keys_near, values_near = project(
+        keep(tokens), gains, keep(w_query), keep(w_key), keep(w_value), cosine, sine)
     attended = attend(history, q, cache_keys, cache_values, keys_near, values_near)
     mixed, pay = finish(attended, w_out, tokens, gains, jnp.transpose(w_router), jnp.transpose(routes))
     layer_out = run_experts(pay, mixed, expert_gate, expert_up, expert_down)

time: 168 us -> 142 us (0.85)
  Pallas kernels: 155 us -> 134 us
  local copies, waits for them, and re-layouts: 9.86 us -> 2.76 us
    pallas_call x1, Pallas kernels: 136 us -> 110 us  [run_experts(): pl.pallas_call(experts_kernel, in_specs=[vmem, vmem, hbm, hbm, hbm], out_...]
    unnamed x25 -> x17, local copies, waits for them, and re-layouts: 8.47 us -> 2.75 us
    pallas_call x1, Pallas kernels: 12.1 us -> 15.5 us  [attend(): pl.pallas_call(attn_kernel, grid_spec=pltpu.PrefetchScalarGridSpec(num_sc...]
    pallas_call x1, Pallas kernels: 3.39 us -> 5.99 us  [project(): pl.pallas_call(qkv_kernel, grid=(w_query.shape[1] // Q_BLOCK,), in_specs=...]
where the time goes in v4:
time: 142 us; the launch traced here: 140 us
  Pallas kernels  134 us (94%)
  local copies, waits for them, and re-layouts  2.76 us (2%)
  between operations  1.45 us (1%)
    pallas_call x1, Pallas kernels, run_experts(): pl.pallas_call(experts_kernel, in_specs=[vmem, vmem, hbm, hbm, hbm], out_...  110 us
    pallas_call x1, Pallas kernels, attend(): pl.pallas_call(attn_kernel, grid_spec=pltpu.PrefetchScalarGridSpec(num_sc...  15.5 us
    pallas_call x1, Pallas kernels, project(): pl.pallas_call(qkv_kernel, grid=(w_query.shape[1] // Q_BLOCK,), in_specs=...  5.99 us
    pallas_call x1, Pallas kernels, finish(): pl.pallas_call(out_kernel, grid=(width // O_BLOCK,), in_specs=[full(atten...  2.96 us

profile of v4, /device:TPU:2, one launch (start us, length us, event | category | flops | bytes accessed | tf_op | source)
XLA Modules:
  0.0 140.0 jit_solution(9705854759524241226)
XLA Ops:
  1.3 0.7 maximum_convert_fusion
  2.0 0.5 fusion
  2.6 0.1 pad_maximum_fusion
  2.7 0.0 copy-start.3
  2.7 6.0 %project.1 = (bf16[12,256,128]{2,1,0:T(8,128)(2,1)S(1)}, bf16[256,256]{1,0:T(8,128)(2,1)}, bf16[256,256]{1,0:T(8,128)(2,1)}, bf16[256,256]{1,0:T(8,128)(2,1)S(1)}, bf16[256,256]{1,0:T(8,128)(2,1)S(1)}) custom-call(bf16[256,1536]{1,0:T(8,128)(2,1)} %tok_ref.3, f32[2,1536]{1,0:T(2,128)S(1)} %reshape.21.gain_ref, bf16[1536,1536]{1,0:T(8,128)(2,1)} %wq_ref.1, ...), custom_call_target="tpu_custom_call" | custom-call | tf_op jit(solution)/shard_map/project/pallas_call | solution.py:80
  8.7 0.0 copy-start.4
  8.7 0.0 copy-done.3
  8.7 0.0 slice-start
  8.8 0.3 copy.18.kc_ref
  9.0 1.3 copy-done.4
  10.3 0.0 slice-start.1
  10.3 0.3 copy.19.vc_ref
  10.6 0.0 copy-start
  10.6 0.0 copy-start.1
  10.6 0.0 copy-start.2
  10.6 15.5 %attend.1.att_ref = bf16[256,1536]{1,0:T(8,128)(2,1)S(1)} custom-call(s32[1]{0:T(128)} %copy.21.past_ref, bf16[12,256,128]{2,1,0:T(8,128)(2,1)S(1)} %get-tuple-element.10.q_ref, bf16[1,2,4100,128]{3,2,1,0:T(8,128)(2,1)S(1)} %copy.18.kc_ref, bf16[1,2,4100,128]{3,2,1,0:T(8,128)(2,1)S(1)} %copy.19.vc_ref, bf16[256,256]{1,0:T(8,128)(2,1)S(1)} %get-tuple-element.11.kn_ref, ...), custom_call_target="tpu_custom_call" | custom-call | tf_op jit(solution)/shard_map/attend/pallas_call | solution.py:196
  26.1 0.0 slice-done
  26.1 0.0 slice-done.1
  26.1 0.0 copy-done
  26.2 0.0 copy-done.1
  26.2 0.0 copy-done.2
  26.2 3.0 %finish.1 = (f32[256,1536]{1,0:T(8,128)S(1)}, bf16[2,256,896]{2,1,0:T(8,128)(2,1)S(1)}) custom-call(bf16[256,1536]{1,0:T(8,128)(2,1)S(1)} %attend.1.att_ref, bf16[1536,1536]{1,0:T(8,128)(2,1)S(1)} %bitcast.5, bf16[256,1536]{1,0:T(8,128)(2,1)S(1)} %copy-done, f32[2,1536]{1,0:T(2,128)S(1)} %reshape.21.gain_ref, bf16[32,1536]{1,0:T(8,128)(2,1)S(1)} %bitcast.6, ...), custom_call_target="tpu_custom_call" | custom-call | tf_op jit(solution)/shard_map/finish/pallas_call | solution.py:264
  29.1 109.9 %experts.1 = bf16[256,1536]{1,0:T(8,128)(2,1)S(1)} custom-call(bf16[2,256,896]{2,1,0:T(8,128)(2,1)S(1)} %get-tuple-element.13.pay_ref, f32[256,1536]{1,0:T(8,128)S(1)} %get-tuple-element.14.mixed_ref, bf16[1,1536,768]{2,1,0:T(8,128)(2,1)} %gate_hbm.1, bf16[1,1536,768]{2,1,0:T(8,128)(2,1)} %up_hbm.1, bf16[1,768,1536]{2,1,0:T(8,128)(2,1)} %down_hbm.1), custom_call_target="tpu_custom_call" | custom-call | tf_op jit(solution)/shard_map/experts/pallas_call | solution.py:585
  139.1 0.9 copy.22
  (4 shorter events, 0.0 us)
Async XLA Ops:
  2.7 6.0 %copy-start.3 = (bf16[1,2,4100,128]{3,1,2,0:T(2,128)(2,1)S(1)}, bf16[1,2,4100,128]{3,1,2,0:T(2,128)(2,1)}, u32[]{:S(2)}) copy-start(bf16[1,2,4100,128]{3,1,2,0:T(2,128)(2,1)} %param.18) | copy-start | bytes 6297604
  8.7 1.6 %copy-start.4 = (bf16[1,2,4100,128]{3,1,2,0:T(2,128)(2,1)S(1)}, bf16[1,2,4100,128]{3,1,2,0:T(2,128)(2,1)}, u32[]{:S(2)}) copy-start(bf16[1,2,4100,128]{3,1,2,0:T(2,128)(2,1)} %param.19) | copy-start | bytes 6297604
  8.7 17.4 %slice-start = ((s8[4718592]{0:T(1024)(128)(4,1)}), s8[4194304]{0:T(1024)(128)(4,1)S(1)}, s32[]{:S(2)}) async-start(s8[4718592]{0:T(1024)(128)(4,1)} %bitcast.4), calls=%async_computation | async-start | bytes 8388608
  10.3 15.8 %slice-start.1 = ((s8[4718592]{0:T(1024)(128)(4,1)}), s8[524288]{0:T(1024)(128)(4,1)S(1)}, s32[]{:S(2)}) async-start(s8[4718592]{0:T(1024)(128)(4,1)} %bitcast.4), calls=%async_computation.1 | async-start | bytes 1048576
  10.6 15.6 %copy-start = (bf16[256,1536]{1,0:T(8,128)(2,1)S(1)}, bf16[256,1536]{1,0:T(8,128)(2,1)}, u32[]{:S(2)}) copy-start(bf16[256,1536]{1,0:T(8,128)(2,1)} %tok_ref.3) | copy-start | bytes 2359300
  10.6 15.6 %copy-start.1 = (bf16[1536,32]{0,1:T(8,128)(2,1)S(1)}, bf16[1536,32]{0,1:T(8,128)(2,1)}, u32[]{:S(2)}) copy-start(bf16[1536,32]{0,1:T(8,128)(2,1)} %param.26) | copy-start | bytes 294916
  10.6 15.6 %copy-start.2 = (s32[256,4]{0,1:T(4,128)S(1)}, s32[256,4]{0,1:T(4,128)}, u32[]{:S(2)}) copy-start(s32[256,4]{0,1:T(4,128)} %param.16) | copy-start | bytes 12292

commit v5 on v4

--- a/solution.py
+++ b/solution.py
@@ -214,71 +214,12 @@
             ],
         ),
         out_shape=jax.ShapeDtypeStruct((rows, HEADS * HEAD_DIM), bf16),
-        compiler_params=pltpu.CompilerParams(vmem_limit_bytes=48 * MB),
+        compiler_params=pltpu.CompilerParams(vmem_limit_bytes=40 * MB),
         name="attend",
     )(past, q, cache_keys, cache_values, keys_new, values_new)
 
 
-O_BLOCK = 512
 META = 128
-
-
-def out_kernel(att_ref, wo_ref, tok_ref, gain_ref, wr_t_ref, routes_t_ref, mixed_ref, pay_ref):
-    n = pl.program_id(0)
-    rows, width = tok_ref.shape
-    steps = width // O_BLOCK
-    half = width // 2
-    experts = wr_t_ref.shape[0]
-    cols = pl.ds(pl.multiple_of(n * O_BLOCK, O_BLOCK), O_BLOCK)
-    mixed_ref[:, cols] = tok_ref[:, cols].astype(f32) + dot(att_ref[...], wo_ref[...])
-
-    @pl.when(n == steps - 1)
-    def _():
-        ffn = norm_rows(mixed_ref[...], gain_ref[1:2])
-        expert = lax.broadcasted_iota(jnp.int32, (experts, rows), 0)
-        named_t = routes_t_ref[0:1] == expert
-        for j in range(1, TOP):
-            named_t = named_t | (routes_t_ref[j:j + 1] == expert)
-        named_t = jnp.where(named_t, 1.0, 0.0).astype(bf16)
-        a = lax.broadcasted_iota(jnp.int32, (rows, rows), 0)
-        b = lax.broadcasted_iota(jnp.int32, (rows, rows), 1)
-        named = dot_nt(jnp.where(a == b, 1.0, 0.0).astype(bf16), named_t) > 0.5
-        ranks = dot_nt(jnp.where(b < a, 1.0, 0.0).astype(bf16), named_t)
-        rank = jnp.where(named, ranks, -1.0).astype(bf16)
-        score = jnp.where(named, jax.nn.sigmoid(dot_nt(ffn, wr_t_ref[...])), 0.0)
-        mix = score / jnp.sum(score, axis=1, keepdims=True)
-        high = mix.astype(bf16)
-        low = (mix - high.astype(f32)).astype(bf16)
-        source = lax.broadcasted_iota(jnp.int32, (experts, META), 0)
-        column = lax.broadcasted_iota(jnp.int32, (experts, META), 1)
-        put = lambda x, i: dot(x, jnp.where(column == source + i * experts, 1.0, 0.0).astype(bf16))
-        meta = (put(high, 0) + put(low, 1) + put(rank, 2)).astype(bf16)
-        for h in range(2):
-            pay_ref[h, :, 0:half] = ffn[:, h * half:(h + 1) * half]
-            pay_ref[h, :, half:half + META] = meta
-
-
-def finish(attended, w_out, tokens, gain, router_t, routes_t):
-    rows, width = tokens.shape
-    full = lambda a: pl.BlockSpec(a.shape, lambda n: (0,) * a.ndim)
-    return pl.pallas_call(
-        out_kernel,
-        grid=(width // O_BLOCK,),
-        in_specs=[
-            full(attended), pl.BlockSpec((width, O_BLOCK), lambda n: (0, n)),
-            full(tokens), full(gain), full(router_t), full(routes_t),
-        ],
-        out_specs=[
-            pl.BlockSpec((rows, width), lambda n: (0, 0)),
-            pl.BlockSpec((2, rows, width // 2 + META), lambda n: (0, 0, 0)),
-        ],
-        out_shape=[
-            jax.ShapeDtypeStruct((rows, width), f32),
-            jax.ShapeDtypeStruct((2, rows, width // 2 + META), bf16),
-        ],
-        compiler_params=pltpu.CompilerParams(vmem_limit_bytes=32 * MB),
-        name="finish",
-    )(attended, w_out, tokens, gain, router_t, routes_t)
 
 
 SIDE = 4
@@ -315,7 +256,7 @@
                 others.append(peer(axis, step, flip))
     for other in others:
         pl.semaphore_signal(barrier, inc=1, device_id={"expert": other}, device_id_type=pl.DeviceIdType.MESH)
-    pl.semaphore_wait(barrier, len(others))
+    return lambda: pl.semaphore_wait(barrier, len(others))
 
 
 def group_expert(h, index):
@@ -384,9 +325,11 @@
         copy.start()
 
 
-def experts_kernel(pay_ref, mixed_ref, gate_hbm, up_hbm, down_hbm, out_ref, near, send, x, relay_out, back, relay_in,
-                   sums, parts, passed, final, gate_w, up_w, down_w, own_sem, weight_sem, sems):
-    rows, width = mixed_ref.shape
+def experts_kernel(att_ref, wo_ref, tok_ref, gain_ref, wr_t_ref, routes_t_ref, gate_hbm, up_hbm, down_hbm, out_ref,
+                   mixed, near, send, x, relay_out, back, relay_in, sums, parts, passed, final, gate_w, up_w, down_w,
+                   weight_sem, sems):
+    rows, width = tok_ref.shape
+    experts = wr_t_ref.shape[0]
     half = width // 2
     mid = rows // 2
     slots = SIDE * CAP
@@ -396,18 +339,16 @@
         pltpu.make_async_copy(src.at[0], dst, weight_sem.at[i])
         for i, (src, dst) in enumerate(((gate_hbm, gate_w), (up_hbm, up_w), (down_hbm, down_w)))
     ]
-    own = [pltpu.make_async_copy(pay_ref.at[h], near.at[h, 0], own_sem.at[h]) for h in both]
-    start(own)
-    greet()
+    all_here = greet()
     gather, passing, out, home, pass_back, last = [], [], [], [], [], []
     for h in both:
         up, down = peer(h, 1, 0), peer(h, SIDE - 1, 0)
         base = h * 54
         gather.append([
-            remote(pay_ref.at[h, top], near.at[h, 3, top], sems, base, up),
-            remote(pay_ref.at[h, low], near.at[h, 1, low], sems, base + 1, down),
-            remote(pay_ref.at[h, low], near.at[h, 3, low], sems, base + 2, up),
-            remote(pay_ref.at[h, top], near.at[h, 1, top], sems, base + 3, down),
+            remote(near.at[h, 0, top], near.at[h, 3, top], sems, base, up),
+            remote(near.at[h, 0, low], near.at[h, 1, low], sems, base + 1, down),
+            remote(near.at[h, 0, low], near.at[h, 3, low], sems, base + 2, up),
+            remote(near.at[h, 0, top], near.at[h, 1, top], sems, base + 3, down),
         ])
         passing.append([
             remote(near.at[h, 3, top], near.at[h, 2, top], sems, base + 4, up),
@@ -428,7 +369,41 @@
             remote(parts.at[h, 2, low], final.at[h, 1, low], sems, base + 51, down),
         ])
 
-    for i in range(4):
+    expert_row = lax.broadcasted_iota(jnp.int32, (experts, rows), 0)
+    named_t = routes_t_ref[0:1] == expert_row
+    for j in range(1, TOP):
+        named_t = named_t | (routes_t_ref[j:j + 1] == expert_row)
+    named_t = jnp.where(named_t, 1.0, 0.0).astype(bf16)
+    meta_from = lax.broadcasted_iota(jnp.int32, (experts, META), 0)
+    meta_to = lax.broadcasted_iota(jnp.int32, (experts, META), 1)
+
+    def prepare(first):
+        span = slice(first, first + mid)
+        total = tok_ref[span].astype(f32) + dot(att_ref[span], wo_ref[...])
+        mixed[span] = total
+        ffn = norm_rows(total, gain_ref[1:2])
+        a = lax.broadcasted_iota(jnp.int32, (mid, rows), 0) + first
+        b = lax.broadcasted_iota(jnp.int32, (mid, rows), 1)
+        named = dot_nt(jnp.where(a == b, 1.0, 0.0).astype(bf16), named_t) > 0.5
+        ranks = dot_nt(jnp.where(b < a, 1.0, 0.0).astype(bf16), named_t)
+        rank = jnp.where(named, ranks, -1.0).astype(bf16)
+        score = jnp.where(named, jax.nn.sigmoid(dot_nt(ffn, wr_t_ref[...])), 0.0)
+        mix = score / jnp.sum(score, axis=1, keepdims=True)
+        high = mix.astype(bf16)
+        rest = (mix - high.astype(f32)).astype(bf16)
+        put = lambda v, i: dot(v, jnp.where(meta_to == meta_from + i * experts, 1.0, 0.0).astype(bf16))
+        meta = (put(high, 0) + put(rest, 1) + put(rank, 2)).astype(bf16)
+        for h in both:
+            near[h, 0, span, 0:half] = ffn[:, h * half:(h + 1) * half]
+            near[h, 0, span, half:half + META] = meta
+
+    prepare(0)
+    all_here()
+    for i in (0, 3):
+        for h in both:
+            gather[h][i].start()
+    prepare(mid)
+    for i in (1, 2):
         for h in both:
             gather[h][i].start()
     start(weights)
@@ -446,13 +421,14 @@
             send[h, 2 * k + d, lane(s) * CAP:(lane(s) + 1) * CAP] = chosen[k * CAP:(k + 1) * CAP]
 
     for h in both:
-        own[h].wait()
+        gather[h][0].wait_recv()
+        passing[h][0].start()
+    for h in both:
         for d in both:
             choose(h, 0, d)
-    for i in both:
-        for h in both:
-            gather[h][i].wait_recv()
-            passing[h][i].start()
+    for h in both:
+        gather[h][1].wait_recv()
+        passing[h][1].start()
     for h in both:
         gather[h][2].wait_recv()
         for d in both:
@@ -564,7 +540,7 @@
             copy.wait_recv()
         cols = slice(h * half, (h + 1) * half)
         out_ref[:, cols] = (
-            mixed_ref[:, cols] + (sums[h, 0] + final[h, 0].astype(f32) + final[h, 1].astype(f32))
+            mixed[:, cols] + (sums[h, 0] + final[h, 0].astype(f32) + final[h, 1].astype(f32))
         ).astype(bf16)
     for h in both:
         for copy in gather[h] + passing[h] + pass_back[h] + last[h]:
@@ -575,8 +551,8 @@
             home[h][d].wait_onward()
 
 
-def run_experts(pay, mixed, gate, up, down):
-    rows, width = mixed.shape
+def run_experts(attended, w_out, tokens, gains, router_t, routes_t, gate, up, down):
+    rows, width = tokens.shape
     half, ff = width // 2, gate.shape[2]
     vmem = pl.BlockSpec(memory_space=pltpu.VMEM)
     hbm = pl.BlockSpec(memory_space=pl.ANY)
@@ -584,10 +560,11 @@
     part = (SIDE * CAP // 2, half)
     return pl.pallas_call(
         experts_kernel,
-        in_specs=[vmem, vmem, hbm, hbm, hbm],
+        in_specs=[vmem] * 6 + [hbm] * 3,
         out_specs=vmem,
         out_shape=jax.ShapeDtypeStruct((rows, width), bf16),
         scratch_shapes=[
+            pltpu.VMEM((rows, width), f32),
             pltpu.VMEM((2, SIDE, rows, half + META), bf16),
             pltpu.VMEM((2, GROUPS) + unit, bf16),
             pltpu.VMEM((2, GROUPS) + unit, bf16),
@@ -601,13 +578,12 @@
             pltpu.VMEM((width, ff), bf16),
             pltpu.VMEM((width, ff), bf16),
             pltpu.VMEM((ff, width), bf16),
-            pltpu.SemaphoreType.DMA((2,)),
             pltpu.SemaphoreType.DMA((3,)),
             pltpu.SemaphoreType.DMA((2, 108)),
         ],
-        compiler_params=pltpu.CompilerParams(collective_id=1, has_side_effects=True, vmem_limit_bytes=50 * MB),
+        compiler_params=pltpu.CompilerParams(collective_id=1, has_side_effects=True, vmem_limit_bytes=45 * MB),
         name="experts",
-    )(pay, mixed, gate, up, down)
+    )(attended, w_out, tokens, gains, router_t, routes_t, gate, up, down)
 
 
 def shards(tokens, routes, history, cache_keys, cache_values, attn_gain, w_query, w_key, w_value, w_out,
@@ -620,8 +596,9 @@
     q, keys_new, values_new, keys_near, values_near = project(
         keep(tokens), gains, keep(w_query), keep(w_key), keep(w_value), cosine, sine)
     attended = attend(history, q, cache_keys, cache_values, keys_near, values_near)
-    mixed, pay = finish(attended, w_out, tokens, gains, jnp.transpose(w_router), jnp.transpose(routes))
-    layer_out = run_experts(pay, mixed, expert_gate, expert_up, expert_down)
+    layer_out = run_experts(
+        attended, w_out, tokens, gains, jnp.transpose(w_router), jnp.transpose(routes),
+        keep(expert_gate), keep(expert_up), keep(expert_down))
     return layer_out, keys_new, values_new
 
 

time: 142 us -> 140 us (0.986)
    pallas_call x1, Pallas kernels: 15.5 us -> 7.5 us  [attend(): pl.pallas_call(attn_kernel, grid_spec=pltpu.PrefetchScalarGridSpec(num_sc...]
    pallas_call x2 -> x1, Pallas kernels: 113 us -> 119 us  [run_experts(): pl.pallas_call(experts_kernel, in_specs=[vmem] * 6 + [hbm] * 3, out_specs...]
where the time goes in v5:
time: 140 us; the launch traced here: 139 us
  Pallas kernels  133 us (95%)
  local copies, waits for them, and re-layouts  2.76 us (2%)
  between operations  1.44 us (1%)
    pallas_call x1, Pallas kernels, run_experts(): pl.pallas_call(experts_kernel, in_specs=[vmem] * 6 + [hbm] * 3, out_specs...  119 us
    pallas_call x1, Pallas kernels, attend(): pl.pallas_call(attn_kernel, grid_spec=pltpu.PrefetchScalarGridSpec(num_sc...  7.5 us
    pallas_call x1, Pallas kernels, project(): pl.pallas_call(qkv_kernel, grid=(w_query.shape[1] // Q_BLOCK,), in_specs=...  5.99 us

profile of v5, /device:TPU:2, one launch (start us, length us, event | category | flops | bytes accessed | tf_op | source)
XLA Modules:
  0.0 138.5 jit_solution(1968982198249378356)
XLA Ops:
  1.3 0.7 maximum_convert_fusion
  2.0 0.5 fusion
  2.6 0.1 pad_maximum_fusion
  2.7 0.0 copy-start.3
  2.7 6.0 %project.1 = (bf16[12,256,128]{2,1,0:T(8,128)(2,1)S(1)}, bf16[256,256]{1,0:T(8,128)(2,1)}, bf16[256,256]{1,0:T(8,128)(2,1)}, bf16[256,256]{1,0:T(8,128)(2,1)S(1)}, bf16[256,256]{1,0:T(8,128)(2,1)S(1)}) custom-call(bf16[256,1536]{1,0:T(8,128)(2,1)} %tok_ref.3, f32[2,1536]{1,0:T(2,128)S(1)} %reshape.21.gain_ref, bf16[1536,1536]{1,0:T(8,128)(2,1)} %wq_ref.1, ...), custom_call_target="tpu_custom_call" | custom-call | tf_op jit(solution)/shard_map/project/pallas_call | solution.py:80
  8.7 0.0 copy-start.4
  8.7 0.0 copy-done.3
  8.7 0.0 slice-start
  8.8 0.3 copy.18.kc_ref
  9.0 1.3 copy-done.4
  10.3 0.0 slice-start.1
  10.3 0.3 copy.19.vc_ref
  10.6 0.0 copy-start
  10.6 0.0 copy-start.1
  10.6 0.0 copy-start.2
  10.6 7.5 %attend.1.att_ref = bf16[256,1536]{1,0:T(8,128)(2,1)S(1)} custom-call(s32[1]{0:T(128)} %copy.21.past_ref, bf16[12,256,128]{2,1,0:T(8,128)(2,1)S(1)} %get-tuple-element.8.q_ref, bf16[1,2,4100,128]{3,2,1,0:T(8,128)(2,1)S(1)} %copy.18.kc_ref, bf16[1,2,4100,128]{3,2,1,0:T(8,128)(2,1)S(1)} %copy.19.vc_ref, bf16[256,256]{1,0:T(8,128)(2,1)S(1)} %get-tuple-element.9.kn_ref, ...), custom_call_target="tpu_custom_call" | custom-call | tf_op jit(solution)/shard_map/attend/pallas_call | solution.py:196
  18.1 0.0 slice-done
  18.1 0.0 slice-done.1
  18.2 0.0 copy-done
  18.2 0.0 copy-done.1
  18.2 0.0 copy-done.2
  18.2 119.4 %experts.1 = bf16[256,1536]{1,0:T(8,128)(2,1)S(1)} custom-call(bf16[256,1536]{1,0:T(8,128)(2,1)S(1)} %attend.1.att_ref, bf16[1536,1536]{1,0:T(8,128)(2,1)S(1)} %bitcast.5, bf16[256,1536]{1,0:T(8,128)(2,1)S(1)} %copy-done, f32[2,1536]{1,0:T(2,128)S(1)} %reshape.21.gain_ref, bf16[32,1536]{1,0:T(8,128)(2,1)S(1)} %bitcast.6, s32[4,256]{1,0:T(4,128)S(1)} %bitcast.7, ...), custom_call_target="tpu_custom_call" | custom-call | tf_op jit(solution)/shard_map/experts/pallas_call | solution.py:561
  137.6 0.9 copy.22
  (4 shorter events, 0.0 us)
Async XLA Ops:
  2.7 6.0 %copy-start.3 = (bf16[1,2,4100,128]{3,1,2,0:T(2,128)(2,1)S(1)}, bf16[1,2,4100,128]{3,1,2,0:T(2,128)(2,1)}, u32[]{:S(2)}) copy-start(bf16[1,2,4100,128]{3,1,2,0:T(2,128)(2,1)} %param.18) | copy-start | bytes 6297604
  8.7 1.6 %copy-start.4 = (bf16[1,2,4100,128]{3,1,2,0:T(2,128)(2,1)S(1)}, bf16[1,2,4100,128]{3,1,2,0:T(2,128)(2,1)}, u32[]{:S(2)}) copy-start(bf16[1,2,4100,128]{3,1,2,0:T(2,128)(2,1)} %param.19) | copy-start | bytes 6297604
  8.7 9.4 %slice-start = ((s8[4718592]{0:T(1024)(128)(4,1)}), s8[4194304]{0:T(1024)(128)(4,1)S(1)}, s32[]{:S(2)}) async-start(s8[4718592]{0:T(1024)(128)(4,1)} %bitcast.4), calls=%async_computation | async-start | bytes 8388608
  10.3 7.8 %slice-start.1 = ((s8[4718592]{0:T(1024)(128)(4,1)}), s8[524288]{0:T(1024)(128)(4,1)S(1)}, s32[]{:S(2)}) async-start(s8[4718592]{0:T(1024)(128)(4,1)} %bitcast.4), calls=%async_computation.1 | async-start | bytes 1048576
  10.6 7.6 %copy-start = (bf16[256,1536]{1,0:T(8,128)(2,1)S(1)}, bf16[256,1536]{1,0:T(8,128)(2,1)}, u32[]{:S(2)}) copy-start(bf16[256,1536]{1,0:T(8,128)(2,1)} %tok_ref.3) | copy-start | bytes 2359300
  10.6 7.6 %copy-start.1 = (bf16[1536,32]{0,1:T(8,128)(2,1)S(1)}, bf16[1536,32]{0,1:T(8,128)(2,1)}, u32[]{:S(2)}) copy-start(bf16[1536,32]{0,1:T(8,128)(2,1)} %param.26) | copy-start | bytes 294916
  10.6 7.6 %copy-start.2 = (s32[256,4]{0,1:T(4,128)S(1)}, s32[256,4]{0,1:T(4,128)}, u32[]{:S(2)}) copy-start(s32[256,4]{0,1:T(4,128)} %param.16) | copy-start | bytes 12292

commit v6 on v5

--- a/solution.py
+++ b/solution.py
@@ -274,49 +274,30 @@
 
 
 class Spread:
-    copies = 10
-
-    def __init__(self, h, flip, src, dst, relay, sems, base, split=False):
+    copies = 8
+
+    def __init__(self, h, flip, src, dst, sems, base):
         axis, rows = 1 - h, src.shape[2]
-        top, low = pl.ds(0, rows // 2), pl.ds(rows // 2, rows // 2)
-        unit = lambda step: (h, step * 2 + flip)
-        slot = lambda step: (h, (SIDE - step) % SIDE * 2 + flip)
-        ways = (1, SIDE - 1) if flip == 0 else (SIDE - 1, 1)
-        self.relays, self.onward = [], []
-        for i, (step, part) in enumerate(zip(ways, (top, low))):
-            self.relays.append(
-                remote(src.at[unit(2) + (part,)], relay.at[h, flip, i], sems, base + i, peer(axis, step, 0)))
-            self.onward.append(
-                remote(relay.at[h, flip, i], dst.at[slot(2) + (part,)], sems, base + 2 + i, peer(axis, step, flip)))
-        steps = (1, SIDE - 1, 0)[:2 + flip]
-        parts = ((low,), (top,)) if split else ((),)
-        self.direct = [
+        steps = (2, 1, SIDE - 1, 0)[:3 + flip]
+        self.parts = [
             [
-                remote(src.at[unit(step) + part], dst.at[slot(step) + part], sems,
-                       base + 4 + i * len(steps) + j, peer(axis, step, flip))
+                remote(src.at[h, step * 2 + flip, part], dst.at[h, (SIDE - step) % SIDE * 2 + flip, part], sems,
+                       base + i * len(steps) + j, peer(axis, step, flip))
                 for j, step in enumerate(steps)
             ]
-            for i, part in enumerate(parts)
+            for i, part in enumerate((pl.ds(rows // 2, rows // 2), pl.ds(0, rows // 2)))
         ]
 
-    def forward(self, i):
-        self.relays[i].wait_recv()
-        self.onward[i].start()
-
     def wait_part(self, i):
-        for copy in self.direct[i] + [self.onward[1 - i]]:
+        for copy in self.parts[i]:
             copy.wait_recv()
 
     def wait_recv(self):
-        for copy in sum(self.direct, []) + self.onward:
-            copy.wait_recv()
+        self.wait_part(0)
+        self.wait_part(1)
 
     def wait_src(self):
-        for copy in self.relays + sum(self.direct, []):
-            copy.wait_send()
-
-    def wait_onward(self):
-        for copy in self.onward:
+        for copy in self.parts[0] + self.parts[1]:
             copy.wait_send()
 
 
@@ -326,8 +307,7 @@
 
 
 def experts_kernel(att_ref, wo_ref, tok_ref, gain_ref, wr_t_ref, routes_t_ref, gate_hbm, up_hbm, down_hbm, out_ref,
-                   mixed, near, send, x, relay_out, back, relay_in, sums, parts, passed, final, gate_w, up_w, down_w,
-                   weight_sem, sems):
+                   mixed, near, send, x, back, sums, parts, passed, final, gate_w, up_w, down_w, weight_sem, sems):
     rows, width = tok_ref.shape
     experts = wr_t_ref.shape[0]
     half = width // 2
@@ -343,7 +323,7 @@
     gather, passing, out, home, pass_back, last = [], [], [], [], [], []
     for h in both:
         up, down = peer(h, 1, 0), peer(h, SIDE - 1, 0)
-        base = h * 54
+        base = h * 44
         gather.append([
             remote(near.at[h, 0, top], near.at[h, 3, top], sems, base, up),
             remote(near.at[h, 0, low], near.at[h, 1, low], sems, base + 1, down),
@@ -354,19 +334,17 @@
             remote(near.at[h, 3, top], near.at[h, 2, top], sems, base + 4, up),
             remote(near.at[h, 1, low], near.at[h, 2, low], sems, base + 5, down),
         ])
-        out.append([Spread(h, d, send, x, relay_out, sems, base + 6 + d * Spread.copies) for d in both])
-        home.append([
-            Spread(h, d, send, back, relay_in, sems, base + 26 + d * Spread.copies, split=d == 1) for d in both
-        ])
+        out.append([Spread(h, d, send, x, sems, base + 6 + d * Spread.copies) for d in both])
+        home.append([Spread(h, d, send, back, sems, base + 22 + d * Spread.copies) for d in both])
         pass_back.append([
-            remote(parts.at[h, 1, top], passed.at[h, 0], sems, base + 46, up),
-            remote(parts.at[h, 1, low], passed.at[h, 1], sems, base + 47, down),
+            remote(parts.at[h, 1, top], passed.at[h, 0], sems, base + 38, up),
+            remote(parts.at[h, 1, low], passed.at[h, 1], sems, base + 39, down),
         ])
         last.append([
-            remote(parts.at[h, 0, low], final.at[h, 0, low], sems, base + 48, up),
-            remote(parts.at[h, 2, top], final.at[h, 1, top], sems, base + 49, down),
-            remote(parts.at[h, 0, top], final.at[h, 0, top], sems, base + 50, up),
-            remote(parts.at[h, 2, low], final.at[h, 1, low], sems, base + 51, down),
+            remote(parts.at[h, 0, low], final.at[h, 0, low], sems, base + 40, up),
+            remote(parts.at[h, 2, top], final.at[h, 1, top], sems, base + 41, down),
+            remote(parts.at[h, 0, top], final.at[h, 0, top], sems, base + 42, up),
+            remote(parts.at[h, 2, low], final.at[h, 1, low], sems, base + 43, down),
         ])
 
     expert_row = lax.broadcasted_iota(jnp.int32, (experts, rows), 0)
@@ -433,7 +411,7 @@
         gather[h][2].wait_recv()
         for d in both:
             choose(h, 3, d)
-        start([out[h][d].relays[0] for d in both])
+        start([out[h][d].parts[1][0] for d in both])
     for h in both:
         gather[h][3].wait_recv()
         for d in both:
@@ -442,18 +420,13 @@
         for copy in passing[h]:
             copy.wait_recv()
         choose(h, 2, 0)
-        start([out[h][0].relays[1]] + out[h][0].direct[0])
+        start(out[h][0].parts[0] + out[h][0].parts[1][1:])
     for h in both:
         choose(h, 2, 1)
-        start([out[h][1].relays[1]])
     for h in both:
         x[h, 0] = send[h, 0]
-    for i in both:
-        for d in both:
-            for h in both:
-                out[h][d].forward(i)
-    for h in both:
-        start(out[h][1].direct[0])
+    for h in both:
+        start(out[h][1].parts[0] + out[h][1].parts[1][1:])
     for copy in weights:
         copy.wait()
 
@@ -478,22 +451,13 @@
 
     run_expert(0)
     for h in both:
-        start(home[h][0].relays + home[h][0].direct[0])
+        start(home[h][0].parts[0] + home[h][0].parts[1])
     run_expert(1)
-    for h in both:
-        start(home[h][1].relays[::-1])
     for i in both:
         for h in both:
-            home[h][0].forward(i)
-    for h in both:
-        start(home[h][1].direct[0])
+            start(home[h][1].parts[i])
     for h in both:
         back[h, 0] = send[h, 0]
-    for i in (1, 0):
-        for h in both:
-            home[h][1].forward(i)
-    for h in both:
-        start(home[h][1].direct[1])
 
     place_back = (lax.broadcasted_iota(jnp.int32, (rows, slots), 1) % CAP).astype(f32)
     meta_row = lax.broadcasted_iota(jnp.int32, (META, slots), 0)
@@ -546,9 +510,7 @@
         for copy in gather[h] + passing[h] + pass_back[h] + last[h]:
             copy.wait_send()
         for d in both:
-            out[h][d].wait_onward()
             home[h][d].wait_src()
-            home[h][d].wait_onward()
 
 
 def run_experts(attended, w_out, tokens, gains, router_t, routes_t, gate, up, down):
@@ -557,7 +519,6 @@
     vmem = pl.BlockSpec(memory_space=pltpu.VMEM)
     hbm = pl.BlockSpec(memory_space=pl.ANY)
     unit = (SIDE * CAP, half)
-    part = (SIDE * CAP // 2, half)
     return pl.pallas_call(
         experts_kernel,
         in_specs=[vmem] * 6 + [hbm] * 3,
@@ -568,9 +529,7 @@
             pltpu.VMEM((2, SIDE, rows, half + META), bf16),
             pltpu.VMEM((2, GROUPS) + unit, bf16),
             pltpu.VMEM((2, GROUPS) + unit, bf16),
-            pltpu.VMEM((2, 2, 2) + part, bf16),
             pltpu.VMEM((2, GROUPS) + unit, bf16),
-            pltpu.VMEM((2, 2, 2) + part, bf16),
             pltpu.VMEM((2, SIDE, rows, half), f32),
             pltpu.VMEM((2, 3, rows, half), bf16),
             pltpu.VMEM((2, 2, rows // 2, half), bf16),
@@ -579,7 +538,7 @@
             pltpu.VMEM((width, ff), bf16),
             pltpu.VMEM((ff, width), bf16),
             pltpu.SemaphoreType.DMA((3,)),
-            pltpu.SemaphoreType.DMA((2, 108)),
+            pltpu.SemaphoreType.DMA((2, 88)),
         ],
         compiler_params=pltpu.CompilerParams(collective_id=1, has_side_effects=True, vmem_limit_bytes=45 * MB),
         name="experts",

time: 140 us -> 142 us (1.014)
  Pallas kernels: 133 us -> 136 us
    pallas_call x1, Pallas kernels: 119 us -> 122 us  [run_experts(): pl.pallas_call(experts_kernel, in_specs=[vmem] * 6 + [hbm] * 3, out_specs...]
where the time goes in v6:
time: 142 us; the launch traced here: 141 us
  Pallas kernels  136 us (96%)
  local copies, waits for them, and re-layouts  2.76 us (2%)
  between operations  1.44 us (1%)
    pallas_call x1, Pallas kernels, run_experts(): pl.pallas_call(experts_kernel, in_specs=[vmem] * 6 + [hbm] * 3, out_specs...  122 us
    pallas_call x1, Pallas kernels, attend(): pl.pallas_call(attn_kernel, grid_spec=pltpu.PrefetchScalarGridSpec(num_sc...  7.31 us
    pallas_call x1, Pallas kernels, project(): pl.pallas_call(qkv_kernel, grid=(w_query.shape[1] // Q_BLOCK,), in_specs=...  5.99 us

profile of v6, /device:TPU:2, one launch (start us, length us, event | category | flops | bytes accessed | tf_op | source)
XLA Modules:
  0.0 141.1 jit_solution(16525190995385751266)
XLA Ops:
  1.3 0.7 maximum_convert_fusion
  2.0 0.5 fusion
  2.6 0.1 pad_maximum_fusion
  2.7 0.0 copy-start.3
  2.7 6.0 %project.1 = (bf16[12,256,128]{2,1,0:T(8,128)(2,1)S(1)}, bf16[256,256]{1,0:T(8,128)(2,1)}, bf16[256,256]{1,0:T(8,128)(2,1)}, bf16[256,256]{1,0:T(8,128)(2,1)S(1)}, bf16[256,256]{1,0:T(8,128)(2,1)S(1)}) custom-call(bf16[256,1536]{1,0:T(8,128)(2,1)} %tok_ref.3, f32[2,1536]{1,0:T(2,128)S(1)} %reshape.21.gain_ref, bf16[1536,1536]{1,0:T(8,128)(2,1)} %wq_ref.1, ...), custom_call_target="tpu_custom_call" | custom-call | tf_op jit(solution)/shard_map/project/pallas_call | solution.py:80
  8.7 0.0 copy-start.4
  8.7 0.0 copy-done.3
  8.7 0.0 slice-start
  8.8 0.3 copy.18.kc_ref
  9.0 1.3 copy-done.4
  10.3 0.0 slice-start.1
  10.3 0.3 copy.19.vc_ref
  10.6 0.0 copy-start
  10.6 0.0 copy-start.1
  10.6 0.0 copy-start.2
  10.6 7.3 %attend.1.att_ref = bf16[256,1536]{1,0:T(8,128)(2,1)S(1)} custom-call(s32[1]{0:T(128)} %copy.21.past_ref, bf16[12,256,128]{2,1,0:T(8,128)(2,1)S(1)} %get-tuple-element.8.q_ref, bf16[1,2,4100,128]{3,2,1,0:T(8,128)(2,1)S(1)} %copy.18.kc_ref, bf16[1,2,4100,128]{3,2,1,0:T(8,128)(2,1)S(1)} %copy.19.vc_ref, bf16[256,256]{1,0:T(8,128)(2,1)S(1)} %get-tuple-element.9.kn_ref, ...), custom_call_target="tpu_custom_call" | custom-call | tf_op jit(solution)/shard_map/attend/pallas_call | solution.py:196
  18.0 0.0 slice-done
  18.0 0.0 slice-done.1
  18.0 0.0 copy-done
  18.0 0.0 copy-done.1
  18.0 0.0 copy-done.2
  18.0 122.2 %experts.1 = bf16[256,1536]{1,0:T(8,128)(2,1)S(1)} custom-call(bf16[256,1536]{1,0:T(8,128)(2,1)S(1)} %attend.1.att_ref, bf16[1536,1536]{1,0:T(8,128)(2,1)S(1)} %bitcast.5, bf16[256,1536]{1,0:T(8,128)(2,1)S(1)} %copy-done, f32[2,1536]{1,0:T(2,128)S(1)} %reshape.21.gain_ref, bf16[32,1536]{1,0:T(8,128)(2,1)S(1)} %bitcast.6, s32[4,256]{1,0:T(4,128)S(1)} %bitcast.7, ...), custom_call_target="tpu_custom_call" | custom-call | tf_op jit(solution)/shard_map/experts/pallas_call | solution.py:522
  140.2 0.9 copy.22
  (4 shorter events, 0.0 us)
Async XLA Ops:
  2.7 6.0 %copy-start.3 = (bf16[1,2,4100,128]{3,1,2,0:T(2,128)(2,1)S(1)}, bf16[1,2,4100,128]{3,1,2,0:T(2,128)(2,1)}, u32[]{:S(2)}) copy-start(bf16[1,2,4100,128]{3,1,2,0:T(2,128)(2,1)} %param.18) | copy-start | bytes 6297604
  8.7 1.6 %copy-start.4 = (bf16[1,2,4100,128]{3,1,2,0:T(2,128)(2,1)S(1)}, bf16[1,2,4100,128]{3,1,2,0:T(2,128)(2,1)}, u32[]{:S(2)}) copy-start(bf16[1,2,4100,128]{3,1,2,0:T(2,128)(2,1)} %param.19) | copy-start | bytes 6297604
  8.7 9.2 %slice-start = ((s8[4718592]{0:T(1024)(128)(4,1)}), s8[4194304]{0:T(1024)(128)(4,1)S(1)}, s32[]{:S(2)}) async-start(s8[4718592]{0:T(1024)(128)(4,1)} %bitcast.4), calls=%async_computation | async-start | bytes 8388608
  10.3 7.6 %slice-start.1 = ((s8[4718592]{0:T(1024)(128)(4,1)}), s8[524288]{0:T(1024)(128)(4,1)S(1)}, s32[]{:S(2)}) async-start(s8[4718592]{0:T(1024)(128)(4,1)} %bitcast.4), calls=%async_computation.1 | async-start | bytes 1048576
  10.6 7.4 %copy-start = (bf16[256,1536]{1,0:T(8,128)(2,1)S(1)}, bf16[256,1536]{1,0:T(8,128)(2,1)}, u32[]{:S(2)}) copy-start(bf16[256,1536]{1,0:T(8,128)(2,1)} %tok_ref.3) | copy-start | bytes 2359300
  10.6 7.4 %copy-start.1 = (bf16[1536,32]{0,1:T(8,128)(2,1)S(1)}, bf16[1536,32]{0,1:T(8,128)(2,1)}, u32[]{:S(2)}) copy-start(bf16[1536,32]{0,1:T(8,128)(2,1)} %param.26) | copy-start | bytes 294916
  10.6 7.4 %copy-start.2 = (s32[256,4]{0,1:T(4,128)S(1)}, s32[256,4]{0,1:T(4,128)}, u32[]{:S(2)}) copy-start(s32[256,4]{0,1:T(4,128)} %param.16) | copy-start | bytes 12292

commit v7 on v6

--- a/solution.py
+++ b/solution.py
@@ -104,7 +104,7 @@
 LOW = -1e30
 
 
-def attn_kernel(past_ref, q_ref, kc_ref, vc_ref, kn_ref, vn_ref, o_ref, s_main, s_tail, m_scr, l_scr, acc, kx, vx):
+def attn_kernel(past_ref, q_ref, kc_ref, vc_ref, kn_ref, vn_ref, o_ref, s_main, s_tail, m_scr, acc, kx, vx):
     rows = kn_ref.shape[0]
     tile = HT * rows
     past = past_ref[0]
@@ -128,12 +128,6 @@
         out = s[:, 0:128]
         for c in range(1, s.shape[1] // 128):
             out = jnp.maximum(out, s[:, c * 128:(c + 1) * 128])
-        return out
-
-    def lane_sum(s):
-        out = s[:, 0:128]
-        for c in range(1, s.shape[1] // 128):
-            out = out + s[:, c * 128:(c + 1) * 128]
         return out
 
     column = lax.broadcasted_iota(jnp.int32, (1, EXTRA), 1)
@@ -168,20 +162,18 @@
 
     lax.fori_loop(0, blocks, score, 0)
     top = jnp.max(m_scr[...], axis=1, keepdims=True)
-    p = jnp.exp2(s_tail[...] - top)
-    l_scr[...] = lane_sum(p)
-    acc[...] = dot(p.astype(bf16), vx[...])
+    ones = jnp.ones((KB, HEAD_DIM), bf16)
+    p = jnp.exp2(s_tail[...] - top).astype(bf16)
+    acc[...] = dot(p, jnp.concatenate([vx[...], ones[:EXTRA]], axis=1))
 
     def weigh(j, carry):
         start = pl.multiple_of(j * KB, KB)
-        p = jnp.exp2(s_main[j] - top)
-        l_scr[...] += lane_sum(p)
-        acc[...] += dot(p.astype(bf16), vc_ref[0, 0, pl.ds(start, KB), :])
+        p = jnp.exp2(s_main[j] - top).astype(bf16)
+        acc[...] += dot(p, jnp.concatenate([vc_ref[0, 0, pl.ds(start, KB), :], ones], axis=1))
         return carry
 
     lax.fori_loop(0, blocks, weigh, 0)
-    total = jnp.sum(l_scr[...], axis=1, keepdims=True)
-    out = (acc[...] / total).astype(bf16)
+    out = (acc[:, 0:HEAD_DIM] / acc[:, HEAD_DIM:2 * HEAD_DIM]).astype(bf16)
     for h in range(HT):
         o_ref[:, h * HEAD_DIM:(h + 1) * HEAD_DIM] = out[h * rows:(h + 1) * rows]
 
@@ -207,8 +199,7 @@
                 pltpu.VMEM((WINDOW // KB, tile, KB), f32),
                 pltpu.VMEM((tile, EXTRA), f32),
                 pltpu.VMEM((tile, 128), f32),
-                pltpu.VMEM((tile, 128), f32),
-                pltpu.VMEM((tile, HEAD_DIM), f32),
+                pltpu.VMEM((tile, 2 * HEAD_DIM), f32),
                 pltpu.VMEM((EXTRA, HEAD_DIM), bf16),
                 pltpu.VMEM((EXTRA, HEAD_DIM), bf16),
             ],
@@ -219,7 +210,7 @@
     )(past, q, cache_keys, cache_values, keys_new, values_new)
 
 
-META = 128
+META = 4 * TOP
 
 
 SIDE = 4
@@ -307,7 +298,7 @@
 
 
 def experts_kernel(att_ref, wo_ref, tok_ref, gain_ref, wr_t_ref, routes_t_ref, gate_hbm, up_hbm, down_hbm, out_ref,
-                   mixed, near, send, x, back, sums, parts, passed, final, gate_w, up_w, down_w, weight_sem, sems):
+                   mixed, near, notes, send, x, back, sums, parts, passed, final, gate_w, up_w, down_w, weight_sem, sems):
     rows, width = tok_ref.shape
     experts = wr_t_ref.shape[0]
     half = width // 2
@@ -320,10 +311,10 @@
         for i, (src, dst) in enumerate(((gate_hbm, gate_w), (up_hbm, up_w), (down_hbm, down_w)))
     ]
     all_here = greet()
-    gather, passing, out, home, pass_back, last = [], [], [], [], [], []
+    gather, passing, noted, out, home, pass_back, last = [], [], [], [], [], [], []
     for h in both:
         up, down = peer(h, 1, 0), peer(h, SIDE - 1, 0)
-        base = h * 44
+        base = h * 48
         gather.append([
             remote(near.at[h, 0, top], near.at[h, 3, top], sems, base, up),
             remote(near.at[h, 0, low], near.at[h, 1, low], sems, base + 1, down),
@@ -333,6 +324,10 @@
         passing.append([
             remote(near.at[h, 3, top], near.at[h, 2, top], sems, base + 4, up),
             remote(near.at[h, 1, low], near.at[h, 2, low], sems, base + 5, down),
+        ])
+        noted.append([
+            remote(notes.at[h, 0], notes.at[h, SIDE - step], sems, base + 43 + step, peer(h, step, 0))
+            for step in range(1, SIDE)
         ])
         out.append([Spread(h, d, send, x, sems, base + 6 + d * Spread.copies) for d in both])
         home.append([Spread(h, d, send, back, sems, base + 22 + d * Spread.copies) for d in both])
@@ -352,28 +347,31 @@
     for j in range(1, TOP):
         named_t = named_t | (routes_t_ref[j:j + 1] == expert_row)
     named_t = jnp.where(named_t, 1.0, 0.0).astype(bf16)
-    meta_from = lax.broadcasted_iota(jnp.int32, (experts, META), 0)
-    meta_to = lax.broadcasted_iota(jnp.int32, (experts, META), 1)
+    note_row = lax.broadcasted_iota(jnp.int32, (META, mid), 0)
 
     def prepare(first):
         span = slice(first, first + mid)
         total = tok_ref[span].astype(f32) + dot(att_ref[span], wo_ref[...])
         mixed[span] = total
         ffn = norm_rows(total, gain_ref[1:2])
+        for h in both:
+            near[h, 0, span] = ffn[:, h * half:(h + 1) * half]
         a = lax.broadcasted_iota(jnp.int32, (mid, rows), 0) + first
         b = lax.broadcasted_iota(jnp.int32, (mid, rows), 1)
-        named = dot_nt(jnp.where(a == b, 1.0, 0.0).astype(bf16), named_t) > 0.5
-        ranks = dot_nt(jnp.where(b < a, 1.0, 0.0).astype(bf16), named_t)
-        rank = jnp.where(named, ranks, -1.0).astype(bf16)
-        score = jnp.where(named, jax.nn.sigmoid(dot_nt(ffn, wr_t_ref[...])), 0.0)
-        mix = score / jnp.sum(score, axis=1, keepdims=True)
-        high = mix.astype(bf16)
-        rest = (mix - high.astype(f32)).astype(bf16)
-        put = lambda v, i: dot(v, jnp.where(meta_to == meta_from + i * experts, 1.0, 0.0).astype(bf16))
-        meta = (put(high, 0) + put(rest, 1) + put(rank, 2)).astype(bf16)
+        ranks = dot_nt(named_t, jnp.where(b < a, 1.0, 0.0).astype(bf16))
+        score = jax.nn.sigmoid(dot_nt(wr_t_ref[...], ffn))
+        chosen = [routes_t_ref[j:j + 1, span] for j in range(TOP)]
+        pick = lambda j, v: jnp.sum(jnp.where(chosen[j] == expert_row[:, span], v, 0.0), axis=0, keepdims=True)
+        shares = [pick(j, score) for j in range(TOP)]
+        whole = (shares[0] + shares[1]) + (shares[2] + shares[3])
+        note = jnp.zeros((META, mid), f32)
+        for j in range(TOP):
+            mix = shares[j] / whole
+            high = mix.astype(bf16).astype(f32)
+            for i, value in enumerate((chosen[j].astype(f32), pick(j, ranks), high, mix - high)):
+                note = jnp.where(note_row == i * TOP + j, value, note)
         for h in both:
-            near[h, 0, span, 0:half] = ffn[:, h * half:(h + 1) * half]
-            near[h, 0, span, half:half + META] = meta
+            notes[h, 0, :, span] = note.astype(bf16)
 
     prepare(0)
     all_here()
@@ -381,26 +379,32 @@
         for h in both:
             gather[h][i].start()
     prepare(mid)
+    for h in both:
+        start([noted[h][0], noted[h][2]])
     for i in (1, 2):
         for h in both:
             gather[h][i].start()
     start(weights)
 
-    place = (lax.broadcasted_iota(jnp.int32, (slots, rows), 0) % CAP).astype(f32)
-    step_rows = (lax.broadcasted_iota(jnp.int32, (slots, META), 0) // CAP) * 2
-    meta_column = lax.broadcasted_iota(jnp.int32, (slots, META), 1)
+    slot = lax.broadcasted_iota(jnp.int32, (slots, rows), 0)
+
+    def slot_key(h, d, slot):
+        return (group_expert(h, (slot // CAP) * 2 + d) * CAP + slot % CAP).astype(f32)
 
     def choose(h, s, d):
-        spread = jnp.where(meta_column == group_expert(h, step_rows + d) + 2 * EXPERTS, 1.0, 0.0).astype(bf16)
-        wanted = dot_nt(spread, near[h, s, :, half:half + META])
-        select = jnp.where(wanted == place, 1.0, 0.0).astype(bf16)
-        chosen = dot(select, near[h, s, :, 0:half]).astype(bf16)
+        note = notes[h, s].astype(f32)
+        wanted = slot_key(h, d, slot)
+        select = jnp.zeros((slots, rows), f32)
+        for j in range(TOP):
+            select = jnp.where(note[j:j + 1] * CAP + note[TOP + j:TOP + j + 1] == wanted, 1.0, select)
+        select = select.astype(bf16)
+        chosen = dot(select, near[h, s]).astype(bf16)
         for k in range(SIDE):
             send[h, 2 * k + d, lane(s) * CAP:(lane(s) + 1) * CAP] = chosen[k * CAP:(k + 1) * CAP]
 
     for h in both:
         gather[h][0].wait_recv()
-        passing[h][0].start()
+        start([passing[h][0], noted[h][1]])
     for h in both:
         for d in both:
             choose(h, 0, d)
@@ -409,15 +413,17 @@
         passing[h][1].start()
     for h in both:
         gather[h][2].wait_recv()
+        noted[h][0].wait_recv()
         for d in both:
             choose(h, 3, d)
         start([out[h][d].parts[1][0] for d in both])
     for h in both:
         gather[h][3].wait_recv()
+        noted[h][2].wait_recv()
         for d in both:
             choose(h, 1, d)
     for h in both:
-        for copy in passing[h]:
+        for copy in passing[h] + [noted[h][1]]:
             copy.wait_recv()
         choose(h, 2, 0)
         start(out[h][0].parts[0] + out[h][0].parts[1][1:])
@@ -459,18 +465,22 @@
     for h in both:
         back[h, 0] = send[h, 0]
 
-    place_back = (lax.broadcasted_iota(jnp.int32, (rows, slots), 1) % CAP).astype(f32)
-    meta_row = lax.broadcasted_iota(jnp.int32, (META, slots), 0)
-    step_columns = (lax.broadcasted_iota(jnp.int32, (META, slots), 1) // CAP) * 2
+    slot_back = lax.broadcasted_iota(jnp.int32, (rows, slots), 1)
+    a = lax.broadcasted_iota(jnp.int32, (rows, rows), 0)
+    b = lax.broadcasted_iota(jnp.int32, (rows, rows), 1)
+    same = jnp.where(a == b, 1.0, 0.0).astype(bf16)
 
     def weigh(h, s, d):
-        meta = near[h, s, :, half:half + META]
-        expert = group_expert(h, step_columns + d)
-        take = lambda i: dot(meta, jnp.where(meta_row == expert + i * EXPERTS, 1.0, 0.0).astype(bf16))
-        here = take(2) == place_back
+        note = dot_nt(same, notes[h, s])
+        here = slot_key(h, d, slot_back)
+        high, rest = jnp.zeros((rows, slots), f32), jnp.zeros((rows, slots), f32)
+        for j in range(TOP):
+            column = lambda i: note[:, i * TOP + j:i * TOP + j + 1]
+            hit = column(0) * CAP + column(1) == here
+            high = jnp.where(hit, column(2), high)
+            rest = jnp.where(hit, column(3), rest)
+        high, rest = high.astype(bf16), rest.astype(bf16)
         outs = jnp.concatenate([back[h, 2 * k + d, lane(s) * CAP:(lane(s) + 1) * CAP] for k in range(SIDE)], axis=0)
-        high = jnp.where(here, take(0), 0.0).astype(bf16)
-        rest = jnp.where(here, take(1), 0.0).astype(bf16)
         return dot(high, outs) + dot(rest, outs)
 
     for h in both:
@@ -507,7 +517,7 @@
             mixed[:, cols] + (sums[h, 0] + final[h, 0].astype(f32) + final[h, 1].astype(f32))
         ).astype(bf16)
     for h in both:
-        for copy in gather[h] + passing[h] + pass_back[h] + last[h]:
+        for copy in gather[h] + passing[h] + noted[h] + pass_back[h] + last[h]:
             copy.wait_send()
         for d in both:
             home[h][d].wait_src()
@@ -526,7 +536,8 @@
         out_shape=jax.ShapeDtypeStruct((rows, width), bf16),
         scratch_shapes=[
             pltpu.VMEM((rows, width), f32),
-            pltpu.VMEM((2, SIDE, rows, half + META), bf16),
+            pltpu.VMEM((2, SIDE, rows, half), bf16),
+            pltpu.VMEM((2, SIDE, META, rows), bf16),
             pltpu.VMEM((2, GROUPS) + unit, bf16),
             pltpu.VMEM((2, GROUPS) + unit, bf16),
             pltpu.VMEM((2, GROUPS) + unit, bf16),
@@ -538,7 +549,7 @@
             pltpu.VMEM((width, ff), bf16),
             pltpu.VMEM((ff, width), bf16),
             pltpu.SemaphoreType.DMA((3,)),
-            pltpu.SemaphoreType.DMA((2, 88)),
+            pltpu.SemaphoreType.DMA((2, 96)),
         ],
         compiler_params=pltpu.CompilerParams(collective_id=1, has_side_effects=True, vmem_limit_bytes=45 * MB),
         name="experts",

time: 142 us -> 139 us (0.979)
  Pallas kernels: 136 us -> 133 us
    pallas_call x1, Pallas kernels: 122 us -> 108 us  [run_experts(): pl.pallas_call(experts_kernel, in_specs=[vmem] * 6 + [hbm] * 3, out_specs...]
    pallas_call x1, Pallas kernels: 7.31 us -> 19.2 us  [attend(): pl.pallas_call(attn_kernel, grid_spec=pltpu.PrefetchScalarGridSpec(num_sc...]
where the time goes in v7:
time: 139 us
  Pallas kernels  133 us (96%)
  local copies, waits for them, and re-layouts  2.76 us (2%)
  between operations  1.44 us (1%)
    pallas_call x1, Pallas kernels, run_experts(): pl.pallas_call(experts_kernel, in_specs=[vmem] * 6 + [hbm] * 3, out_specs...  108 us
    pallas_call x1, Pallas kernels, attend(): pl.pallas_call(attn_kernel, grid_spec=pltpu.PrefetchScalarGridSpec(num_sc...  19.2 us
    pallas_call x1, Pallas kernels, project(): pl.pallas_call(qkv_kernel, grid=(w_query.shape[1] // Q_BLOCK,), in_specs=...  5.99 us

profile of v7, /device:TPU:2, one launch (start us, length us, event | category | flops | bytes accessed | tf_op | source)
XLA Modules:
  0.0 138.6 jit_solution(9610630968105563156)
XLA Ops:
  1.3 0.7 maximum_convert_fusion
  2.0 0.5 fusion
  2.6 0.1 pad_maximum_fusion
  2.7 0.0 copy-start.3
  2.7 6.0 %project.1 = (bf16[12,256,128]{2,1,0:T(8,128)(2,1)S(1)}, bf16[256,256]{1,0:T(8,128)(2,1)}, bf16[256,256]{1,0:T(8,128)(2,1)}, bf16[256,256]{1,0:T(8,128)(2,1)S(1)}, bf16[256,256]{1,0:T(8,128)(2,1)S(1)}) custom-call(bf16[256,1536]{1,0:T(8,128)(2,1)} %tok_ref.3, f32[2,1536]{1,0:T(2,128)S(1)} %reshape.21.gain_ref, bf16[1536,1536]{1,0:T(8,128)(2,1)} %wq_ref.1, ...), custom_call_target="tpu_custom_call" | custom-call | tf_op jit(solution)/shard_map/project/pallas_call | solution.py:80
  8.7 0.0 copy-start.4
  8.7 0.0 copy-done.3
  8.7 0.0 slice-start
  8.8 0.3 copy.18.kc_ref
  9.0 1.3 copy-done.4
  10.3 0.0 slice-start.1
  10.3 0.3 copy.19.vc_ref
  10.6 0.0 copy-start
  10.6 0.0 copy-start.1
  10.6 0.0 copy-start.2
  10.6 19.2 %attend.1.att_ref = bf16[256,1536]{1,0:T(8,128)(2,1)S(1)} custom-call(s32[1]{0:T(128)} %copy.21.past_ref, bf16[12,256,128]{2,1,0:T(8,128)(2,1)S(1)} %get-tuple-element.8.q_ref, bf16[1,2,4100,128]{3,2,1,0:T(8,128)(2,1)S(1)} %copy.18.kc_ref, bf16[1,2,4100,128]{3,2,1,0:T(8,128)(2,1)S(1)} %copy.19.vc_ref, bf16[256,256]{1,0:T(8,128)(2,1)S(1)} %get-tuple-element.9.kn_ref, ...), custom_call_target="tpu_custom_call" | custom-call | tf_op jit(solution)/shard_map/attend/pallas_call | solution.py:188
  29.9 0.0 slice-done
  29.9 0.0 slice-done.1
  29.9 0.0 copy-done
  29.9 0.0 copy-done.1
  29.9 0.0 copy-done.2
  29.9 107.8 %experts.1 = bf16[256,1536]{1,0:T(8,128)(2,1)S(1)} custom-call(bf16[256,1536]{1,0:T(8,128)(2,1)S(1)} %attend.1.att_ref, bf16[1536,1536]{1,0:T(8,128)(2,1)S(1)} %bitcast.5, bf16[256,1536]{1,0:T(8,128)(2,1)S(1)} %copy-done, f32[2,1536]{1,0:T(2,128)S(1)} %reshape.21.gain_ref, bf16[32,1536]{1,0:T(8,128)(2,1)S(1)} %bitcast.6, s32[4,256]{1,0:T(4,128)S(1)} %bitcast.7, ...), custom_call_target="tpu_custom_call" | custom-call | tf_op jit(solution)/shard_map/experts/pallas_call | solution.py:532
  137.7 0.9 copy.22
  (4 shorter events, 0.0 us)
Async XLA Ops:
  2.7 6.0 %copy-start.3 = (bf16[1,2,4100,128]{3,1,2,0:T(2,128)(2,1)S(1)}, bf16[1,2,4100,128]{3,1,2,0:T(2,128)(2,1)}, u32[]{:S(2)}) copy-start(bf16[1,2,4100,128]{3,1,2,0:T(2,128)(2,1)} %param.18) | copy-start | bytes 6297604
  8.7 1.6 %copy-start.4 = (bf16[1,2,4100,128]{3,1,2,0:T(2,128)(2,1)S(1)}, bf16[1,2,4100,128]{3,1,2,0:T(2,128)(2,1)}, u32[]{:S(2)}) copy-start(bf16[1,2,4100,128]{3,1,2,0:T(2,128)(2,1)} %param.19) | copy-start | bytes 6297604
  8.7 21.1 %slice-start = ((s8[4718592]{0:T(1024)(128)(4,1)}), s8[4194304]{0:T(1024)(128)(4,1)S(1)}, s32[]{:S(2)}) async-start(s8[4718592]{0:T(1024)(128)(4,1)} %bitcast.4), calls=%async_computation | async-start | bytes 8388608
  10.3 19.6 %slice-start.1 = ((s8[4718592]{0:T(1024)(128)(4,1)}), s8[524288]{0:T(1024)(128)(4,1)S(1)}, s32[]{:S(2)}) async-start(s8[4718592]{0:T(1024)(128)(4,1)} %bitcast.4), calls=%async_computation.1 | async-start | bytes 1048576
  10.6 19.3 %copy-start = (bf16[256,1536]{1,0:T(8,128)(2,1)S(1)}, bf16[256,1536]{1,0:T(8,128)(2,1)}, u32[]{:S(2)}) copy-start(bf16[256,1536]{1,0:T(8,128)(2,1)} %tok_ref.3) | copy-start | bytes 2359300
  10.6 19.3 %copy-start.1 = (bf16[1536,32]{0,1:T(8,128)(2,1)S(1)}, bf16[1536,32]{0,1:T(8,128)(2,1)}, u32[]{:S(2)}) copy-start(bf16[1536,32]{0,1:T(8,128)(2,1)} %param.26) | copy-start | bytes 294916
  10.6 19.3 %copy-start.2 = (s32[256,4]{0,1:T(4,128)S(1)}, s32[256,4]{0,1:T(4,128)}, u32[]{:S(2)}) copy-start(s32[256,4]{0,1:T(4,128)} %param.16) | copy-start | bytes 12292
